TPU v7x, 512 devices: a whole 4x4x16 slice. The times are simulated.
512 devices in a mesh: group: 64 (over x_lo, z, core), shard: 8 (over y, x_hi).
Axes of the slice: x: 4 (x_hi: 2, x_lo: 2; x = x_hi * 2 + x_lo), y: 4, z: 16, core: 2. Of those that a mesh axis runs over, the one named last changes fastest.
Arguments:
- prompts: bfloat16 [512, 128, 1280], P(('group', 'shard')), may hold values from -6 to 6
- lengths: int32 [512], P(('group', 'shard')), may hold values from 32 to 128
- qkv_master: float32 [1280, 1920], P('group', 'shard')
- out_master: float32 [1280, 1280], P('group', 'shard'), may hold values from -0.15625 to 0.15625
- gate_up_master: float32 [1280, 2, 3584], P('group', None, 'shard'), may hold values from -0.15625 to 0.15625
- down_weight: bfloat16 [3584, 1280], P('shard'), may hold values from -0.09375 to 0.09375
- attn_gain: float32 [1280], replicated, may hold values from 0.25 to 1.75
- mlp_gain: float32 [1280], replicated, may hold values from 0.25 to 1.75
Outputs:
- hidden: bfloat16 [512, 128, 1280], P(('group', 'shard'))
- cache: bfloat16 [512, 128, 640], P(('group', 'shard'))
Inputs may be any that keep to these rules, and one draw needn't show every extreme that they name: `lengths`: live tokens of each prompt; positions from the length on are padding.
All inputs are finite; a program needn't handle non-finite values.
Results may differ from a plain program's by a relative error of at most 0.013.
The roundings to bfloat16 on the way count: a program that leaves them out, or rounds other values in their place, can miss the bound.
Values may be sent and summed in bfloat16 or wider, within the bound.
No kernel may reach another device: no remote copies, remote signals or barrier semaphores. Data moves between devices by JAX's collectives and lax.ppermute only.
A program may use at most 64 MiB of HBM per device.

v0:
```python
import jax
import jax.numpy as jnp
from jax import lax
from jax.sharding import PartitionSpec as P

QUERY_HEADS = 20
KEY_VALUE_HEADS = 5
HEAD_SIZE = 64


def norm_rows(stream, scale_gain):
    return (
        stream * lax.rsqrt(jnp.mean(stream * stream, axis=-1, keepdims=True) + 1e-05) * scale_gain
    )


def rotary(heads, positions):
    half_dim = heads.shape[-1] // 2
    frequency = 10000.0 ** (-(jnp.arange(half_dim).astype(heads.dtype) * 2.0 / heads.shape[-1]))
    angles = positions[:, None] * frequency[None, :]
    cosine = jnp.cos(angles)[:, None, :]
    sine_part = jnp.sin(angles)[:, None, :]
    first_half = heads[..., :half_dim]
    second_half = heads[..., half_dim:]
    return jnp.concatenate(
        [
            first_half * cosine - second_half * sine_part,
            second_half * cosine + first_half * sine_part,
        ],
        axis=-1,
    )


def attention(query_key_value, length):
    token_rows = query_key_value.shape[0]
    query = (
        query_key_value[:, : QUERY_HEADS * HEAD_SIZE]
        .astype(jnp.float32)
        .reshape(token_rows, QUERY_HEADS, HEAD_SIZE)
    )
    key_rows = (
        query_key_value[:, QUERY_HEADS * HEAD_SIZE : (QUERY_HEADS + KEY_VALUE_HEADS) * HEAD_SIZE]
        .astype(jnp.float32)
        .reshape(token_rows, KEY_VALUE_HEADS, HEAD_SIZE)
    )
    value_rows = query_key_value[:, (QUERY_HEADS + KEY_VALUE_HEADS) * HEAD_SIZE :].reshape(
        token_rows, KEY_VALUE_HEADS, HEAD_SIZE
    )
    positions = jnp.arange(token_rows).astype(jnp.float32)
    rotated_query = rotary(query, positions).astype(jnp.bfloat16)
    rotated_keys = rotary(key_rows, positions).astype(jnp.bfloat16)
    grouped_queries = rotated_query.reshape(
        token_rows, KEY_VALUE_HEADS, QUERY_HEADS // KEY_VALUE_HEADS, HEAD_SIZE
    )
    scores = jnp.einsum(
        "qkgd,skd->kgqs", grouped_queries, rotated_keys, preferred_element_type=jnp.float32
    ) * HEAD_SIZE ** (-0.5)
    indices = jnp.arange(token_rows)
    allowed = (indices[None, :] <= indices[:, None]) & (indices[None, :] < length)
    scores = jnp.where(allowed, scores, -1e30)
    largest = jnp.max(scores, axis=-1, keepdims=True)
    weights = jnp.exp(scores - largest)
    probability = (weights / jnp.sum(weights, axis=-1, keepdims=True)).astype(jnp.bfloat16)
    attended = jnp.einsum(
        "kgqs,skd->qkgd", probability, value_rows, preferred_element_type=jnp.float32
    )
    return (
        attended.reshape(token_rows, QUERY_HEADS * HEAD_SIZE).astype(jnp.bfloat16),
        rotated_keys,
        value_rows,
    )


def fold_rows(left, blocks):
    summed = jnp.dot(left, blocks[0], preferred_element_type=jnp.float32)
    placed = blocks[1]
    return (summed, placed)


def fold_units(left, block_rows):
    span_rows = block_rows.shape[0]
    return jnp.dot(left, block_rows.reshape(span_rows, -1), preferred_element_type=jnp.float32)


def shards(
    prompts, lengths, qkv_master, out_master, gate_up_master, down_weight, attn_gain, mlp_gain
):
    stream = prompts[0].astype(jnp.float32)
    token_rows = stream.shape[0]
    length = lengths[0]
    normed_in = norm_rows(stream, attn_gain).astype(jnp.bfloat16)
    qkv_columns, out_columns = (
        lax.all_gather(qkv_master.astype(jnp.bfloat16), "shard", axis=1, tiled=True),
        lax.all_gather(out_master.astype(jnp.bfloat16), "shard", axis=1, tiled=True),
    )
    summed, w_out = fold_rows(
        normed_in,
        (
            lax.all_gather(qkv_columns, "group", axis=0, tiled=True),
            lax.all_gather(out_columns, "group", axis=0, tiled=True),
        ),
    )
    query_key_value = summed.astype(jnp.bfloat16)
    attended, rotated_keys, value_rows = attention(query_key_value, length)
    middle = stream + jnp.dot(attended, w_out, preferred_element_type=jnp.float32)
    normed_mid = norm_rows(middle, mlp_gain).astype(jnp.bfloat16)
    gathered_mid = lax.all_gather(normed_mid, "shard", axis=0, tiled=True)
    units = gate_up_master.shape[2]
    summed_units = fold_units(
        gathered_mid,
        lax.all_gather(gate_up_master.astype(jnp.bfloat16), "group", axis=0, tiled=True),
    )
    gate_up = summed_units.reshape(-1, 2, units)
    hidden_units = (jax.nn.silu(gate_up[:, 0]) * gate_up[:, 1]).astype(jnp.bfloat16)
    feed_out = lax.psum_scatter(
        jnp.dot(hidden_units, down_weight, preferred_element_type=jnp.float32).astype(jnp.bfloat16),
        "shard",
        scatter_dimension=0,
        tiled=True,
    ).astype(jnp.float32)
    live_rows = (jnp.arange(token_rows) < length).astype(jnp.float32)[:, None]
    hidden = (live_rows * (middle + feed_out)).astype(jnp.bfloat16)
    joined_heads = jnp.concatenate(
        [
            rotated_keys.reshape(token_rows, KEY_VALUE_HEADS * HEAD_SIZE).astype(jnp.float32),
            value_rows.reshape(token_rows, KEY_VALUE_HEADS * HEAD_SIZE).astype(jnp.float32),
        ],
        axis=-1,
    )
    cache = (live_rows * joined_heads).astype(jnp.bfloat16)
    return (hidden[None], cache[None])


def solution(mesh):
    in_specs = (
        P(("group", "shard"), None, None),
        P(("group", "shard")),
        P("group", "shard"),
        P("group", "shard"),
        P("group", None, "shard"),
        P("shard", None),
        P(),
        P(),
    )
    out_specs = (P(("group", "shard"), None, None), P(("group", "shard"), None, None))
    return jax.shard_map(shards, mesh=mesh, in_specs=in_specs, out_specs=out_specs, check_vma=False)
```

profile of v0, /device:TPU:1, one launch (start us, length us, event | category | flops | bytes accessed | tf_op | source)
XLA Modules:
  0.0 599.5 jit_solution(9727599761350218476)
XLA Ops:
  7.2 0.8 convert_bitcast_fusion
  8.1 29.4 %all-gather.2 = bf16[8,160,20]{1,2,0:T(8,128)(2,1)S(1)} all-gather(bf16[1,160,20]{1,2,0:T(8,128)(2,1)S(1)} %convert_bitcast_fusion), channel_id=1, replica_groups=mesh['group'=64,'shard'=8] {'shard'}, dimensions={0}, use_global_device_ids=true | all-gather | bytes 57600 | tf_op jit(solution)/shard_map/all_gather | solution.py:94
  37.5 0.8 reshape.195
  38.3 0.7 convert_bitcast_fusion.1
  39.1 28.1 %all-gather = bf16[8,240,20]{1,2,0:T(8,128)(2,1)S(1)} all-gather(bf16[1,240,20]{1,2,0:T(8,128)(2,1)S(1)} %convert_bitcast_fusion.1), channel_id=1, replica_groups=mesh['group'=64,'shard'=8] {'shard'}, dimensions={0}, use_global_device_ids=true | all-gather | bytes 86400 | tf_op jit(solution)/shard_map/all_gather | solution.py:93
  67.2 0.8 reshape.191
  68.1 1.5 convert_element_type.147
  70.3 1.1 fusion.12
  71.7 101.3 %all-gather.15.cloned.1.call-done = bf16[64,20,1280]{2,1,0:T(8,128)(2,1)} async-done(((bf16[1,20,1280]{2,1,0:T(8,128)(2,1)}), bf16[64,20,1280]{2,1,0:T(8,128)(2,1)}) %all-gather.15.cloned.1.call-update) | async-done | bytes 3276816 | tf_op jit(solution)/shard_map/all_gather | solution.py:100
  173.0 6.1 %reshape.197 = bf16[1280,1280]{1,0:T(8,128)(2,1)} reshape(bf16[64,20,1280]{2,1,0:T(8,128)(2,1)} %all-gather.15.cloned.1.call-done) | data formatting | bytes 6553600
  179.2 119.6 %all-gather.13.cloned.1.call-done = bf16[64,20,1920]{2,1,0:T(8,128)(2,1)} async-done(((bf16[1,20,1920]{2,1,0:T(8,128)(2,1)}), bf16[64,20,1920]{2,1,0:T(8,128)(2,1)}) %all-gather.13.cloned.1.call-update) | async-done | bytes 4915216 | tf_op jit(solution)/shard_map/all_gather | solution.py:99
  298.8 7.5 %reshape.193 = bf16[1280,1920]{1,0:T(8,128)(2,1)} reshape(bf16[64,20,1920]{2,1,0:T(8,128)(2,1)} %all-gather.13.cloned.1.call-done) | data formatting | bytes 9830400
  306.3 4.4 convolution_convert_fusion.1
  311.0 1.7 fusion.41
  312.7 1.7 convolution_convert_fusion.2
  315.8 0.9 multiply_convert_fusion.1
  316.7 103.4 %all-gather.11.cloned.1.call-done = bf16[1280,2,448]{2,1,0:T(2,128)(2,1)} async-done(((bf16[20,2,448]{2,1,0:T(2,128)(2,1)}), bf16[1280,2,448]{2,1,0:T(2,128)(2,1)}) %all-gather.11.cloned.1.call-update) | async-done | bytes 2293776 | tf_op jit(solution)/shard_map/all_gather | solution.py:111
  420.2 7.4 %copy.40 = bf16[1280,2,448]{0,2,1:T(8,128)(2,1)} copy(bf16[1280,2,448]{2,1,0:T(2,128)(2,1)} %all-gather.11.cloned.1.call-done) | data formatting | bytes 4587520 | tf_op jit(solution)/shard_map/all_gather | solution.py:111
  427.6 65.6 %all-gather.9.cloned.1.call-done = bf16[1024,1280]{1,0:T(8,128)(2,1)} async-done(((bf16[128,1280]{1,0:T(8,128)(2,1)}), bf16[1024,1280]{1,0:T(8,128)(2,1)}) %all-gather.9.cloned.1.call-update) | async-done | bytes 2621456 | tf_op jit(solution)/shard_map/all_gather | solution.py:107
  493.2 5.0 fusion.1
  498.2 3.2 convolution_convert_fusion
  501.5 0.8 copy.41
  502.3 88.9 %reduce-scatter.2.cloned.1.call-done = bf16[128,1280]{1,0:T(8,128)(2,1)} async-done(((bf16[1024,1280]{1,0:T(8,128)(2,1)}), bf16[128,1280]{1,0:T(8,128)(2,1)}) %reduce-scatter.2.cloned.1.call-update) | async-done | bytes 327696 | tf_op jit(solution)/shard_map/reduce_scatter | solution.py:115
  591.2 1.8 fusion.15
  (39 shorter events, 2.2 us)
Async XLA Ops:
  7.2 491.0 %copy-start = (bf16[448,1280]{1,0:T(8,128)(2,1)S(1)}, bf16[448,1280]{1,0:T(8,128)(2,1)}, u32[]{:S(2)}) copy-start(bf16[448,1280]{1,0:T(8,128)(2,1)} %param.13) | copy-start | bytes 3440644
  7.2 165.9 %all-gather.15.cloned.1.call-start = ((), (), s32[]{:S(2)}) async-start(), calls=%async_computation.5 | async-start | bytes 3993600 | tf_op jit(solution)/shard_map/all_gather | solution.py:100
  38.3 260.5 %all-gather.13.cloned.1.call-start = ((), (), s32[]{:S(2)}) async-start(), calls=%async_computation.4 | async-start | bytes 5990400 | tf_op jit(solution)/shard_map/all_gather | solution.py:99
  68.0 352.2 %all-gather.11.cloned.1.call-start = ((), (), s32[]{:S(2)}) async-start(), calls=%async_computation.2 | async-start | bytes 2662400 | tf_op jit(solution)/shard_map/all_gather | solution.py:111
  69.6 423.6 %all-gather.9.cloned.1.call-start = ((), (), s32[]{:S(2)}) async-start(), calls=%async_computation.1 | async-start | bytes 2949120 | tf_op jit(solution)/shard_map/all_gather | solution.py:107
  179.1 127.2 %copy-start.2 = (bf16[1,128,1280]{2,1,0:T(8,128)(2,1)S(1)}, bf16[1,128,1280]{2,1,0:T(8,128)(2,1)}, u32[]{:S(2)}) copy-start(bf16[1,128,1280]{2,1,0:T(8,128)(2,1)} %param.8) | copy-start | bytes 983044
  179.2 127.2 %copy-start.3 = (f32[1280]{0:T(1024)S(1)}, f32[1280]{0:T(1024)}, u32[]{:S(2)}) copy-start(f32[1280]{0:T(1024)} %param.14) | copy-start | bytes 15364
  312.7 2.3 copy-start.1
  315.1 0.8 copy-start.4
  316.7 274.5 %reduce-scatter.2.cloned.1.call-start = ((), (), s32[]{:S(2)}) async-start(), calls=%async_computation.3 | async-start | bytes 2949120 | tf_op jit(solution)/shard_map/reduce_scatter | solution.py:115
Sparse Core Ops, SparseCore 0:
  38.4 134.5 all-gather.14
  175.8 122.9 all-gather.12
  300.9 119.2 all-gather.10
  423.8 69.3 all-gather.8
  501.5 89.6 reduce-scatter.1
where the time goes:
time: 601 us; the launch traced here: 600 us
  waiting for transfers between devices  479 us (80%)
  blocking collectives  57.5 us (10%)
  local copies, waits for them, and re-layouts  24.2 us (4%)
  matrix products  16.8 us (3%)
  between operations  14.6 us (2%)
  other arithmetic  7.38 us (1%)
    all_gather x1, waiting for transfers between devices, shards(): lax.all_gather(qkv_columns, 'group', axis=0, tiled=True)  120 us
    all_gather x1, waiting for transfers between devices, shards(): lax.all_gather(gate_up_master.astype(jnp.bfloat16), 'group', axis=0, tile...  103 us
    all_gather x1, waiting for transfers between devices, shards(): lax.all_gather(out_columns, 'group', axis=0, tiled=True)  101 us
    reduce_scatter x1, waiting for transfers between devices, shards(): lax.psum_scatter(jnp.dot(hidden_units, down_weight, preferred_element_typ...  88.9 us
    all_gather x1, waiting for transfers between devices, shards(): gathered_mid = lax.all_gather(normed_mid, 'shard', axis=0, tiled=True)  65.6 us
    all_gather x1, blocking collectives, shards(): lax.all_gather(out_master.astype(jnp.bfloat16), 'shard', axis=1, tiled=True)  29.4 us
    all_gather x1, blocking collectives, shards(): lax.all_gather(qkv_master.astype(jnp.bfloat16), 'shard', axis=1, tiled=True)  28.1 us
    unnamed x15, local copies, waits for them, and re-layouts  16.7 us
  transfers between devices with their start and end apart: 5, of which 5 were waited for; matrix products, arithmetic and copies ran while one was open for 6% of the time, Pallas kernels for 0%

commit v1 on v0

v1 whole, which is shorter than its diff:
```python
import jax
import jax.numpy as jnp
import numpy as np
from jax import lax
from jax.experimental import pallas as pl
from jax.experimental.pallas import tpu as pltpu
from jax.sharding import Mesh, PartitionSpec as P

QUERY_HEADS = 20
KEY_VALUE_HEADS = 5
HEAD_SIZE = 64
D = 1280
LMAX = 128
QW = 120
OW = 80
KHALF = 640
UNITS = 448
F32 = jnp.float32
BF16 = jnp.bfloat16

AXES = ("x_lo", "z", "core", "y", "x_hi")
SIZES = (2, 16, 2, 4, 2)


def tables():
    half_dim = HEAD_SIZE // 2
    frequency = np.float32(10000.0) ** (
        -(np.arange(half_dim).astype(np.float32) * np.float32(2.0) / np.float32(HEAD_SIZE))
    )
    angles = frequency.astype(np.float32)[:, None] * np.arange(LMAX).astype(np.float32)[None, :]
    return np.cos(angles).astype(np.float32), np.sin(angles).astype(np.float32)


def dot_nt(left, right):
    return lax.dot_general(left, right, (((1,), (1,)), ((), ())), preferred_element_type=F32)


def dot_nn(left, right):
    return jnp.dot(left, right, preferred_element_type=F32)


def attention_kernel(
    length_ref,
    core_ref,
    tokens_ref,
    own_ref,
    other_ref,
    cos_ref,
    sin_ref,
    gain_in_ref,
    gain_mid_ref,
    middle_ref,
    normed_ref,
    cache_ref,
    qkv,
    attended,
    mid,
):
    length = length_ref[0]
    core = core_ref[0]
    halves = ((own_ref, core), (other_ref, 1 - core))
    stream = tokens_ref[...].astype(F32)
    square = jnp.mean(stream * stream, axis=-1, keepdims=True)
    normed = (stream * lax.rsqrt(square + 1e-05) * gain_in_ref[...]).astype(BF16)
    low, high = normed[:, :KHALF], normed[:, KHALF:]
    for weights, half in halves:
        for s in range(8):
            rows = dot_nt(weights[s, OW : OW + QW, :], low) + dot_nt(
                weights[8 + s, OW : OW + QW, :], high
            )
            start = pl.multiple_of((2 * s + half) * QW, 8)
            qkv[pl.ds(start, QW), :] = rows.astype(BF16).astype(F32)
    cosine = cos_ref[...]
    sine = sin_ref[...]

    def rotate(start):
        first = qkv[start : start + 32, :]
        second = qkv[start + 32 : start + 64, :]
        return jnp.concatenate(
            [first * cosine - second * sine, second * cosine + first * sine], axis=0
        )

    key_at = lax.broadcasted_iota(jnp.int32, (LMAX, LMAX), 0)
    query_at = lax.broadcasted_iota(jnp.int32, (LMAX, LMAX), 1)
    allowed = (key_at <= query_at) & (key_at < length)
    allowed = jnp.concatenate([allowed.astype(F32)] * 4, axis=1) > 0.5
    for g in range(KEY_VALUE_HEADS):
        key_start = (QUERY_HEADS + g) * HEAD_SIZE
        value_start = (QUERY_HEADS + KEY_VALUE_HEADS + g) * HEAD_SIZE
        keys = rotate(key_start).astype(BF16).astype(F32)
        qkv[key_start : key_start + HEAD_SIZE, :] = keys
        keys = keys.T.astype(BF16)
        values = qkv[value_start : value_start + HEAD_SIZE, :].astype(BF16)
        queries = jnp.concatenate(
            [rotate((4 * g + h) * HEAD_SIZE).astype(BF16) for h in range(4)], axis=1
        )
        scores = dot_nn(keys, queries) * HEAD_SIZE ** (-0.5)
        scores = jnp.where(allowed, scores, -1e30)
        weights = jnp.exp(scores - jnp.max(scores, axis=0, keepdims=True))
        probability = (weights / jnp.sum(weights, axis=0, keepdims=True)).astype(BF16)
        out = dot_nn(values, probability).astype(BF16)
        for h in range(4):
            row = (4 * g + h) * HEAD_SIZE
            attended[row : row + HEAD_SIZE, :] = out[:, h * LMAX : (h + 1) * LMAX]
    live = (lax.broadcasted_iota(jnp.int32, (LMAX, LMAX), 0) < length).astype(F32)
    for j in range(5):
        row = QUERY_HEADS * HEAD_SIZE + j * LMAX
        block = qkv[row : row + LMAX, :].T
        cache_ref[:, j * LMAX : (j + 1) * LMAX] = (live * block).astype(BF16)
    low, high = attended[:KHALF, :], attended[KHALF:, :]
    for weights, half in halves:
        for s in range(8):
            rows = dot_nn(weights[s, :OW, :], low) + dot_nn(weights[8 + s, :OW, :], high)
            start = pl.multiple_of((2 * s + half) * OW, 8)
            mid[pl.ds(start, OW), :] = rows
    total = jnp.zeros((1, LMAX), F32)
    for j in range(10):
        cols = slice(j * LMAX, (j + 1) * LMAX)
        block = mid[cols, :] + tokens_ref[:, cols].astype(F32).T
        mid[cols, :] = block
        middle_ref[:, cols] = block.T
        total = total + jnp.sum(block * block, axis=0, keepdims=True)
    scale = lax.rsqrt(total * (1.0 / D) + 1e-05)
    for j in range(16):
        for lo in range(2):
            start = lo * KHALF + j * 40
            block = mid[start : start + 40, :] * scale * gain_mid_ref[start : start + 40, :]
            qkv[j * 80 + lo * 40 : j * 80 + lo * 40 + 40, :] = block
    for j in range(10):
        cols = slice(j * LMAX, (j + 1) * LMAX)
        normed_ref[:, cols] = qkv[cols, :].T.astype(BF16)


def attention(length, core, tokens, own, other, gain_in, gain_mid):
    cosine, sine = tables()
    vmem = pl.BlockSpec(memory_space=pltpu.VMEM)
    smem = pl.BlockSpec(memory_space=pltpu.SMEM)
    return pl.pallas_call(
        attention_kernel,
        out_shape=(
            jax.ShapeDtypeStruct((LMAX, D), F32),
            jax.ShapeDtypeStruct((LMAX, D), BF16),
            jax.ShapeDtypeStruct((LMAX, 640), BF16),
        ),
        in_specs=[smem, smem] + [vmem] * 7,
        out_specs=(vmem, vmem, vmem),
        scratch_shapes=[
            pltpu.VMEM((1920, LMAX), F32),
            pltpu.VMEM((D, LMAX), BF16),
            pltpu.VMEM((D, LMAX), F32),
        ],
        compiler_params=pltpu.CompilerParams(vmem_limit_bytes=32 << 20),
        cost_estimate=pl.CostEstimate(
            flops=1200000000, bytes_accessed=10000000, transcendentals=400000
        ),
        name="attention",
    )(
        length,
        core,
        tokens,
        own,
        other,
        jnp.asarray(cosine),
        jnp.asarray(sine),
        gain_in[None, :],
        gain_mid[:, None],
    )


def spread(block, axes, count):
    copies = jnp.broadcast_to(block[None], (count,) + block.shape)
    return lax.all_to_all(copies, axes, 0, 0, tiled=False)


def after(value, *others):
    return lax.optimization_barrier((value,) + others)[0]


SWAP = [(0, 1), (1, 0)]


def shards(
    prompts, lengths, qkv_master, out_master, gate_up_master, down_weight, attn_gain, mlp_gain
):
    core = lax.axis_index("core")
    x_hi = lax.axis_index("x_hi")
    tokens = prompts[0]
    gate_up = gate_up_master.astype(BF16).reshape(20, 2 * UNITS)
    near = spread(gate_up, ("x_lo", "core", "x_hi"), 8).reshape(4, 2, 20, 2 * UNITS)
    near = lax.dynamic_index_in_dim(near, core, axis=1, keepdims=False).reshape(80, 2 * UNITS)
    gate_up_own = lax.all_gather(near, "z", axis=0, tiled=True)
    down_other = lax.ppermute(down_weight, "x_hi", SWAP)
    merged = jnp.concatenate([out_master, qkv_master], axis=1).astype(BF16)
    merged = lax.all_gather(merged, "core", axis=0, tiled=True)
    part = jnp.concatenate(
        [
            lax.dynamic_slice_in_dim(merged[:, :160], core * OW, OW, axis=1),
            lax.dynamic_slice_in_dim(merged[:, 160:], core * QW, QW, axis=1),
        ],
        axis=1,
    )
    part = after(part, near)
    part = spread(part, "z", 16).reshape(KHALF, OW + QW).T
    own = spread(part, ("x_lo", "y", "x_hi"), 16)
    other = lax.ppermute(own, "core", SWAP)
    gate_up_other = lax.ppermute(after(gate_up_own, own), "core", SWAP)
    middle, normed_mid, cache = attention(
        lengths, core.astype(jnp.int32)[None], tokens, own, other, attn_gain, mlp_gain
    )
    gathered = spread(normed_mid, "y", 4).reshape(4 * LMAX, D)
    same = core == x_hi
    down_first = jnp.where(same, down_weight, down_other)
    down_second = jnp.where(same, down_other, down_weight)

    def units_block(gate_up_rows, down_rows):
        gate_up = jnp.dot(gathered, gate_up_rows, preferred_element_type=F32)
        hidden_units = (jax.nn.silu(gate_up[:, :UNITS]) * gate_up[:, UNITS:]).astype(BF16)
        return jnp.dot(hidden_units, down_rows, preferred_element_type=F32).astype(BF16)

    partial = units_block(gate_up_own, down_first).astype(F32) + units_block(
        gate_up_other, down_second
    ).astype(F32)
    partial = partial.astype(BF16).reshape(4, LMAX, D)
    partial = lax.all_to_all(partial, "y", 0, 0, tiled=False)
    feed_out = jnp.sum(partial.astype(F32), axis=0)
    live_rows = (jnp.arange(LMAX) < lengths[0]).astype(F32)[:, None]
    hidden = (live_rows * (middle + feed_out)).astype(BF16)
    return (hidden[None], cache[None])


def solution(mesh):
    fine = Mesh(mesh.devices.reshape(SIZES), AXES)
    group = ("x_lo", "z", "core")
    shard = ("y", "x_hi")
    in_specs = (
        P(group + shard, None, None),
        P(group + shard),
        P(group, shard),
        P(group, shard),
        P(group, None, shard),
        P(shard, None),
        P(),
        P(),
    )
    out_specs = (P(group + shard, None, None), P(group + shard, None, None))
    return jax.shard_map(shards, mesh=fine, in_specs=in_specs, out_specs=out_specs, check_vma=False)
```

time: 601 us -> 222 us (0.37)
  waiting for transfers between devices: 479 us -> 106 us
  starting transfers between devices: 0.21 us -> 44.2 us
  blocking collectives: 57.5 us -> 27.6 us
  local copies, waits for them, and re-layouts: 24.2 us -> 5.74 us
  Pallas kernels: 0 us -> 8.98 us
    all_gather x4 -> x1, waiting for transfers between devices: 390 us -> 8.95 us  [shards(): gate_up_own = lax.all_gather(near, 'z', axis=0, tiled=True)]
    all_to_all x0 -> x4, waiting for transfers between devices: none -> 90 us  [the longest x3 73.8 us: spread(): return lax.all_to_all(copies, axes, 0, 0, tiled=False)]
    reduce_scatter x1 -> x0, waiting for transfers between devices: 88.9 us -> none  [shards(): lax.psum_scatter(jnp.dot(hidden_units, down_weight, preferred_element_typ...]
    all_gather x2 -> x1, blocking collectives: 57.5 us -> 1.83 us  [shards(): merged = lax.all_gather(merged, 'core', axis=0, tiled=True)]
    all_to_all x0 -> x1, blocking collectives: none -> 25.8 us  [spread(): return lax.all_to_all(copies, axes, 0, 0, tiled=False)]
    all_to_all x0 -> x4, starting transfers between devices: none -> 25.3 us  [the longest x3 21.4 us: spread(): return lax.all_to_all(copies, axes, 0, 0, tiled=False)]
    ppermute x0 -> x3, starting transfers between devices: none -> 18.8 us  [the longest x1 10.8 us: shards(): gate_up_other = lax.ppermute(after(gate_up_own, own), 'core', SWAP)]
    unnamed x15 -> x17, local copies, waits for them, and re-layouts: 16.7 us -> 0.06 us
  transfers between devices with their start and end apart: 5 -> 8, of which waited for: 5 -> 6; matrix products, arithmetic and copies ran while one was open for 6% -> 4% of each run, Pallas kernels for 0% -> 4%
where the time goes in v1:
time: 222 us; the launch traced here: 220 us
  waiting for transfers between devices  106 us (48%)
  starting transfers between devices  44.2 us (20%)
  blocking collectives  27.6 us (12%)
  between operations  14.9 us (7%)
  matrix products  10.9 us (5%)
  Pallas kernels  8.98 us (4%)
  local copies, waits for them, and re-layouts  5.74 us (3%)
    all_to_all x3, waiting for transfers between devices, spread(): return lax.all_to_all(copies, axes, 0, 0, tiled=False)  73.8 us
    all_to_all x1, blocking collectives, spread(): return lax.all_to_all(copies, axes, 0, 0, tiled=False)  25.8 us
    all_to_all x3, starting transfers between devices, spread(): return lax.all_to_all(copies, axes, 0, 0, tiled=False)  21.4 us
    all_to_all x1, waiting for transfers between devices, shards(): partial = lax.all_to_all(partial, 'y', 0, 0, tiled=False)  16.2 us
    ppermute x1, starting transfers between devices, shards(): gate_up_other = lax.ppermute(after(gate_up_own, own), 'core', SWAP)  10.8 us
    pallas_call x1, Pallas kernels, attention(): pl.pallas_call(attention_kernel, out_shape=(jax.ShapeDtypeStruct((LMAX, D...  8.98 us
    all_gather x1, waiting for transfers between devices, shards(): gate_up_own = lax.all_gather(near, 'z', axis=0, tiled=True)  8.95 us
    dot_general x2, matrix products, units_block(): gate_up = jnp.dot(gathered, gate_up_rows, preferred_element_type=F32)  6.32 us
  transfers between devices with their start and end apart: 8, of which 6 were waited for; matrix products, arithmetic and copies ran while one was open for 4% of the time, Pallas kernels for 4%

profile of v1, /device:TPU:1, one launch (start us, length us, event | category | flops | bytes accessed | tf_op | source)
XLA Modules:
  0.0 219.9 jit_solution(10727899171256502544)
XLA Ops:
  7.2 0.9 convert_element_type.39
  9.0 10.2 %all-to-all-start = ((bf16[8,20,896]{2,1,0:T(8,128)(2,1)}), bf16[8,20,896]{2,1,0:T(8,128)(2,1)S(1)}, u32[]{:S(2)}, u32[]{:S(2)}) async-start(bf16[8,20,896]{2,1,0:T(8,128)(2,1)} %broadcast_in_dim.43), calls=%async_computation | async-start | bytes 688128 | tf_op jit(solution)/shard_map/all_to_all | solution.py:172
  19.3 1.8 all-gather
  21.5 5.2 %all-to-all-done = bf16[8,20,896]{2,1,0:T(8,128)(2,1)S(1)} async-done(((bf16[8,20,896]{2,1,0:T(8,128)(2,1)}), bf16[8,20,896]{2,1,0:T(8,128)(2,1)S(1)}, u32[]{:S(2)}, u32[]{:S(2)}) %all-to-all-start) | async-done | bytes 286752 | tf_op jit(solution)/shard_map/all_to_all | solution.py:172
  27.4 25.8 %all_to_all.25 = bf16[16,40,200]{2,1,0:T(8,128)(2,1)S(1)} all-to-all(bf16[16,40,200]{2,1,0:T(8,128)(2,1)S(1)} %broadcast_in_dim.44), channel_id=1, replica_groups=mesh['x_lo'=2,'z'=16,'core'=2,'y'=4,'x_hi'=2] {'z'}, dimensions={0} | all-to-all | bytes 512000 | tf_op jit(solution)/shard_map/all_to_all | solution.py:172
  53.4 2.3 %broadcast_in_dim.45 = bf16[16,200,640]{2,1,0:T(8,128)(2,1)} broadcast(bf16[200,640]{1,0:T(8,128)(2,1)S(1)} %copy.20), dimensions={1,2} | broadcast | bytes 4352000 | tf_op jit(solution)/shard_map/broadcast_in_dim | solution.py:171
  55.7 6.9 %all-to-all-start.2 = ((bf16[16,200,640]{2,1,0:T(8,128)(2,1)}), bf16[16,200,640]{2,1,0:T(8,128)(2,1)}, u32[]{:S(2)}, u32[]{:S(2)}) async-start(bf16[16,200,640]{2,1,0:T(8,128)(2,1)} %broadcast_in_dim.45), calls=%async_computation.2 | async-start | bytes 8192000 | tf_op jit(solution)/shard_map/all_to_all | solution.py:172
  63.3 55.3 %all-to-all-done.2.own_ref = bf16[16,200,640]{2,1,0:T(8,128)(2,1)} async-done(((bf16[16,200,640]{2,1,0:T(8,128)(2,1)}), bf16[16,200,640]{2,1,0:T(8,128)(2,1)}, u32[]{:S(2)}, u32[]{:S(2)}) %all-to-all-start.2) | async-done | bytes 4096032 | tf_op jit(solution)/shard_map/all_to_all | solution.py:172
  118.7 3.5 %collective-permute-start = (bf16[16,200,640]{2,1,0:T(8,128)(2,1)}, bf16[16,200,640]{2,1,0:T(8,128)(2,1)}, u32[]{:S(2)}, u32[]{:S(2)}) collective-permute-start(bf16[16,200,640]{2,1,0:T(8,128)(2,1)} %all-to-all-done.2.own_ref), channel_id=1, source_target_pairs={{0,8},{8,0},{1,9},{9,1},{2,10},{10,2},{3,11},{11,3},{4,12},{12,4},... | collective-permute-start | bytes 12288008 | tf_op jit(solution)/shard_map/ppermute | solution.py:205
  122.2 8.9 %all-gather.3.cloned.1.call-done = bf16[1280,896]{1,0:T(8,128)(2,1)} async-done(((bf16[80,896]{1,0:T(8,128)(2,1)}), bf16[1280,896]{1,0:T(8,128)(2,1)}) %all-gather.3.cloned.1.call-update) | async-done | bytes 2293776 | tf_op jit(solution)/shard_map/all_gather | solution.py:191
  131.1 10.8 %collective-permute-start.2 = (bf16[1280,896]{1,0:T(8,128)(2,1)}, bf16[1280,896]{1,0:T(8,128)(2,1)}, u32[]{:S(2)}, u32[]{:S(2)}) collective-permute-start(bf16[1280,896]{1,0:T(8,128)(2,1)} %all-gather.3.cloned.1.call-done), channel_id=1, source_target_pairs={{0,8},{8,0},{1,9},{9,1},{2,10},{10,2},{3,11},{11,3},{4,12},{12,4},... | collective-permute-start | bytes 6881288 | tf_op jit(solution)/shard_map/ppermute | solution.py:206
  142.9 9.0 %attention.1 = (f32[128,1280]{1,0:T(8,128)S(1)}, bf16[128,1280]{1,0:T(8,128)(2,1)S(1)}, bf16[128,640]{1,0:T(8,128)(2,1)}) custom-call(s32[1]{0:T(128)} %copy.25.length_ref, s32[1]{0:T(128)} %bitcast.1.core_ref, bf16[128,1280]{1,0:T(8,128)(2,1)S(1)} %bitcast.19, bf16[16,200,640]{2,1,0:T(8,128)(2,1)} %all-to-all-done.2.own_ref, ...), custom_call_target="tpu_custom_call" | custom-call | flops 1200000000 | bytes 10000000 | tf_op jit(solution)/shard_map/attention/pallas_call | solution.py:138
  151.9 1.2 broadcast_in_dim.48
  153.0 4.3 %all-to-all-start.3 = ((bf16[4,128,1280]{2,1,0:T(8,128)(2,1)}), bf16[4,128,1280]{2,1,0:T(8,128)(2,1)S(1)}, u32[]{:S(2)}, u32[]{:S(2)}) async-start(bf16[4,128,1280]{2,1,0:T(8,128)(2,1)} %broadcast_in_dim.48), calls=%async_computation.3 | async-start | bytes 2621440 | tf_op jit(solution)/shard_map/all_to_all | solution.py:172
  157.3 4.5 %collective-permute-start.1 = (bf16[448,1280]{1,0:T(8,128)(2,1)S(1)}, bf16[448,1280]{1,0:T(8,128)(2,1)}, u32[]{:S(2)}, u32[]{:S(2)}) collective-permute-start(bf16[448,1280]{1,0:T(8,128)(2,1)S(1)} %copy-done.7), channel_id=1, source_target_pairs={{0,1},{1,0},{2,3},{3,2},{4,5},{5,4},{6,7},{7,6},{8,9},{9,8},{10,11... | collective-permute-start | bytes 3440648 | tf_op jit(solution)/shard_map/ppermute | solution.py:192
  161.8 13.3 %all-to-all-done.3 = bf16[4,128,1280]{2,1,0:T(8,128)(2,1)S(1)} async-done(((bf16[4,128,1280]{2,1,0:T(8,128)(2,1)}), bf16[4,128,1280]{2,1,0:T(8,128)(2,1)S(1)}, u32[]{:S(2)}, u32[]{:S(2)}) %all-to-all-start.3) | async-done | bytes 1310752 | tf_op jit(solution)/shard_map/all_to_all | solution.py:172
  175.1 3.2 %fusion.17 = f32[512,896]{1,0:T(8,128)S(1)} fusion(bf16[512,1280]{1,0:T(8,128)(2,1)S(1)} %bitcast.20, bf16[1280,896]{1,0:T(8,128)(2,1)} %all-gather.3.cloned.1.call-done), kind=kOutput, calls=%fused_computation.27 | convolution fusion | flops 1174405120 | bytes 5439488 | tf_op jit(solution)/shard_map/dot_general | solution.py:216
  178.3 3.2 %fusion.18 = f32[512,896]{1,0:T(8,128)S(1)} fusion(bf16[512,1280]{1,0:T(8,128)(2,1)S(1)} %bitcast.21, bf16[1280,896]{1,0:T(8,128)(2,1)} %collective-permute-done.2), kind=kOutput, calls=%fused_computation.28 | convolution fusion | flops 1174405120 | bytes 5439488 | tf_op jit(solution)/shard_map/dot_general | solution.py:216
  181.5 5.9 %collective-permute-done.1 = bf16[448,1280]{1,0:T(8,128)(2,1)} collective-permute-done((bf16[448,1280]{1,0:T(8,128)(2,1)S(1)}, bf16[448,1280]{1,0:T(8,128)(2,1)}, u32[]{:S(2)}, u32[]{:S(2)}) %collective-permute-start.1) | collective-permute-done | bytes 1146912 | tf_op jit(solution)/shard_map/ppermute | solution.py:192
  187.3 1.1 fusion.3
  188.4 3.5 %fusion.2 = bf16[512,1280]{1,0:T(8,128)(2,1)} fusion(f32[512,1280]{1,0:T(8,128)S(1)} %fusion.3, bf16[448,1280]{1,0:T(8,128)(2,1)S(1)} %copy-done.7, bf16[448,1280]{1,0:T(8,128)(2,1)} %collective-permute-done.1, pred[]{:T(512)S(6)} %eq.3, f32[512,896]{1,0:T(8,128)S(1)} %fusion.17), kind=kOutput, calls=%fused_computation.4 | convolution fusion | flops 591773696 | bytes 8323073 | tf_op jit(solution)/shard_map/dot_general | solution.py:218
  191.9 3.9 %all-to-all-start.4 = ((bf16[4,128,1280]{2,1,0:T(8,128)(2,1)}), bf16[4,128,1280]{2,1,0:T(8,128)(2,1)S(1)}, u32[]{:S(2)}, u32[]{:S(2)}) async-start(bf16[4,128,1280]{2,1,0:T(8,128)(2,1)} %bitcast.8), calls=%async_computation.4 | async-start | bytes 2621440 | tf_op jit(solution)/shard_map/all_to_all | solution.py:224
  195.9 16.2 %all-to-all-done.4 = bf16[4,128,1280]{2,1,0:T(8,128)(2,1)S(1)} async-done(((bf16[4,128,1280]{2,1,0:T(8,128)(2,1)}), bf16[4,128,1280]{2,1,0:T(8,128)(2,1)S(1)}, u32[]{:S(2)}, u32[]{:S(2)}) %all-to-all-start.4) | async-done | bytes 1310752 | tf_op jit(solution)/shard_map/all_to_all | solution.py:224
  212.3 0.8 fusion.14
  (39 shorter events, 3.4 us)
Async XLA Ops:
  7.2 12.0 %copy-start.3 = (f32[20,160]{1,0:T(8,128)S(1)}, f32[20,160]{1,0:T(8,128)}, u32[]{:S(2)}) copy-start(f32[20,160]{1,0:T(8,128)} %param.13) | copy-start | bytes 38404
  7.2 12.0 %copy-start.4 = (f32[20,240]{1,0:T(8,128)S(1)}, f32[20,240]{1,0:T(8,128)}, u32[]{:S(2)}) copy-start(f32[20,240]{1,0:T(8,128)} %param.12) | copy-start | bytes 57604
  9.0 17.7 %all-to-all-start = ((bf16[8,20,896]{2,1,0:T(8,128)(2,1)}), bf16[8,20,896]{2,1,0:T(8,128)(2,1)S(1)}, u32[]{:S(2)}, u32[]{:S(2)}) async-start(bf16[8,20,896]{2,1,0:T(8,128)(2,1)} %broadcast_in_dim.43), calls=%async_computation | async-start | bytes 688128 | tf_op jit(solution)/shard_map/all_to_all | solution.py:172
  55.7 86.9 %copy-start.6 = (f32[1280]{0:T(1024)S(1)}, f32[1280]{0:T(1024)}, u32[]{:S(2)}) copy-start(f32[1280]{0:T(1024)} %param.17) | copy-start | bytes 15364
  55.7 87.1 %copy-start.5 = (f32[1280]{0:T(1024)S(1)}, f32[1280]{0:T(1024)}, u32[]{:S(2)}) copy-start(f32[1280]{0:T(1024)} %param.16) | copy-start | bytes 15364
  55.7 87.2 %copy-start = (bf16[1,128,1280]{2,1,0:T(8,128)(2,1)S(1)}, bf16[1,128,1280]{2,1,0:T(8,128)(2,1)}, u32[]{:S(2)}) copy-start(bf16[1,128,1280]{2,1,0:T(8,128)(2,1)} %param.10) | copy-start | bytes 983044
  55.7 87.2 %copy-start.1 = (f32[32,128]{1,0:T(8,128)S(1)}, f32[32,128]{1,0:T(8,128)}, u32[]{:S(2)}) copy-start(f32[32,128]{1,0:T(8,128)} %constant.33.clone.cos_ref) | copy-start | bytes 49156
  55.7 87.2 %copy-start.2 = (f32[32,128]{1,0:T(8,128)S(1)}, f32[32,128]{1,0:T(8,128)}, u32[]{:S(2)}) copy-start(f32[32,128]{1,0:T(8,128)} %constant.34.clone.sin_ref) | copy-start | bytes 49156
  55.7 63.0 %all-to-all-start.2 = ((bf16[16,200,640]{2,1,0:T(8,128)(2,1)}), bf16[16,200,640]{2,1,0:T(8,128)(2,1)}, u32[]{:S(2)}, u32[]{:S(2)}) async-start(bf16[16,200,640]{2,1,0:T(8,128)(2,1)} %broadcast_in_dim.45), calls=%async_computation.2 | async-start | bytes 8192000 | tf_op jit(solution)/shard_map/all_to_all | solution.py:172
  62.6 68.5 %all-gather.3.cloned.1.call-start = ((), (), s32[]{:S(2)}) async-start(), calls=%async_computation.5 | async-start | bytes 2437120 | tf_op jit(solution)/shard_map/all_gather | solution.py:191
  118.7 24.1 %collective-permute-start = (bf16[16,200,640]{2,1,0:T(8,128)(2,1)}, bf16[16,200,640]{2,1,0:T(8,128)(2,1)}, u32[]{:S(2)}, u32[]{:S(2)}) collective-permute-start(bf16[16,200,640]{2,1,0:T(8,128)(2,1)} %all-to-all-done.2.own_ref), channel_id=1, source_target_pairs={{0,8},{8,0},{1,9},{9,1},{2,10},{10,2},{3,11},{11,3},{4,12},{12,4},... | collective-permute-start | bytes 12288008 | tf_op jit(solution)/shard_map/ppermute | solution.py:205
  131.1 47.2 %collective-permute-start.2 = (bf16[1280,896]{1,0:T(8,128)(2,1)}, bf16[1280,896]{1,0:T(8,128)(2,1)}, u32[]{:S(2)}, u32[]{:S(2)}) collective-permute-start(bf16[1280,896]{1,0:T(8,128)(2,1)} %all-gather.3.cloned.1.call-done), channel_id=1, source_target_pairs={{0,8},{8,0},{1,9},{9,1},{2,10},{10,2},{3,11},{11,3},{4,12},{12,4},... | collective-permute-start | bytes 6881288 | tf_op jit(solution)/shard_map/ppermute | solution.py:206
  153.0 4.3 %copy-start.7 = (bf16[448,1280]{1,0:T(8,128)(2,1)S(1)}, bf16[448,1280]{1,0:T(8,128)(2,1)}, u32[]{:S(2)}) copy-start(bf16[448,1280]{1,0:T(8,128)(2,1)} %param.15) | copy-start | bytes 3440644
  153.0 22.1 %all-to-all-start.3 = ((bf16[4,128,1280]{2,1,0:T(8,128)(2,1)}), bf16[4,128,1280]{2,1,0:T(8,128)(2,1)S(1)}, u32[]{:S(2)}, u32[]{:S(2)}) async-start(bf16[4,128,1280]{2,1,0:T(8,128)(2,1)} %broadcast_in_dim.48), calls=%async_computation.3 | async-start | bytes 2621440 | tf_op jit(solution)/shard_map/all_to_all | solution.py:172
  157.3 30.1 %collective-permute-start.1 = (bf16[448,1280]{1,0:T(8,128)(2,1)S(1)}, bf16[448,1280]{1,0:T(8,128)(2,1)}, u32[]{:S(2)}, u32[]{:S(2)}) collective-permute-start(bf16[448,1280]{1,0:T(8,128)(2,1)S(1)} %copy-done.7), channel_id=1, source_target_pairs={{0,1},{1,0},{2,3},{3,2},{4,5},{5,4},{6,7},{7,6},{8,9},{9,8},{10,11... | collective-permute-start | bytes 3440648 | tf_op jit(solution)/shard_map/ppermute | solution.py:192
  191.9 20.1 %all-to-all-start.4 = ((bf16[4,128,1280]{2,1,0:T(8,128)(2,1)}), bf16[4,128,1280]{2,1,0:T(8,128)(2,1)S(1)}, u32[]{:S(2)}, u32[]{:S(2)}) async-start(bf16[4,128,1280]{2,1,0:T(8,128)(2,1)} %bitcast.8), calls=%async_computation.4 | async-start | bytes 2621440 | tf_op jit(solution)/shard_map/all_to_all | solution.py:224
Sparse Core Ops, SparseCore 0:
  66.1 64.9 all-gather.2

commit v2 on v1

--- a/solution.py
+++ b/solution.py
@@ -47,27 +47,20 @@
     other_ref,
     cos_ref,
     sin_ref,
-    gain_in_ref,
-    gain_mid_ref,
-    middle_ref,
-    normed_ref,
+    gain_ref,
+    attended_ref,
     cache_ref,
     qkv,
-    attended,
-    mid,
 ):
     length = length_ref[0]
     core = core_ref[0]
-    halves = ((own_ref, core), (other_ref, 1 - core))
     stream = tokens_ref[...].astype(F32)
     square = jnp.mean(stream * stream, axis=-1, keepdims=True)
-    normed = (stream * lax.rsqrt(square + 1e-05) * gain_in_ref[...]).astype(BF16)
+    normed = (stream * lax.rsqrt(square + 1e-05) * gain_ref[...]).astype(BF16)
     low, high = normed[:, :KHALF], normed[:, KHALF:]
-    for weights, half in halves:
+    for weights, half in ((own_ref, core), (other_ref, 1 - core)):
         for s in range(8):
-            rows = dot_nt(weights[s, OW : OW + QW, :], low) + dot_nt(
-                weights[8 + s, OW : OW + QW, :], high
-            )
+            rows = dot_nt(weights[s], low) + dot_nt(weights[8 + s], high)
             start = pl.multiple_of((2 * s + half) * QW, 8)
             qkv[pl.ds(start, QW), :] = rows.astype(BF16).astype(F32)
     cosine = cos_ref[...]
@@ -101,16 +94,31 @@
         out = dot_nn(values, probability).astype(BF16)
         for h in range(4):
             row = (4 * g + h) * HEAD_SIZE
-            attended[row : row + HEAD_SIZE, :] = out[:, h * LMAX : (h + 1) * LMAX]
+            attended_ref[row : row + HEAD_SIZE, :] = out[:, h * LMAX : (h + 1) * LMAX]
     live = (lax.broadcasted_iota(jnp.int32, (LMAX, LMAX), 0) < length).astype(F32)
     for j in range(5):
         row = QUERY_HEADS * HEAD_SIZE + j * LMAX
         block = qkv[row : row + LMAX, :].T
         cache_ref[:, j * LMAX : (j + 1) * LMAX] = (live * block).astype(BF16)
-    low, high = attended[:KHALF, :], attended[KHALF:, :]
-    for weights, half in halves:
+
+
+def middle_kernel(
+    core_ref,
+    tokens_ref,
+    attended_ref,
+    own_ref,
+    other_ref,
+    gain_ref,
+    middle_ref,
+    normed_ref,
+    mid,
+    moved,
+):
+    core = core_ref[0]
+    low, high = attended_ref[:KHALF, :], attended_ref[KHALF:, :]
+    for weights, half in ((own_ref, core), (other_ref, 1 - core)):
         for s in range(8):
-            rows = dot_nn(weights[s, :OW, :], low) + dot_nn(weights[8 + s, :OW, :], high)
+            rows = dot_nn(weights[s], low) + dot_nn(weights[8 + s], high)
             start = pl.multiple_of((2 * s + half) * OW, 8)
             mid[pl.ds(start, OW), :] = rows
     total = jnp.zeros((1, LMAX), F32)
@@ -124,47 +132,54 @@
     for j in range(16):
         for lo in range(2):
             start = lo * KHALF + j * 40
-            block = mid[start : start + 40, :] * scale * gain_mid_ref[start : start + 40, :]
-            qkv[j * 80 + lo * 40 : j * 80 + lo * 40 + 40, :] = block
+            block = mid[start : start + 40, :] * scale * gain_ref[start : start + 40, :]
+            moved[j * 80 + lo * 40 : j * 80 + lo * 40 + 40, :] = block
     for j in range(10):
         cols = slice(j * LMAX, (j + 1) * LMAX)
-        normed_ref[:, cols] = qkv[cols, :].T.astype(BF16)
-
-
-def attention(length, core, tokens, own, other, gain_in, gain_mid):
+        normed_ref[:, cols] = moved[cols, :].T.astype(BF16)
+
+
+VMEM = pl.BlockSpec(memory_space=pltpu.VMEM)
+SMEM = pl.BlockSpec(memory_space=pltpu.SMEM)
+
+
+def attention(length, core, tokens, own, other, gain):
     cosine, sine = tables()
-    vmem = pl.BlockSpec(memory_space=pltpu.VMEM)
-    smem = pl.BlockSpec(memory_space=pltpu.SMEM)
     return pl.pallas_call(
         attention_kernel,
         out_shape=(
+            jax.ShapeDtypeStruct((D, LMAX), BF16),
+            jax.ShapeDtypeStruct((LMAX, 640), BF16),
+        ),
+        in_specs=[SMEM, SMEM] + [VMEM] * 6,
+        out_specs=(VMEM, VMEM),
+        scratch_shapes=[pltpu.VMEM((1920, LMAX), F32)],
+        compiler_params=pltpu.CompilerParams(vmem_limit_bytes=32 << 20),
+        cost_estimate=pl.CostEstimate(
+            flops=800000000, bytes_accessed=6000000, transcendentals=400000
+        ),
+        name="attention",
+    )(
+        length, core, tokens, own, other, jnp.asarray(cosine), jnp.asarray(sine), gain[None, :]
+    )
+
+
+def middle_rows(core, tokens, attended, own, other, gain):
+    return pl.pallas_call(
+        middle_kernel,
+        out_shape=(
             jax.ShapeDtypeStruct((LMAX, D), F32),
             jax.ShapeDtypeStruct((LMAX, D), BF16),
-            jax.ShapeDtypeStruct((LMAX, 640), BF16),
-        ),
-        in_specs=[smem, smem] + [vmem] * 7,
-        out_specs=(vmem, vmem, vmem),
-        scratch_shapes=[
-            pltpu.VMEM((1920, LMAX), F32),
-            pltpu.VMEM((D, LMAX), BF16),
-            pltpu.VMEM((D, LMAX), F32),
-        ],
+        ),
+        in_specs=[SMEM] + [VMEM] * 5,
+        out_specs=(VMEM, VMEM),
+        scratch_shapes=[pltpu.VMEM((D, LMAX), F32), pltpu.VMEM((D, LMAX), F32)],
         compiler_params=pltpu.CompilerParams(vmem_limit_bytes=32 << 20),
         cost_estimate=pl.CostEstimate(
-            flops=1200000000, bytes_accessed=10000000, transcendentals=400000
-        ),
-        name="attention",
-    )(
-        length,
-        core,
-        tokens,
-        own,
-        other,
-        jnp.asarray(cosine),
-        jnp.asarray(sine),
-        gain_in[None, :],
-        gain_mid[:, None],
-    )
+            flops=420000000, bytes_accessed=4000000, transcendentals=1000
+        ),
+        name="middle",
+    )(core, tokens, attended, own, other, gain[:, None])
 
 
 def spread(block, axes, count):
@@ -184,12 +199,12 @@
 ):
     core = lax.axis_index("core")
     x_hi = lax.axis_index("x_hi")
+    core_at = core.astype(jnp.int32)[None]
     tokens = prompts[0]
     gate_up = gate_up_master.astype(BF16).reshape(20, 2 * UNITS)
     near = spread(gate_up, ("x_lo", "core", "x_hi"), 8).reshape(4, 2, 20, 2 * UNITS)
     near = lax.dynamic_index_in_dim(near, core, axis=1, keepdims=False).reshape(80, 2 * UNITS)
     gate_up_own = lax.all_gather(near, "z", axis=0, tiled=True)
-    down_other = lax.ppermute(down_weight, "x_hi", SWAP)
     merged = jnp.concatenate([out_master, qkv_master], axis=1).astype(BF16)
     merged = lax.all_gather(merged, "core", axis=0, tiled=True)
     part = jnp.concatenate(
@@ -199,14 +214,16 @@
         ],
         axis=1,
     )
-    part = after(part, near)
-    part = spread(part, "z", 16).reshape(KHALF, OW + QW).T
-    own = spread(part, ("x_lo", "y", "x_hi"), 16)
-    other = lax.ppermute(own, "core", SWAP)
-    gate_up_other = lax.ppermute(after(gate_up_own, own), "core", SWAP)
-    middle, normed_mid, cache = attention(
-        lengths, core.astype(jnp.int32)[None], tokens, own, other, attn_gain, mlp_gain
-    )
+    part = spread(after(part, near), "z", 16).reshape(KHALF, OW + QW).T
+    down_other = lax.ppermute(down_weight, "x_hi", SWAP)
+    qkv_own = spread(after(part[OW:], down_other), ("x_lo", "y", "x_hi"), 16)
+    out_own = spread(after(part[:OW], qkv_own), ("x_lo", "y", "x_hi"), 16)
+    qkv_other = lax.ppermute(qkv_own, "core", SWAP)
+    attended, cache = attention(lengths, core_at, tokens, qkv_own, qkv_other, attn_gain)
+    out_own = after(out_own, attended)
+    out_other = lax.ppermute(out_own, "core", SWAP)
+    middle, normed_mid = middle_rows(core_at, tokens, attended, out_own, out_other, mlp_gain)
+    gate_up_other = lax.ppermute(after(gate_up_own, normed_mid), "core", SWAP)
     gathered = spread(normed_mid, "y", 4).reshape(4 * LMAX, D)
     same = core == x_hi
     down_first = jnp.where(same, down_weight, down_other)

time: 222 us -> 210 us (0.946)
  waiting for transfers between devices: 106 us -> 88.4 us
    all_gather x1, waiting for transfers between devices: 8.95 us -> 0.02 us  [shards(): gate_up_own = lax.all_gather(near, 'z', axis=0, tiled=True)]
    all_to_all x3 -> x4, waiting for transfers between devices: 73.8 us -> 67.6 us  [spread(): return lax.all_to_all(copies, axes, 0, 0, tiled=False)]
    ppermute x1, waiting for transfers between devices: 5.87 us -> 0.01 us  [shards(): down_other = lax.ppermute(down_weight, 'x_hi', SWAP)]
    ppermute x2 -> x3, waiting for transfers between devices: 0.01 us -> 3.08 us  [the longest x1 3.08 us: shards(): out_other = lax.ppermute(out_own, 'core', SWAP)]
    all_to_all x3 -> x4, starting transfers between devices: 21.4 us -> 24.4 us  [spread(): return lax.all_to_all(copies, axes, 0, 0, tiled=False)]
    broadcast_in_dim x5 -> x6, local copies, waits for them, and re-layouts: 4.32 us -> 5.01 us  [spread(): copies = jnp.broadcast_to(block[None], (count,) + block.shape)]
    ppermute x2 -> x3, starting transfers between devices: 14.3 us -> 13.6 us  [the longest x1 8.31 us: shards(): qkv_other = lax.ppermute(qkv_own, 'core', SWAP)]
    pallas_call x1 -> x2, Pallas kernels: 8.98 us -> 8.84 us  [the longest x1 5.89 us: attention(): pl.pallas_call(attention_kernel, out_shape=(jax.ShapeDtypeStruct((D, LMAX...]
  transfers between devices with their start and end apart: 8 -> 10, of which waited for: 6 -> 5; matrix products, arithmetic and copies ran while one was open for 4% -> 4% of each run, Pallas kernels for 4% -> 4%
where the time goes in v2:
time: 210 us; the launch traced here: 207 us
  waiting for transfers between devices  88.4 us (42%)
  starting transfers between devices  46.4 us (22%)
  blocking collectives  27.9 us (13%)
  between operations  15 us (7%)
  matrix products  9.77 us (5%)
  Pallas kernels  8.84 us (4%)
  local copies, waits for them, and re-layouts  6.68 us (3%)
  other arithmetic  3.58 us (2%)
    all_to_all x4, waiting for transfers between devices, spread(): return lax.all_to_all(copies, axes, 0, 0, tiled=False)  67.6 us
    all_to_all x1, blocking collectives, spread(): return lax.all_to_all(copies, axes, 0, 0, tiled=False)  25.8 us
    all_to_all x4, starting transfers between devices, spread(): return lax.all_to_all(copies, axes, 0, 0, tiled=False)  24.4 us
    all_to_all x1, waiting for transfers between devices, shards(): partial = lax.all_to_all(partial, 'y', 0, 0, tiled=False)  16.9 us
    ppermute x1, starting transfers between devices, shards(): qkv_other = lax.ppermute(qkv_own, 'core', SWAP)  8.31 us
    dot_general x2, matrix products, units_block(): gate_up = jnp.dot(gathered, gate_up_rows, preferred_element_type=F32)  6.47 us
    pallas_call x1, Pallas kernels, attention(): pl.pallas_call(attention_kernel, out_shape=(jax.ShapeDtypeStruct((D, LMAX...  5.89 us
    broadcast_in_dim x6, local copies, waits for them, and re-layouts, spread(): copies = jnp.broadcast_to(block[None], (count,) + block.shape)  5.01 us
  transfers between devices with their start and end apart: 10, of which 5 were waited for; matrix products, arithmetic and copies ran while one was open for 4% of the time, Pallas kernels for 4%

profile of v2, /device:TPU:1, one launch (start us, length us, event | category | flops | bytes accessed | tf_op | source)
XLA Modules:
  0.0 206.5 jit_solution(13936557392971365498)
XLA Ops:
  8.9 10.2 %all-to-all-start = ((bf16[8,20,896]{2,1,0:T(8,128)(2,1)}), bf16[8,20,896]{2,1,0:T(8,128)(2,1)S(1)}, u32[]{:S(2)}, u32[]{:S(2)}) async-start(bf16[8,20,896]{2,1,0:T(8,128)(2,1)} %broadcast_in_dim.24), calls=%async_computation | async-start | bytes 688128 | tf_op jit(solution)/shard_map/all_to_all | solution.py:187
  19.2 4.8 %collective-permute-start = (bf16[448,1280]{1,0:T(8,128)(2,1)}, bf16[448,1280]{1,0:T(8,128)(2,1)S(1)}, u32[]{:S(2)}, u32[]{:S(2)}) collective-permute-start(bf16[448,1280]{1,0:T(8,128)(2,1)} %param.15), channel_id=1, source_target_pairs={{0,1},{1,0},{2,3},{3,2},{4,5},{5,4},{6,7},{7,6},{8,9},{9,8},{10,11... | collective-permute-start | bytes 3440648 | tf_op jit(solution)/shard_map/ppermute | solution.py:218
  25.5 2.1 %all-gather = bf16[2,20,400]{2,1,0:T(8,128)(2,1)S(1)} all-gather(bf16[1,20,400]{2,1,0:T(8,128)(2,1)S(1)} %maximum_bitcast_fusion), channel_id=1, replica_groups=mesh['x_lo'=2,'z'=16,'core'=2,'y'=4,'x_hi'=2] {'core'}, dimensions={0}, use_global_device_ids=true | all-gather | bytes 48000 | tf_op jit(solution)/shard_map/all_gather | solution.py:209
  28.8 25.8 %all_to_all.30 = bf16[16,40,200]{2,1,0:T(8,128)(2,1)S(1)} all-to-all(bf16[16,40,200]{2,1,0:T(8,128)(2,1)S(1)} %broadcast_in_dim.50), channel_id=1, replica_groups=mesh['x_lo'=2,'z'=16,'core'=2,'y'=4,'x_hi'=2] {'z'}, dimensions={0} | all-to-all | bytes 512000 | tf_op jit(solution)/shard_map/all_to_all | solution.py:187
  54.8 1.6 broadcast_in_dim.51
  56.5 4.9 %all-to-all-start.2 = ((bf16[16,120,640]{2,1,0:T(8,128)(2,1)}), bf16[16,120,640]{2,1,0:T(8,128)(2,1)S(1)}, u32[]{:S(2)}, u32[]{:S(2)}) async-start(bf16[16,120,640]{2,1,0:T(8,128)(2,1)} %broadcast_in_dim.51), calls=%async_computation.2 | async-start | bytes 4915200 | tf_op jit(solution)/shard_map/all_to_all | solution.py:187
  62.1 29.1 %all-to-all-done.2.own_ref = bf16[16,120,640]{2,1,0:T(8,128)(2,1)S(1)} async-done(((bf16[16,120,640]{2,1,0:T(8,128)(2,1)}), bf16[16,120,640]{2,1,0:T(8,128)(2,1)S(1)}, u32[]{:S(2)}, u32[]{:S(2)}) %all-to-all-start.2) | async-done | bytes 2457632 | tf_op jit(solution)/shard_map/all_to_all | solution.py:187
  91.3 8.3 %collective-permute-start.1 = (bf16[16,120,640]{2,1,0:T(8,128)(2,1)S(1)}, bf16[16,120,640]{2,1,0:T(8,128)(2,1)}, u32[]{:S(2)}, u32[]{:S(2)}) collective-permute-start(bf16[16,120,640]{2,1,0:T(8,128)(2,1)S(1)} %all-to-all-done.2.own_ref), channel_id=1, source_target_pairs={{0,8},{8,0},{1,9},{9,1},{2,10},{10,2},{3,11},{11,3},{4,12},{12,4},... | collective-permute-start | bytes 7372808 | tf_op jit(solution)/shard_map/ppermute | solution.py:221
  99.7 1.3 broadcast_in_dim.53
  101.1 5.8 %all-to-all-start.3 = ((bf16[16,80,640]{2,1,0:T(8,128)(2,1)}), bf16[16,80,640]{2,1,0:T(8,128)(2,1)}, u32[]{:S(2)}, u32[]{:S(2)}) async-start(bf16[16,80,640]{2,1,0:T(8,128)(2,1)} %broadcast_in_dim.53), calls=%async_computation.3 | async-start | bytes 3276800 | tf_op jit(solution)/shard_map/all_to_all | solution.py:187
  107.6 5.9 %attention.1 = (bf16[1280,128]{1,0:T(8,128)(2,1)S(1)}, bf16[128,640]{1,0:T(8,128)(2,1)}) custom-call(s32[1]{0:T(128)} %copy.28.length_ref, s32[1]{0:T(128)} %bitcast.1.core_ref, bf16[128,1280]{1,0:T(8,128)(2,1)S(1)} %bitcast.19, bf16[16,120,640]{2,1,0:T(8,128)(2,1)S(1)} %all-to-all-done.2.own_ref, bf16[16,120,640]{2,1,0:T(8,128)(2,1)} %collective-permute-done.1.other_ref, ...), custom_call_target="tpu_custom_call" | custom-call | flops 800000000 | bytes 6000000 | tf_op jit(solution)/shard_map/attention/pallas_call | solution.py:148
  113.5 20.6 %all-to-all-done.3.own_ref = bf16[16,80,640]{2,1,0:T(8,128)(2,1)} async-done(((bf16[16,80,640]{2,1,0:T(8,128)(2,1)}), bf16[16,80,640]{2,1,0:T(8,128)(2,1)}, u32[]{:S(2)}, u32[]{:S(2)}) %all-to-all-start.3) | async-done | bytes 1638432 | tf_op jit(solution)/shard_map/all_to_all | solution.py:187
  134.1 3.0 %collective-permute-start.2 = (bf16[16,80,640]{2,1,0:T(8,128)(2,1)}, bf16[16,80,640]{2,1,0:T(8,128)(2,1)S(1)}, u32[]{:S(2)}, u32[]{:S(2)}) collective-permute-start(bf16[16,80,640]{2,1,0:T(8,128)(2,1)} %all-to-all-done.3.own_ref), channel_id=1, source_target_pairs={{0,8},{8,0},{1,9},{9,1},{2,10},{10,2},{3,11},{11,3},{4,12},{12,4},... | collective-permute-start | bytes 4915208 | tf_op jit(solution)/shard_map/ppermute | solution.py:224
  137.4 3.1 %collective-permute-done.2.other_ref = bf16[16,80,640]{2,1,0:T(8,128)(2,1)S(1)} collective-permute-done((bf16[16,80,640]{2,1,0:T(8,128)(2,1)}, bf16[16,80,640]{2,1,0:T(8,128)(2,1)S(1)}, u32[]{:S(2)}, u32[]{:S(2)}) %collective-permute-start.2) | collective-permute-done | bytes 1638432 | tf_op jit(solution)/shard_map/ppermute | solution.py:224
  140.4 3.0 %middle.1 = (f32[128,1280]{1,0:T(8,128)S(1)}, bf16[128,1280]{1,0:T(8,128)(2,1)S(1)}) custom-call(s32[1]{0:T(128)} %bitcast.1.core_ref, bf16[128,1280]{1,0:T(8,128)(2,1)S(1)} %bitcast.20, bf16[1280,128]{1,0:T(8,128)(2,1)S(1)} %get-tuple-element.13.attended_ref, bf16[16,80,640]{2,1,0:T(8,128)(2,1)} %all-to-all-done.3.own_ref, ...), custom_call_target="tpu_custom_call" | custom-call | flops 420000000 | bytes 4000000 | tf_op jit(solution)/shard_map/middle/pallas_call | solution.py:168
  143.4 2.3 %collective-permute-start.3 = (bf16[1280,896]{1,0:T(8,128)(2,1)}, bf16[1280,896]{1,0:T(8,128)(2,1)}, u32[]{:S(2)}, u32[]{:S(2)}) collective-permute-start(bf16[1280,896]{1,0:T(8,128)(2,1)} %all-gather.3.cloned.1.call-done), channel_id=1, source_target_pairs={{0,8},{8,0},{1,9},{9,1},{2,10},{10,2},{3,11},{11,3},{4,12},{12,4},... | collective-permute-start | bytes 6881288 | tf_op jit(solution)/shard_map/ppermute | solution.py:226
  145.7 1.2 broadcast_in_dim.55
  146.9 3.5 %all-to-all-start.4 = ((bf16[4,128,1280]{2,1,0:T(8,128)(2,1)}), bf16[4,128,1280]{2,1,0:T(8,128)(2,1)S(1)}, u32[]{:S(2)}, u32[]{:S(2)}) async-start(bf16[4,128,1280]{2,1,0:T(8,128)(2,1)} %broadcast_in_dim.55), calls=%async_computation.4 | async-start | bytes 2621440 | tf_op jit(solution)/shard_map/all_to_all | solution.py:187
  150.4 17.9 %all-to-all-done.4 = bf16[4,128,1280]{2,1,0:T(8,128)(2,1)S(1)} async-done(((bf16[4,128,1280]{2,1,0:T(8,128)(2,1)}), bf16[4,128,1280]{2,1,0:T(8,128)(2,1)S(1)}, u32[]{:S(2)}, u32[]{:S(2)}) %all-to-all-start.4) | async-done | bytes 1310752 | tf_op jit(solution)/shard_map/all_to_all | solution.py:187
  168.3 3.2 %fusion.17 = f32[512,896]{1,0:T(8,128)S(1)} fusion(bf16[512,1280]{1,0:T(8,128)(2,1)S(1)} %bitcast.21, bf16[1280,896]{1,0:T(8,128)(2,1)} %all-gather.3.cloned.1.call-done), kind=kOutput, calls=%fused_computation.27 | convolution fusion | flops 1174405120 | bytes 5439488 | tf_op jit(solution)/shard_map/dot_general | solution.py:233
  171.5 3.3 %fusion.18 = f32[512,896]{1,0:T(8,128)S(1)} fusion(bf16[512,1280]{1,0:T(8,128)(2,1)S(1)} %bitcast.22, bf16[1280,896]{1,0:T(8,128)(2,1)} %collective-permute-done.3), kind=kOutput, calls=%fused_computation.28 | convolution fusion | flops 1174405120 | bytes 5439488 | tf_op jit(solution)/shard_map/dot_general | solution.py:233
  176.0 2.2 %fusion.2 = bf16[512,1280]{1,0:T(8,128)(2,1)} fusion(f32[512,1280]{1,0:T(8,128)S(1)} %fusion.3, bf16[448,1280]{1,0:T(8,128)(2,1)S(1)} %copy-done.5, bf16[448,1280]{1,0:T(8,128)(2,1)S(1)} %copy-done.7, pred[]{:T(512)S(6)} %eq.3, f32[512,896]{1,0:T(8,128)S(1)} %fusion.17), kind=kOutput, calls=%fused_computation.4 | convolution fusion | flops 591773696 | bytes 8323073 | tf_op jit(solution)/shard_map/dot_general | solution.py:235
  178.1 3.5 %all-to-all-start.5 = ((bf16[4,128,1280]{2,1,0:T(8,128)(2,1)}), bf16[4,128,1280]{2,1,0:T(8,128)(2,1)S(1)}, u32[]{:S(2)}, u32[]{:S(2)}) async-start(bf16[4,128,1280]{2,1,0:T(8,128)(2,1)} %bitcast.9), calls=%async_computation.5 | async-start | bytes 2621440 | tf_op jit(solution)/shard_map/all_to_all | solution.py:241
  181.7 16.9 %all-to-all-done.5 = bf16[4,128,1280]{2,1,0:T(8,128)(2,1)S(1)} async-done(((bf16[4,128,1280]{2,1,0:T(8,128)(2,1)}), bf16[4,128,1280]{2,1,0:T(8,128)(2,1)S(1)}, u32[]{:S(2)}, u32[]{:S(2)}) %all-to-all-start.5) | async-done | bytes 1310752 | tf_op jit(solution)/shard_map/all_to_all | solution.py:241
  (48 shorter events, 8.0 us)
Async XLA Ops:
  8.9 19.1 %all-to-all-start = ((bf16[8,20,896]{2,1,0:T(8,128)(2,1)}), bf16[8,20,896]{2,1,0:T(8,128)(2,1)S(1)}, u32[]{:S(2)}, u32[]{:S(2)}) async-start(bf16[8,20,896]{2,1,0:T(8,128)(2,1)} %broadcast_in_dim.24), calls=%async_computation | async-start | bytes 688128 | tf_op jit(solution)/shard_map/all_to_all | solution.py:187
  19.2 35.5 %collective-permute-start = (bf16[448,1280]{1,0:T(8,128)(2,1)}, bf16[448,1280]{1,0:T(8,128)(2,1)S(1)}, u32[]{:S(2)}, u32[]{:S(2)}) collective-permute-start(bf16[448,1280]{1,0:T(8,128)(2,1)} %param.15), channel_id=1, source_target_pairs={{0,1},{1,0},{2,3},{3,2},{4,5},{5,4},{6,7},{7,6},{8,9},{9,8},{10,11... | collective-permute-start | bytes 3440648 | tf_op jit(solution)/shard_map/ppermute | solution.py:218
  54.7 1.8 copy-start.6
  56.5 34.8 %all-to-all-start.2 = ((bf16[16,120,640]{2,1,0:T(8,128)(2,1)}), bf16[16,120,640]{2,1,0:T(8,128)(2,1)S(1)}, u32[]{:S(2)}, u32[]{:S(2)}) async-start(bf16[16,120,640]{2,1,0:T(8,128)(2,1)} %broadcast_in_dim.51), calls=%async_computation.2 | async-start | bytes 4915200 | tf_op jit(solution)/shard_map/all_to_all | solution.py:187
  61.4 82.0 %all-gather.3.cloned.1.call-start = ((), (), s32[]{:S(2)}) async-start(), calls=%async_computation.6 | async-start | bytes 2437120 | tf_op jit(solution)/shard_map/all_gather | solution.py:207
  91.3 16.2 %collective-permute-start.1 = (bf16[16,120,640]{2,1,0:T(8,128)(2,1)S(1)}, bf16[16,120,640]{2,1,0:T(8,128)(2,1)}, u32[]{:S(2)}, u32[]{:S(2)}) collective-permute-start(bf16[16,120,640]{2,1,0:T(8,128)(2,1)S(1)} %all-to-all-done.2.own_ref), channel_id=1, source_target_pairs={{0,8},{8,0},{1,9},{9,1},{2,10},{10,2},{3,11},{11,3},{4,12},{12,4},... | collective-permute-start | bytes 7372808 | tf_op jit(solution)/shard_map/ppermute | solution.py:221
  101.0 6.4 %copy-start.3 = (f32[1280]{0:T(1024)S(1)}, f32[1280]{0:T(1024)}, u32[]{:S(2)}) copy-start(f32[1280]{0:T(1024)} %param.16) | copy-start | bytes 15364
  101.0 6.5 %copy-start = (bf16[1,128,1280]{2,1,0:T(8,128)(2,1)S(1)}, bf16[1,128,1280]{2,1,0:T(8,128)(2,1)}, u32[]{:S(2)}) copy-start(bf16[1,128,1280]{2,1,0:T(8,128)(2,1)} %param.10) | copy-start | bytes 983044
  101.1 6.5 %copy-start.1 = (f32[32,128]{1,0:T(8,128)S(1)}, f32[32,128]{1,0:T(8,128)}, u32[]{:S(2)}) copy-start(f32[32,128]{1,0:T(8,128)} %constant.33.clone.cos_ref) | copy-start | bytes 49156
  101.1 6.5 %copy-start.2 = (f32[32,128]{1,0:T(8,128)S(1)}, f32[32,128]{1,0:T(8,128)}, u32[]{:S(2)}) copy-start(f32[32,128]{1,0:T(8,128)} %constant.34.clone.sin_ref) | copy-start | bytes 49156
  101.1 33.0 %all-to-all-start.3 = ((bf16[16,80,640]{2,1,0:T(8,128)(2,1)}), bf16[16,80,640]{2,1,0:T(8,128)(2,1)}, u32[]{:S(2)}, u32[]{:S(2)}) async-start(bf16[16,80,640]{2,1,0:T(8,128)(2,1)} %broadcast_in_dim.53), calls=%async_computation.3 | async-start | bytes 3276800 | tf_op jit(solution)/shard_map/all_to_all | solution.py:187
  107.6 29.6 %copy-start.4 = (f32[1280]{0:T(1024)S(1)}, f32[1280]{0:T(1024)}, u32[]{:S(2)}) copy-start(f32[1280]{0:T(1024)} %param.17) | copy-start | bytes 15364
  134.1 6.3 %collective-permute-start.2 = (bf16[16,80,640]{2,1,0:T(8,128)(2,1)}, bf16[16,80,640]{2,1,0:T(8,128)(2,1)S(1)}, u32[]{:S(2)}, u32[]{:S(2)}) collective-permute-start(bf16[16,80,640]{2,1,0:T(8,128)(2,1)} %all-to-all-done.3.own_ref), channel_id=1, source_target_pairs={{0,8},{8,0},{1,9},{9,1},{2,10},{10,2},{3,11},{11,3},{4,12},{12,4},... | collective-permute-start | bytes 4915208 | tf_op jit(solution)/shard_map/ppermute | solution.py:224
  143.4 28.1 %collective-permute-start.3 = (bf16[1280,896]{1,0:T(8,128)(2,1)}, bf16[1280,896]{1,0:T(8,128)(2,1)}, u32[]{:S(2)}, u32[]{:S(2)}) collective-permute-start(bf16[1280,896]{1,0:T(8,128)(2,1)} %all-gather.3.cloned.1.call-done), channel_id=1, source_target_pairs={{0,8},{8,0},{1,9},{9,1},{2,10},{10,2},{3,11},{11,3},{4,12},{12,4},... | collective-permute-start | bytes 6881288 | tf_op jit(solution)/shard_map/ppermute | solution.py:226
  146.9 21.4 %all-to-all-start.4 = ((bf16[4,128,1280]{2,1,0:T(8,128)(2,1)}), bf16[4,128,1280]{2,1,0:T(8,128)(2,1)S(1)}, u32[]{:S(2)}, u32[]{:S(2)}) async-start(bf16[4,128,1280]{2,1,0:T(8,128)(2,1)} %broadcast_in_dim.55), calls=%async_computation.4 | async-start | bytes 2621440 | tf_op jit(solution)/shard_map/all_to_all | solution.py:187
  171.5 3.4 %copy-start.5 = (bf16[448,1280]{1,0:T(8,128)(2,1)S(1)}, bf16[448,1280]{1,0:T(8,128)(2,1)}, u32[]{:S(2)}) copy-start(bf16[448,1280]{1,0:T(8,128)(2,1)} %param.15) | copy-start | bytes 3440644
  171.5 3.3 %copy-start.7 = (bf16[448,1280]{1,0:T(8,128)(2,1)S(1)}, bf16[448,1280]{1,0:T(8,128)(2,1)}, u32[]{:S(2)}) copy-start(bf16[448,1280]{1,0:T(8,128)(2,1)} %copy-done.6) | copy-start | bytes 3440644
  178.1 20.5 %all-to-all-start.5 = ((bf16[4,128,1280]{2,1,0:T(8,128)(2,1)}), bf16[4,128,1280]{2,1,0:T(8,128)(2,1)S(1)}, u32[]{:S(2)}, u32[]{:S(2)}) async-start(bf16[4,128,1280]{2,1,0:T(8,128)(2,1)} %bitcast.9), calls=%async_computation.5 | async-start | bytes 2621440 | tf_op jit(solution)/shard_map/all_to_all | solution.py:241
Sparse Core Ops, SparseCore 0:
  64.9 67.2 all-gather.2

commit v3 on v2

--- a/solution.py
+++ b/solution.py
@@ -15,6 +15,7 @@
 OW = 80
 KHALF = 640
 UNITS = 448
+WIDE = 384
 F32 = jnp.float32
 BF16 = jnp.bfloat16
 
@@ -136,7 +137,46 @@
             moved[j * 80 + lo * 40 : j * 80 + lo * 40 + 40, :] = block
     for j in range(10):
         cols = slice(j * LMAX, (j + 1) * LMAX)
-        normed_ref[:, cols] = moved[cols, :].T.astype(BF16)
+        block = moved[cols, :].T.astype(BF16)
+        for copy in range(4):
+            normed_ref[copy, :, cols] = block
+
+
+def hidden_kernel(
+    same_ref, tokens_ref, first_ref, second_ref, down_own_ref, down_other_ref, out_ref
+):
+    def block(tokens, gate_up_ref, down_ref):
+        gate_up = dot_nn(tokens, gate_up_ref[...])
+        gate, up = gate_up[:, :WIDE], gate_up[:, WIDE : 2 * WIDE]
+        units = (gate / (1.0 + jnp.exp(-gate)) * up).astype(BF16)
+        gate = gate_up[:, 2 * WIDE :]
+        up = pltpu.roll(gate, 64, 1)
+        rest = (gate / (1.0 + jnp.exp(-gate)) * up).astype(BF16)[:, :64]
+        total = dot_nn(units, down_ref[:WIDE, :]) + dot_nn(rest, down_ref[WIDE:, :])
+        return total.astype(BF16).astype(F32)
+
+    def run(down_first_ref, down_second_ref):
+        for prompt in range(4):
+            tokens = tokens_ref[prompt]
+            total = block(tokens, first_ref, down_first_ref)
+            total = total + block(tokens, second_ref, down_second_ref)
+            out_ref[prompt] = total.astype(BF16)
+
+    @pl.when(same_ref[0] == 1)
+    def _():
+        run(down_own_ref, down_other_ref)
+
+    @pl.when(same_ref[0] == 0)
+    def _():
+        run(down_other_ref, down_own_ref)
+
+
+def result_kernel(length_ref, middle_ref, parts_ref, out_ref):
+    feed_out = parts_ref[0].astype(F32)
+    for j in range(1, 4):
+        feed_out = feed_out + parts_ref[j].astype(F32)
+    live = lax.broadcasted_iota(jnp.int32, (LMAX, D), 0) < length_ref[0]
+    out_ref[...] = jnp.where(live, middle_ref[...] + feed_out, 0.0).astype(BF16)
 
 
 VMEM = pl.BlockSpec(memory_space=pltpu.VMEM)
@@ -169,7 +209,7 @@
         middle_kernel,
         out_shape=(
             jax.ShapeDtypeStruct((LMAX, D), F32),
-            jax.ShapeDtypeStruct((LMAX, D), BF16),
+            jax.ShapeDtypeStruct((4, LMAX, D), BF16),
         ),
         in_specs=[SMEM] + [VMEM] * 5,
         out_specs=(VMEM, VMEM),
@@ -182,6 +222,41 @@
     )(core, tokens, attended, own, other, gain[:, None])
 
 
+def hidden_rows(same, tokens, first, second, down_own, down_other):
+    return pl.pallas_call(
+        hidden_kernel,
+        out_shape=jax.ShapeDtypeStruct((4, LMAX, D), BF16),
+        in_specs=[SMEM] + [VMEM] * 5,
+        out_specs=VMEM,
+        compiler_params=pltpu.CompilerParams(vmem_limit_bytes=32 << 20),
+        cost_estimate=pl.CostEstimate(
+            flops=3500000000, bytes_accessed=9500000, transcendentals=500000
+        ),
+        name="hidden",
+    )(same, tokens, first, second, down_own, down_other)
+
+
+def result(length, middle, parts):
+    return pl.pallas_call(
+        result_kernel,
+        out_shape=jax.ShapeDtypeStruct((LMAX, D), BF16),
+        in_specs=[SMEM] + [VMEM] * 2,
+        out_specs=VMEM,
+        cost_estimate=pl.CostEstimate(flops=1000000, bytes_accessed=2300000, transcendentals=0),
+        name="result",
+    )(length, middle, parts)
+
+
+def turn(same_x):
+    pairs = []
+    for lo in range(2):
+        for core in range(2):
+            for hi in range(2):
+                to_lo = lo if same_x else 1 - lo
+                pairs.append((lo * 4 + core * 2 + hi, to_lo * 4 + hi * 2 + core))
+    return pairs
+
+
 def spread(block, axes, count):
     copies = jnp.broadcast_to(block[None], (count,) + block.shape)
     return lax.all_to_all(copies, axes, 0, 0, tiled=False)
@@ -197,51 +272,59 @@
 def shards(
     prompts, lengths, qkv_master, out_master, gate_up_master, down_weight, attn_gain, mlp_gain
 ):
-    core = lax.axis_index("core")
-    x_hi = lax.axis_index("x_hi")
-    core_at = core.astype(jnp.int32)[None]
+    core = lax.axis_index("core").astype(jnp.int32)
+    x_hi = lax.axis_index("x_hi").astype(jnp.int32)
+    x_lo = lax.axis_index("x_lo")
+    core_at = core[None]
+    same = (core == x_hi).astype(jnp.int32)[None]
     tokens = prompts[0]
-    gate_up = gate_up_master.astype(BF16).reshape(20, 2 * UNITS)
-    near = spread(gate_up, ("x_lo", "core", "x_hi"), 8).reshape(4, 2, 20, 2 * UNITS)
-    near = lax.dynamic_index_in_dim(near, core, axis=1, keepdims=False).reshape(80, 2 * UNITS)
-    gate_up_own = lax.all_gather(near, "z", axis=0, tiled=True)
-    merged = jnp.concatenate([out_master, qkv_master], axis=1).astype(BF16)
+    gate_up = gate_up_master.astype(BF16)
+    merged = jnp.concatenate(
+        [
+            out_master.astype(BF16),
+            qkv_master.astype(BF16),
+            gate_up[:, 0, :WIDE],
+            gate_up[:, 1, :WIDE],
+            gate_up[:, 0, WIDE:],
+            gate_up[:, 1, WIDE:],
+        ],
+        axis=1,
+    )
     merged = lax.all_gather(merged, "core", axis=0, tiled=True)
     part = jnp.concatenate(
         [
+            lax.dynamic_slice_in_dim(merged[:, 160:400], core * QW, QW, axis=1),
+            jnp.zeros((40, 128 - QW), BF16),
             lax.dynamic_slice_in_dim(merged[:, :160], core * OW, OW, axis=1),
-            lax.dynamic_slice_in_dim(merged[:, 160:], core * QW, QW, axis=1),
+            jnp.zeros((40, 128 - OW), BF16),
         ],
         axis=1,
     )
-    part = spread(after(part, near), "z", 16).reshape(KHALF, OW + QW).T
-    down_other = lax.ppermute(down_weight, "x_hi", SWAP)
-    qkv_own = spread(after(part[OW:], down_other), ("x_lo", "y", "x_hi"), 16)
-    out_own = spread(after(part[:OW], qkv_own), ("x_lo", "y", "x_hi"), 16)
+    part = spread(part, "z", 16).reshape(KHALF, 256)
+    rows = merged[:, 400:]
+    along = ("x_lo", "core", "x_hi")
+    near = lax.ppermute(rows, along, turn(True))
+    far = lax.ppermute(rows, along, turn(False))
+    near = jnp.where(
+        x_lo == 0, jnp.concatenate([near, far], axis=0), jnp.concatenate([far, near], axis=0)
+    )
+    gate_up_own = lax.all_gather(near, "z", axis=0, tiled=True)
+    down_other = lax.ppermute(after(down_weight, merged), "x_hi", SWAP)
+    part_qkv = after(part[:, :QW].T, near, down_other)
+    qkv_own = spread(part_qkv, ("x_lo", "y", "x_hi"), 16)
+    part_out = after(part[:, 128 : 128 + OW].T, qkv_own)
+    out_own = spread(part_out, ("x_lo", "y", "x_hi"), 16)
     qkv_other = lax.ppermute(qkv_own, "core", SWAP)
     attended, cache = attention(lengths, core_at, tokens, qkv_own, qkv_other, attn_gain)
     out_own = after(out_own, attended)
     out_other = lax.ppermute(out_own, "core", SWAP)
     middle, normed_mid = middle_rows(core_at, tokens, attended, out_own, out_other, mlp_gain)
-    gate_up_other = lax.ppermute(after(gate_up_own, normed_mid), "core", SWAP)
-    gathered = spread(normed_mid, "y", 4).reshape(4 * LMAX, D)
-    same = core == x_hi
-    down_first = jnp.where(same, down_weight, down_other)
-    down_second = jnp.where(same, down_other, down_weight)
-
-    def units_block(gate_up_rows, down_rows):
-        gate_up = jnp.dot(gathered, gate_up_rows, preferred_element_type=F32)
-        hidden_units = (jax.nn.silu(gate_up[:, :UNITS]) * gate_up[:, UNITS:]).astype(BF16)
-        return jnp.dot(hidden_units, down_rows, preferred_element_type=F32).astype(BF16)
-
-    partial = units_block(gate_up_own, down_first).astype(F32) + units_block(
-        gate_up_other, down_second
-    ).astype(F32)
-    partial = partial.astype(BF16).reshape(4, LMAX, D)
-    partial = lax.all_to_all(partial, "y", 0, 0, tiled=False)
-    feed_out = jnp.sum(partial.astype(F32), axis=0)
-    live_rows = (jnp.arange(LMAX) < lengths[0]).astype(F32)[:, None]
-    hidden = (live_rows * (middle + feed_out)).astype(BF16)
+    gate_up_other = lax.ppermute(after(gate_up_own, middle), "core", SWAP)
+    normed_mid = after(normed_mid, same)
+    gathered = lax.all_to_all(normed_mid, "y", 0, 0, tiled=False)
+    partial = hidden_rows(same, gathered, gate_up_own, gate_up_other, down_weight, down_other)
+    parts = lax.all_to_all(partial, "y", 0, 0, tiled=False)
+    hidden = result(lengths, middle, parts)
     return (hidden[None], cache[None])
 
 

time: 210 us -> 214 us (1.019); the launches traced: 207 us -> 213 us
  blocking collectives: 27.9 us -> 49.2 us
  Pallas kernels: 8.84 us -> 19.5 us
  matrix products: 9.77 us -> 0 us
  waiting for transfers between devices: 88.4 us -> 79 us
  starting transfers between devices: 46.4 us -> 39.6 us
    ppermute x2 -> x4, waiting for transfers between devices: 0.01 us -> 21 us  [the longest x1 20.3 us: shards(): far = lax.ppermute(rows, along, turn(False))]
    all_to_all x1 -> x0, waiting for transfers between devices: 16.9 us -> none  [shards(): partial = lax.all_to_all(partial, 'y', 0, 0, tiled=False)]
    all_to_all x1 -> x2, blocking collectives: 25.8 us -> 40.7 us  [the longest x1 20.8 us: shards(): gathered = lax.all_to_all(normed_mid, 'y', 0, 0, tiled=False)]
    all_to_all x4 -> x3, waiting for transfers between devices: 67.6 us -> 54.2 us  [spread(): return lax.all_to_all(copies, axes, 0, 0, tiled=False)]
    pallas_call x0 -> x2, Pallas kernels: none -> 10.6 us  [the longest x1 8.17 us: hidden_rows(): pl.pallas_call(hidden_kernel, out_shape=jax.ShapeDtypeStruct((4, LMAX, D)...]
    dot_general x4 -> x0, matrix products: 9.77 us -> none  [the longest x2 6.47 us: units_block(): gate_up = jnp.dot(gathered, gate_up_rows, preferred_element_type=F32)]
    all_gather x1, blocking collectives: 2.12 us -> 8.43 us  [shards(): merged = lax.all_gather(merged, 'core', axis=0, tiled=True)]
    ppermute x2 -> x4, starting transfers between devices: 7.06 us -> 13.1 us  [the longest x1 4.65 us: shards(): down_other = lax.ppermute(after(down_weight, merged), 'x_hi', SWAP)]
  transfers between devices with their start and end apart: 10 -> 10, of which waited for: 5 -> 5; matrix products, arithmetic and copies ran while one was open for 4% -> 1% of each run, Pallas kernels for 4% -> 4%
where the time goes in v3:
time: 214 us; the launch traced here: 213 us
  waiting for transfers between devices  79 us (37%)
  blocking collectives  49.2 us (23%)
  starting transfers between devices  39.6 us (19%)
  Pallas kernels  19.5 us (9%)
  between operations  15 us (7%)
  local copies, waits for them, and re-layouts  8.46 us (4%)
  other arithmetic  2.18 us (1%)
    all_to_all x3, waiting for transfers between devices, spread(): return lax.all_to_all(copies, axes, 0, 0, tiled=False)  54.2 us
    all_to_all x1, blocking collectives, shards(): gathered = lax.all_to_all(normed_mid, 'y', 0, 0, tiled=False)  20.8 us
    ppermute x1, waiting for transfers between devices, shards(): far = lax.ppermute(rows, along, turn(False))  20.3 us
    all_to_all x3, starting transfers between devices, spread(): return lax.all_to_all(copies, axes, 0, 0, tiled=False)  20.1 us
    all_to_all x1, blocking collectives, shards(): parts = lax.all_to_all(partial, 'y', 0, 0, tiled=False)  20 us
    all_gather x1, blocking collectives, shards(): merged = lax.all_gather(merged, 'core', axis=0, tiled=True)  8.43 us
    pallas_call x1, Pallas kernels, hidden_rows(): pl.pallas_call(hidden_kernel, out_shape=jax.ShapeDtypeStruct((4, LMAX, D)...  8.17 us
    pallas_call x1, Pallas kernels, attention(): pl.pallas_call(attention_kernel, out_shape=(jax.ShapeDtypeStruct((D, LMAX...  5.88 us
  transfers between devices with their start and end apart: 10, of which 5 were waited for; matrix products, arithmetic and copies ran while one was open for 1% of the time, Pallas kernels for 4%

profile of v3, /device:TPU:1, one launch (start us, length us, event | category | flops | bytes accessed | tf_op | source)
XLA Modules:
  0.0 212.9 jit_solution(11574758978338251422)
XLA Ops:
  9.8 8.4 %all-gather = bf16[2,20,1296]{2,1,0:T(8,128)(2,1)S(1)} all-gather(bf16[1,20,1296]{2,1,0:T(8,128)(2,1)S(1)} %bitcast.24), channel_id=1, replica_groups=mesh['x_lo'=2,'z'=16,'core'=2,'y'=4,'x_hi'=2] {'core'}, dimensions={0}, use_global_device_ids=true | all-gather | bytes 155520 | tf_op jit(solution)/shard_map/all_gather | solution.py:293
  19.5 9.5 %all-to-all-start = ((bf16[16,40,256]{2,1,0:T(8,128)(2,1)}), bf16[16,40,256]{2,1,0:T(8,128)(2,1)S(1)}, u32[]{:S(2)}, u32[]{:S(2)}) async-start(bf16[16,40,256]{2,1,0:T(8,128)(2,1)} %broadcast_in_dim.47), calls=%async_computation | async-start | bytes 655360 | tf_op jit(solution)/shard_map/all_to_all | solution.py:262
  29.0 4.7 %collective-permute-start.2 = (bf16[448,1280]{1,0:T(8,128)(2,1)S(1)}, bf16[448,1280]{1,0:T(8,128)(2,1)S(1)}, u32[]{:S(2)}, u32[]{:S(2)}) collective-permute-start(bf16[448,1280]{1,0:T(8,128)(2,1)S(1)} %copy-done.5), channel_id=1, source_target_pairs={{0,1},{1,0},{2,3},{3,2},{4,5},{5,4},{6,7},{7,6},{8,9},{9,8},{10,11... | collective-permute-start | bytes 3440648 | tf_op jit(solution)/shard_map/ppermute | solution.py:312
  33.8 3.6 %collective-permute-start.1 = (bf16[40,896]{1,0:T(8,128)(2,1)S(1)}, bf16[40,896]{1,0:T(8,128)(2,1)S(1)}, u32[]{:S(2)}, u32[]{:S(2)}) collective-permute-start(bf16[40,896]{1,0:T(8,128)(2,1)S(1)} %slice.43), channel_id=1, source_target_pairs={{0,256},{1,264},{8,257},{9,265},{256,0},{257,8},{264,1},{265,9},{2... | collective-permute-start | bytes 215048 | tf_op jit(solution)/shard_map/ppermute | solution.py:307
  37.3 2.6 %collective-permute-start = (bf16[40,896]{1,0:T(8,128)(2,1)S(1)}, bf16[40,896]{1,0:T(8,128)(2,1)S(1)}, u32[]{:S(2)}, u32[]{:S(2)}) collective-permute-start(bf16[40,896]{1,0:T(8,128)(2,1)S(1)} %slice.43), channel_id=1, source_target_pairs={{0,0},{1,8},{8,1},{9,9},{256,256},{257,264},{264,257},{265,265},{2... | collective-permute-start | bytes 215048 | tf_op jit(solution)/shard_map/ppermute | solution.py:306
  40.0 20.3 %collective-permute-done.1 = bf16[40,896]{1,0:T(8,128)(2,1)S(1)} collective-permute-done((bf16[40,896]{1,0:T(8,128)(2,1)S(1)}, bf16[40,896]{1,0:T(8,128)(2,1)S(1)}, u32[]{:S(2)}, u32[]{:S(2)}) %collective-permute-start.1) | collective-permute-done | bytes 71712 | tf_op jit(solution)/shard_map/ppermute | solution.py:307
  61.9 1.6 broadcast_in_dim.48
  63.5 5.2 %all-to-all-start.1 = ((bf16[16,120,640]{2,1,0:T(8,128)(2,1)}), bf16[16,120,640]{2,1,0:T(8,128)(2,1)S(1)}, u32[]{:S(2)}, u32[]{:S(2)}) async-start(bf16[16,120,640]{2,1,0:T(8,128)(2,1)} %broadcast_in_dim.48), calls=%async_computation.1 | async-start | bytes 4915200 | tf_op jit(solution)/shard_map/all_to_all | solution.py:262
  69.5 33.6 %all-to-all-done.1.own_ref = bf16[16,120,640]{2,1,0:T(8,128)(2,1)S(1)} async-done(((bf16[16,120,640]{2,1,0:T(8,128)(2,1)}), bf16[16,120,640]{2,1,0:T(8,128)(2,1)S(1)}, u32[]{:S(2)}, u32[]{:S(2)}) %all-to-all-start.1) | async-done | bytes 2457632 | tf_op jit(solution)/shard_map/all_to_all | solution.py:262
  103.1 3.3 %collective-permute-start.3 = (bf16[16,120,640]{2,1,0:T(8,128)(2,1)S(1)}, bf16[16,120,640]{2,1,0:T(8,128)(2,1)}, u32[]{:S(2)}, u32[]{:S(2)}) collective-permute-start(bf16[16,120,640]{2,1,0:T(8,128)(2,1)S(1)} %all-to-all-done.1.own_ref), channel_id=1, source_target_pairs={{0,8},{8,0},{1,9},{9,1},{2,10},{10,2},{3,11},{11,3},{4,12},{12,4},... | collective-permute-start | bytes 7372808 | tf_op jit(solution)/shard_map/ppermute | solution.py:317
  106.5 1.3 broadcast_in_dim.50
  107.8 5.4 %all-to-all-start.2 = ((bf16[16,80,640]{2,1,0:T(8,128)(2,1)}), bf16[16,80,640]{2,1,0:T(8,128)(2,1)}, u32[]{:S(2)}, u32[]{:S(2)}) async-start(bf16[16,80,640]{2,1,0:T(8,128)(2,1)} %broadcast_in_dim.50), calls=%async_computation.2 | async-start | bytes 3276800 | tf_op jit(solution)/shard_map/all_to_all | solution.py:262
  113.9 5.9 %attention.1 = (bf16[1280,128]{1,0:T(8,128)(2,1)S(1)}, bf16[128,640]{1,0:T(8,128)(2,1)}) custom-call(s32[1]{0:T(128)S(6)} %copy.24.length_ref, s32[1]{0:T(128)} %bitcast.core_ref, bf16[128,1280]{1,0:T(8,128)(2,1)S(1)} %bitcast.19, bf16[16,120,640]{2,1,0:T(8,128)(2,1)S(1)} %all-to-all-done.1.own_ref, bf16[16,120,640]{2,1,0:T(8,128)(2,1)} %collective-permute-done.3.other_ref, ...), custom_call_target="tpu_custom_call" | custom-call | flops 800000000 | bytes 6000000 | tf_op jit(solution)/shard_map/attention/pallas_call | solution.py:188
  119.8 20.7 %all-to-all-done.2.own_ref = bf16[16,80,640]{2,1,0:T(8,128)(2,1)} async-done(((bf16[16,80,640]{2,1,0:T(8,128)(2,1)}), bf16[16,80,640]{2,1,0:T(8,128)(2,1)}, u32[]{:S(2)}, u32[]{:S(2)}) %all-to-all-start.2) | async-done | bytes 1638432 | tf_op jit(solution)/shard_map/all_to_all | solution.py:262
  140.5 3.0 %collective-permute-start.4 = (bf16[16,80,640]{2,1,0:T(8,128)(2,1)}, bf16[16,80,640]{2,1,0:T(8,128)(2,1)S(1)}, u32[]{:S(2)}, u32[]{:S(2)}) collective-permute-start(bf16[16,80,640]{2,1,0:T(8,128)(2,1)} %all-to-all-done.2.own_ref), channel_id=1, source_target_pairs={{0,8},{8,0},{1,9},{9,1},{2,10},{10,2},{3,11},{11,3},{4,12},{12,4},... | collective-permute-start | bytes 4915208 | tf_op jit(solution)/shard_map/ppermute | solution.py:320
  143.7 3.1 %collective-permute-done.4.other_ref = bf16[16,80,640]{2,1,0:T(8,128)(2,1)S(1)} collective-permute-done((bf16[16,80,640]{2,1,0:T(8,128)(2,1)}, bf16[16,80,640]{2,1,0:T(8,128)(2,1)S(1)}, u32[]{:S(2)}, u32[]{:S(2)}) %collective-permute-start.4) | collective-permute-done | bytes 1638432 | tf_op jit(solution)/shard_map/ppermute | solution.py:320
  146.8 3.0 %middle.1 = (f32[128,1280]{1,0:T(8,128)S(1)}, bf16[4,128,1280]{2,1,0:T(8,128)(2,1)S(1)}) custom-call(s32[1]{0:T(128)} %bitcast.core_ref, bf16[128,1280]{1,0:T(8,128)(2,1)S(1)} %bitcast.20, bf16[1280,128]{1,0:T(8,128)(2,1)S(1)} %get-tuple-element.14.attended_ref, bf16[16,80,640]{2,1,0:T(8,128)(2,1)} %all-to-all-done.2.own_ref, ...), custom_call_target="tpu_custom_call" | custom-call | flops 420000000 | bytes 4000000 | tf_op jit(solution)/shard_map/middle/pallas_call | solution.py:208
  149.9 2.3 %collective-permute-start.5 = (bf16[1280,896]{1,0:T(8,128)(2,1)}, bf16[1280,896]{1,0:T(8,128)(2,1)}, u32[]{:S(2)}, u32[]{:S(2)}) collective-permute-start(bf16[1280,896]{1,0:T(8,128)(2,1)} %all-gather.3.cloned.1.call-done.first_ref), channel_id=1, source_target_pairs={{0,8},{8,0},{1,9},{9,1},{2,10},{10,2},{3,11},{11,3},{4,12},{12,4},... | collective-permute-start | bytes 6881288 | tf_op jit(solution)/shard_map/ppermute | solution.py:322
  152.2 20.8 %all_to_all.25.tokens_ref = bf16[4,128,1280]{2,1,0:T(8,128)(2,1)S(1)} all-to-all(bf16[4,128,1280]{2,1,0:T(8,128)(2,1)S(1)} %get-tuple-element.19), channel_id=1, replica_groups=mesh['x_lo'=2,'z'=16,'core'=2,'y'=4,'x_hi'=2] {'y'}, dimensions={0} | all-to-all | bytes 2621440 | tf_op jit(solution)/shard_map/all_to_all | solution.py:324
  173.0 1.3 copy-done.6
  174.2 1.3 copy-done.8
  175.5 8.2 %hidden.1 = bf16[4,128,1280]{2,1,0:T(8,128)(2,1)S(1)} custom-call(s32[1]{0:T(128)} %bitcast.10.same_ref, bf16[4,128,1280]{2,1,0:T(8,128)(2,1)S(1)} %all_to_all.25.tokens_ref, bf16[1280,896]{1,0:T(8,128)(2,1)S(1)} %copy-done.4, bf16[1280,896]{1,0:T(8,128)(2,1)} %collective-permute-done.5.second_ref, bf16[448,1280]{1,0:T(8,128)(2,1)S(1)} %copy-done.6, ...), custom_call_target="tpu_custom_call" | custom-call | flops 3500000000 | bytes 9500000 | tf_op jit(solution)/shard_map/hidden/pallas_call | solution.py:226
  183.7 20.0 %all_to_all.26.parts_ref = bf16[4,128,1280]{2,1,0:T(8,128)(2,1)} all-to-all(bf16[4,128,1280]{2,1,0:T(8,128)(2,1)S(1)} %hidden.1), channel_id=1, replica_groups=mesh['x_lo'=2,'z'=16,'core'=2,'y'=4,'x_hi'=2] {'y'}, dimensions={0} | all-to-all | bytes 2621440 | tf_op jit(solution)/shard_map/all_to_all | solution.py:326
  203.6 2.5 %result.1 = bf16[128,1280]{1,0:T(8,128)(2,1)} custom-call(s32[1]{0:T(128)S(6)} %copy.24.length_ref, f32[128,1280]{1,0:T(8,128)} %copy-done.1, bf16[4,128,1280]{2,1,0:T(8,128)(2,1)} %all_to_all.26.parts_ref), custom_call_target="tpu_custom_call" | custom-call | flops 1000000 | bytes 2300000 | tf_op jit(solution)/shard_map/result/pallas_call | solution.py:240
  (53 shorter events, 6.6 us)
Async XLA Ops:
  7.2 21.8 %copy-start.5 = (bf16[448,1280]{1,0:T(8,128)(2,1)S(1)}, bf16[448,1280]{1,0:T(8,128)(2,1)}, u32[]{:S(2)}) copy-start(bf16[448,1280]{1,0:T(8,128)(2,1)} %down_own_ref.1) | copy-start | bytes 3440644
  19.5 42.2 %all-to-all-start = ((bf16[16,40,256]{2,1,0:T(8,128)(2,1)}), bf16[16,40,256]{2,1,0:T(8,128)(2,1)S(1)}, u32[]{:S(2)}, u32[]{:S(2)}) async-start(bf16[16,40,256]{2,1,0:T(8,128)(2,1)} %broadcast_in_dim.47), calls=%async_computation | async-start | bytes 655360 | tf_op jit(solution)/shard_map/all_to_all | solution.py:262
  29.0 32.7 %collective-permute-start.2 = (bf16[448,1280]{1,0:T(8,128)(2,1)S(1)}, bf16[448,1280]{1,0:T(8,128)(2,1)S(1)}, u32[]{:S(2)}, u32[]{:S(2)}) collective-permute-start(bf16[448,1280]{1,0:T(8,128)(2,1)S(1)} %copy-done.5), channel_id=1, source_target_pairs={{0,1},{1,0},{2,3},{3,2},{4,5},{5,4},{6,7},{7,6},{8,9},{9,8},{10,11... | collective-permute-start | bytes 3440648 | tf_op jit(solution)/shard_map/ppermute | solution.py:312
  33.8 26.5 %collective-permute-start.1 = (bf16[40,896]{1,0:T(8,128)(2,1)S(1)}, bf16[40,896]{1,0:T(8,128)(2,1)S(1)}, u32[]{:S(2)}, u32[]{:S(2)}) collective-permute-start(bf16[40,896]{1,0:T(8,128)(2,1)S(1)} %slice.43), channel_id=1, source_target_pairs={{0,256},{1,264},{8,257},{9,265},{256,0},{257,8},{264,1},{265,9},{2... | collective-permute-start | bytes 215048 | tf_op jit(solution)/shard_map/ppermute | solution.py:307
  37.3 23.6 %collective-permute-start = (bf16[40,896]{1,0:T(8,128)(2,1)S(1)}, bf16[40,896]{1,0:T(8,128)(2,1)S(1)}, u32[]{:S(2)}, u32[]{:S(2)}) collective-permute-start(bf16[40,896]{1,0:T(8,128)(2,1)S(1)} %slice.43), channel_id=1, source_target_pairs={{0,0},{1,8},{8,1},{9,9},{256,256},{257,264},{264,257},{265,265},{2... | collective-permute-start | bytes 215048 | tf_op jit(solution)/shard_map/ppermute | solution.py:306
  61.7 1.8 copy-start.7
  63.5 39.5 %all-to-all-start.1 = ((bf16[16,120,640]{2,1,0:T(8,128)(2,1)}), bf16[16,120,640]{2,1,0:T(8,128)(2,1)S(1)}, u32[]{:S(2)}, u32[]{:S(2)}) async-start(bf16[16,120,640]{2,1,0:T(8,128)(2,1)} %broadcast_in_dim.48), calls=%async_computation.1 | async-start | bytes 4915200 | tf_op jit(solution)/shard_map/all_to_all | solution.py:262
  68.7 81.1 %all-gather.3.cloned.1.call-start = ((), (), s32[]{:S(2)}) async-start(), calls=%async_computation.5 | async-start | bytes 2437120 | tf_op jit(solution)/shard_map/all_gather | solution.py:311
  103.1 10.8 %collective-permute-start.3 = (bf16[16,120,640]{2,1,0:T(8,128)(2,1)S(1)}, bf16[16,120,640]{2,1,0:T(8,128)(2,1)}, u32[]{:S(2)}, u32[]{:S(2)}) collective-permute-start(bf16[16,120,640]{2,1,0:T(8,128)(2,1)S(1)} %all-to-all-done.1.own_ref), channel_id=1, source_target_pairs={{0,8},{8,0},{1,9},{9,1},{2,10},{10,2},{3,11},{11,3},{4,12},{12,4},... | collective-permute-start | bytes 7372808 | tf_op jit(solution)/shard_map/ppermute | solution.py:317
  107.8 6.0 %copy-start.9 = (f32[1280]{0:T(1024)S(1)}, f32[1280]{0:T(1024)}, u32[]{:S(2)}) copy-start(f32[1280]{0:T(1024)} %param.16) | copy-start | bytes 15364
  107.8 6.1 %copy-start = (bf16[1,128,1280]{2,1,0:T(8,128)(2,1)S(1)}, bf16[1,128,1280]{2,1,0:T(8,128)(2,1)}, u32[]{:S(2)}) copy-start(bf16[1,128,1280]{2,1,0:T(8,128)(2,1)} %param.10) | copy-start | bytes 983044
  107.8 6.1 %copy-start.2 = (f32[32,128]{1,0:T(8,128)S(1)}, f32[32,128]{1,0:T(8,128)}, u32[]{:S(2)}) copy-start(f32[32,128]{1,0:T(8,128)} %constant.29.clone.cos_ref) | copy-start | bytes 49156
  107.8 6.1 %copy-start.3 = (f32[32,128]{1,0:T(8,128)S(1)}, f32[32,128]{1,0:T(8,128)}, u32[]{:S(2)}) copy-start(f32[32,128]{1,0:T(8,128)} %constant.30.clone.sin_ref) | copy-start | bytes 49156
  107.8 32.6 %all-to-all-start.2 = ((bf16[16,80,640]{2,1,0:T(8,128)(2,1)}), bf16[16,80,640]{2,1,0:T(8,128)(2,1)}, u32[]{:S(2)}, u32[]{:S(2)}) async-start(bf16[16,80,640]{2,1,0:T(8,128)(2,1)} %broadcast_in_dim.50), calls=%async_computation.2 | async-start | bytes 3276800 | tf_op jit(solution)/shard_map/all_to_all | solution.py:262
  113.9 29.6 %copy-start.10 = (f32[1280]{0:T(1024)S(1)}, f32[1280]{0:T(1024)}, u32[]{:S(2)}) copy-start(f32[1280]{0:T(1024)} %param.17) | copy-start | bytes 15364
  140.5 6.3 %collective-permute-start.4 = (bf16[16,80,640]{2,1,0:T(8,128)(2,1)}, bf16[16,80,640]{2,1,0:T(8,128)(2,1)S(1)}, u32[]{:S(2)}, u32[]{:S(2)}) collective-permute-start(bf16[16,80,640]{2,1,0:T(8,128)(2,1)} %all-to-all-done.2.own_ref), channel_id=1, source_target_pairs={{0,8},{8,0},{1,9},{9,1},{2,10},{10,2},{3,11},{11,3},{4,12},{12,4},... | collective-permute-start | bytes 4915208 | tf_op jit(solution)/shard_map/ppermute | solution.py:320
  149.8 33.8 %copy-start.1 = (f32[128,1280]{1,0:T(8,128)}, f32[128,1280]{1,0:T(8,128)S(1)}, u32[]{:S(2)}) copy-start(f32[128,1280]{1,0:T(8,128)S(1)} %get-tuple-element.17.middle_ref) | copy-start | bytes 1966084
  149.9 23.1 %collective-permute-start.5 = (bf16[1280,896]{1,0:T(8,128)(2,1)}, bf16[1280,896]{1,0:T(8,128)(2,1)}, u32[]{:S(2)}, u32[]{:S(2)}) collective-permute-start(bf16[1280,896]{1,0:T(8,128)(2,1)} %all-gather.3.cloned.1.call-done.first_ref), channel_id=1, source_target_pairs={{0,8},{8,0},{1,9},{9,1},{2,10},{10,2},{3,11},{11,3},{4,12},{12,4},... | collective-permute-start | bytes 6881288 | tf_op jit(solution)/shard_map/ppermute | solution.py:322
  152.2 20.8 %copy-start.4 = (bf16[1280,896]{1,0:T(8,128)(2,1)S(1)}, bf16[1280,896]{1,0:T(8,128)(2,1)}, u32[]{:S(2)}) copy-start(bf16[1280,896]{1,0:T(8,128)(2,1)} %all-gather.3.cloned.1.call-done.first_ref) | copy-start | bytes 6881284
  173.0 1.3 copy-start.6
  174.2 1.3 copy-start.8
Sparse Core Ops, SparseCore 0:
  71.7 68.6 all-gather.2

commit v4 on v3

--- a/solution.py
+++ b/solution.py
@@ -137,16 +137,19 @@
             moved[j * 80 + lo * 40 : j * 80 + lo * 40 + 40, :] = block
     for j in range(10):
         cols = slice(j * LMAX, (j + 1) * LMAX)
-        block = moved[cols, :].T.astype(BF16)
-        for copy in range(4):
-            normed_ref[copy, :, cols] = block
+        normed_ref[:, cols] = moved[cols, :].T.astype(BF16)
 
 
 def hidden_kernel(
-    same_ref, tokens_ref, first_ref, second_ref, down_own_ref, down_other_ref, out_ref
+    own_ref, next_ref, across_ref, gate_up_ref, first_ref, second_ref, keep_ref, send_ref, tokens
 ):
-    def block(tokens, gate_up_ref, down_ref):
-        gate_up = dot_nn(tokens, gate_up_ref[...])
+    tokens[:LMAX, :] = own_ref[...]
+    tokens[LMAX : 2 * LMAX, :] = next_ref[...]
+    tokens[2 * LMAX : 3 * LMAX, :] = across_ref[0]
+    tokens[3 * LMAX :, :] = across_ref[1]
+
+    def block(start, down_ref):
+        gate_up = dot_nn(tokens[...], gate_up_ref[:, start : start + 2 * UNITS])
         gate, up = gate_up[:, :WIDE], gate_up[:, WIDE : 2 * WIDE]
         units = (gate / (1.0 + jnp.exp(-gate)) * up).astype(BF16)
         gate = gate_up[:, 2 * WIDE :]
@@ -155,28 +158,11 @@
         total = dot_nn(units, down_ref[:WIDE, :]) + dot_nn(rest, down_ref[WIDE:, :])
         return total.astype(BF16).astype(F32)
 
-    def run(down_first_ref, down_second_ref):
-        for prompt in range(4):
-            tokens = tokens_ref[prompt]
-            total = block(tokens, first_ref, down_first_ref)
-            total = total + block(tokens, second_ref, down_second_ref)
-            out_ref[prompt] = total.astype(BF16)
-
-    @pl.when(same_ref[0] == 1)
-    def _():
-        run(down_own_ref, down_other_ref)
-
-    @pl.when(same_ref[0] == 0)
-    def _():
-        run(down_other_ref, down_own_ref)
-
-
-def result_kernel(length_ref, middle_ref, parts_ref, out_ref):
-    feed_out = parts_ref[0].astype(F32)
-    for j in range(1, 4):
-        feed_out = feed_out + parts_ref[j].astype(F32)
-    live = lax.broadcasted_iota(jnp.int32, (LMAX, D), 0) < length_ref[0]
-    out_ref[...] = jnp.where(live, middle_ref[...] + feed_out, 0.0).astype(BF16)
+    total = block(0, first_ref) + block(2 * UNITS, second_ref)
+    keep_ref[0] = total[:LMAX]
+    keep_ref[1] = total[LMAX : 2 * LMAX]
+    send_ref[0] = total[2 * LMAX : 3 * LMAX].astype(BF16)
+    send_ref[1] = total[3 * LMAX :].astype(BF16)
 
 
 VMEM = pl.BlockSpec(memory_space=pltpu.VMEM)
@@ -209,7 +195,7 @@
         middle_kernel,
         out_shape=(
             jax.ShapeDtypeStruct((LMAX, D), F32),
-            jax.ShapeDtypeStruct((4, LMAX, D), BF16),
+            jax.ShapeDtypeStruct((LMAX, D), BF16),
         ),
         in_specs=[SMEM] + [VMEM] * 5,
         out_specs=(VMEM, VMEM),
@@ -222,29 +208,22 @@
     )(core, tokens, attended, own, other, gain[:, None])
 
 
-def hidden_rows(same, tokens, first, second, down_own, down_other):
+def hidden_rows(own, beside, across, gate_up, down_first, down_second):
     return pl.pallas_call(
         hidden_kernel,
-        out_shape=jax.ShapeDtypeStruct((4, LMAX, D), BF16),
-        in_specs=[SMEM] + [VMEM] * 5,
-        out_specs=VMEM,
-        compiler_params=pltpu.CompilerParams(vmem_limit_bytes=32 << 20),
+        out_shape=(
+            jax.ShapeDtypeStruct((2, LMAX, D), F32),
+            jax.ShapeDtypeStruct((2, LMAX, D), BF16),
+        ),
+        in_specs=[VMEM] * 6,
+        out_specs=(VMEM, VMEM),
+        scratch_shapes=[pltpu.VMEM((4 * LMAX, D), BF16)],
+        compiler_params=pltpu.CompilerParams(vmem_limit_bytes=36 << 20),
         cost_estimate=pl.CostEstimate(
             flops=3500000000, bytes_accessed=9500000, transcendentals=500000
         ),
         name="hidden",
-    )(same, tokens, first, second, down_own, down_other)
-
-
-def result(length, middle, parts):
-    return pl.pallas_call(
-        result_kernel,
-        out_shape=jax.ShapeDtypeStruct((LMAX, D), BF16),
-        in_specs=[SMEM] + [VMEM] * 2,
-        out_specs=VMEM,
-        cost_estimate=pl.CostEstimate(flops=1000000, bytes_accessed=2300000, transcendentals=0),
-        name="result",
-    )(length, middle, parts)
+    )(own, beside, across, gate_up, down_first, down_second)
 
 
 def turn(same_x):
@@ -267,16 +246,15 @@
 
 
 SWAP = [(0, 1), (1, 0)]
+BESIDE = [(y, y ^ 1) for y in range(4)]
 
 
 def shards(
     prompts, lengths, qkv_master, out_master, gate_up_master, down_weight, attn_gain, mlp_gain
 ):
     core = lax.axis_index("core").astype(jnp.int32)
-    x_hi = lax.axis_index("x_hi").astype(jnp.int32)
     x_lo = lax.axis_index("x_lo")
     core_at = core[None]
-    same = (core == x_hi).astype(jnp.int32)[None]
     tokens = prompts[0]
     gate_up = gate_up_master.astype(BF16)
     merged = jnp.concatenate(
@@ -308,9 +286,25 @@
     near = jnp.where(
         x_lo == 0, jnp.concatenate([near, far], axis=0), jnp.concatenate([far, near], axis=0)
     )
-    gate_up_own = lax.all_gather(near, "z", axis=0, tiled=True)
-    down_other = lax.ppermute(after(down_weight, merged), "x_hi", SWAP)
-    part_qkv = after(part[:, :QW].T, near, down_other)
+    opposite = lax.ppermute(near, "y", [(y, y ^ 2) for y in range(4)])
+    gate_up_rows = lax.all_gather(
+        jnp.concatenate([near, opposite], axis=1), "z", axis=0, tiled=True
+    )
+    down = after(down_weight, merged)
+    down_first = lax.ppermute(
+        down, ("core", "x_hi"), [(2 * a + b, 2 * b + a) for a in range(2) for b in range(2)]
+    )
+    down_second = lax.ppermute(
+        down,
+        ("core", "y", "x_hi"),
+        [
+            (8 * a + 2 * y + b, 8 * b + 2 * (y ^ 2) + a)
+            for a in range(2)
+            for y in range(4)
+            for b in range(2)
+        ],
+    )
+    part_qkv = after(part[:, :QW].T, near, down_first, down_second)
     qkv_own = spread(part_qkv, ("x_lo", "y", "x_hi"), 16)
     part_out = after(part[:, 128 : 128 + OW].T, qkv_own)
     out_own = spread(part_out, ("x_lo", "y", "x_hi"), 16)
@@ -319,12 +313,13 @@
     out_own = after(out_own, attended)
     out_other = lax.ppermute(out_own, "core", SWAP)
     middle, normed_mid = middle_rows(core_at, tokens, attended, out_own, out_other, mlp_gain)
-    gate_up_other = lax.ppermute(after(gate_up_own, middle), "core", SWAP)
-    normed_mid = after(normed_mid, same)
-    gathered = lax.all_to_all(normed_mid, "y", 0, 0, tiled=False)
-    partial = hidden_rows(same, gathered, gate_up_own, gate_up_other, down_weight, down_other)
-    parts = lax.all_to_all(partial, "y", 0, 0, tiled=False)
-    hidden = result(lengths, middle, parts)
+    beside = lax.ppermute(normed_mid, "y", BESIDE)
+    across = lax.ppermute(jnp.stack([normed_mid, beside]), "core", SWAP)
+    keep, send = hidden_rows(normed_mid, beside, across, gate_up_rows, down_first, down_second)
+    sums = keep + lax.ppermute(send, "core", SWAP).astype(F32)
+    feed_out = sums[0] + lax.ppermute(sums[1].astype(BF16), "y", BESIDE).astype(F32)
+    live_rows = (jnp.arange(LMAX) < lengths[0]).astype(F32)[:, None]
+    hidden = (live_rows * (middle + feed_out)).astype(BF16)
     return (hidden[None], cache[None])
 
 

time: 214 us -> 210 us (0.981)
  starting transfers between devices: 39.6 us -> 48.9 us
  waiting for transfers between devices: 79 us -> 72.8 us
  blocking collectives: 49.2 us -> 43.9 us
  Pallas kernels: 19.5 us -> 15.1 us
    ppermute x2 -> x7, waiting for transfers between devices: 0.01 us -> 43.2 us  [the longest x1 11.2 us: shards(): lax.ppermute(down, ('core', 'x_hi'), [(2 * a + b, 2 * b + a) for a in ran...]
    all_to_all x3 -> x2, waiting for transfers between devices: 54.2 us -> 21.3 us  [spread(): return lax.all_to_all(copies, axes, 0, 0, tiled=False)]
    ppermute x1, waiting for transfers between devices: 20.3 us -> 0.09 us  [shards(): far = lax.ppermute(rows, along, turn(False))]
    ppermute x2 -> x7, starting transfers between devices: 6.93 us -> 21.2 us  [the longest x1 4.82 us: shards(): opposite = lax.ppermute(near, 'y', [(y, y ^ 2) for y in range(4)])]
    all_to_all x3 -> x2, starting transfers between devices: 20.1 us -> 14.1 us  [spread(): return lax.all_to_all(copies, axes, 0, 0, tiled=False)]
    all_to_all x2 -> x1, blocking collectives: 40.7 us -> 35.4 us  [spread(): return lax.all_to_all(copies, axes, 0, 0, tiled=False)]
    ppermute x1, waiting for transfers between devices: 0.68 us -> 5.15 us  [shards(): near = lax.ppermute(rows, along, turn(True))]
    pallas_call x2 -> x1, Pallas kernels: 10.6 us -> 6.24 us  [hidden_rows(): pl.pallas_call(hidden_kernel, out_shape=(jax.ShapeDtypeStruct((2, LMAX, D...]
  transfers between devices with their start and end apart: 10 -> 14, of which waited for: 5 -> 10; matrix products, arithmetic and copies ran while one was open for 1% -> 1% of each run, Pallas kernels for 4% -> 4%
where the time goes in v4:
time: 210 us; the launch traced here: 209 us
  waiting for transfers between devices  72.8 us (35%)
  starting transfers between devices  48.9 us (23%)
  blocking collectives  43.9 us (21%)
  Pallas kernels  15.1 us (7%)
  between operations  15 us (7%)
  local copies, waits for them, and re-layouts  10 us (5%)
  other arithmetic  3.29 us (2%)
    all_to_all x1, blocking collectives, spread(): return lax.all_to_all(copies, axes, 0, 0, tiled=False)  35.4 us
    all_to_all x2, waiting for transfers between devices, spread(): return lax.all_to_all(copies, axes, 0, 0, tiled=False)  21.3 us
    all_to_all x2, starting transfers between devices, spread(): return lax.all_to_all(copies, axes, 0, 0, tiled=False)  14.1 us
    ppermute x1, waiting for transfers between devices, shards(): lax.ppermute(down, ('core', 'x_hi'), [(2 * a + b, 2 * b + a) for a in ran...  11.2 us
    ppermute x1, waiting for transfers between devices, shards(): lax.ppermute(down, ('core', 'y', 'x_hi'), [(8 * a + 2 * y + b, 8 * b + 2...  11 us
    ppermute x1, waiting for transfers between devices, shards(): beside = lax.ppermute(normed_mid, 'y', BESIDE)  8.89 us
    ppermute x1, waiting for transfers between devices, shards(): lax.ppermute(sums[1].astype(BF16), 'y', BESIDE).astype(F32)  8.88 us
    all_gather x1, blocking collectives, shards(): merged = lax.all_gather(merged, 'core', axis=0, tiled=True)  8.43 us
  transfers between devices with their start and end apart: 14, of which 10 were waited for; matrix products, arithmetic and copies ran while one was open for 1% of the time, Pallas kernels for 4%

profile of v4, /device:TPU:1, one launch (start us, length us, event | category | flops | bytes accessed | tf_op | source)
XLA Modules:
  0.0 209.0 jit_solution(10430853951973440981)
XLA Ops:
  9.7 8.4 %all-gather = bf16[2,20,1296]{2,1,0:T(8,128)(2,1)S(1)} all-gather(bf16[1,20,1296]{2,1,0:T(8,128)(2,1)S(1)} %bitcast.43), channel_id=1, replica_groups=mesh['x_lo'=2,'z'=16,'core'=2,'y'=4,'x_hi'=2] {'core'}, dimensions={0}, use_global_device_ids=true | all-gather | bytes 155520 | tf_op jit(solution)/shard_map/all_gather | solution.py:271
  19.3 9.5 %all-to-all-start = ((bf16[16,40,256]{2,1,0:T(8,128)(2,1)}), bf16[16,40,256]{2,1,0:T(8,128)(2,1)S(1)}, u32[]{:S(2)}, u32[]{:S(2)}) async-start(bf16[16,40,256]{2,1,0:T(8,128)(2,1)} %broadcast_in_dim.43), calls=%async_computation | async-start | bytes 655360 | tf_op jit(solution)/shard_map/all_to_all | solution.py:241
  29.0 4.9 %collective-permute-start.1 = (bf16[40,896]{1,0:T(8,128)(2,1)S(1)}, bf16[40,896]{1,0:T(8,128)(2,1)S(1)}, u32[]{:S(2)}, u32[]{:S(2)}) collective-permute-start(bf16[40,896]{1,0:T(8,128)(2,1)S(1)} %slice.52), channel_id=1, source_target_pairs={{0,256},{1,264},{8,257},{9,265},{256,0},{257,8},{264,1},{265,9},{2... | collective-permute-start | bytes 215048 | tf_op jit(solution)/shard_map/ppermute | solution.py:285
  34.0 2.2 %collective-permute-start = (bf16[40,896]{1,0:T(8,128)(2,1)S(1)}, bf16[40,896]{1,0:T(8,128)(2,1)S(1)}, u32[]{:S(2)}, u32[]{:S(2)}) collective-permute-start(bf16[40,896]{1,0:T(8,128)(2,1)S(1)} %slice.52), channel_id=1, source_target_pairs={{0,0},{1,8},{8,1},{9,9},{256,256},{257,264},{264,257},{265,265},{2... | collective-permute-start | bytes 215048 | tf_op jit(solution)/shard_map/ppermute | solution.py:284
  36.2 5.2 %collective-permute-done = bf16[40,896]{1,0:T(8,128)(2,1)S(1)} collective-permute-done((bf16[40,896]{1,0:T(8,128)(2,1)S(1)}, bf16[40,896]{1,0:T(8,128)(2,1)S(1)}, u32[]{:S(2)}, u32[]{:S(2)}) %collective-permute-start) | collective-permute-done | bytes 71712 | tf_op jit(solution)/shard_map/ppermute | solution.py:284
  41.4 4.8 %collective-permute-start.8 = (bf16[80,896]{1,0:T(8,128)(2,1)S(1)}, bf16[80,896]{1,0:T(8,128)(2,1)S(1)}, u32[]{:S(2)}, u32[]{:S(2)}) collective-permute-start(bf16[80,896]{1,0:T(8,128)(2,1)S(1)} %maximum_select_fusion), channel_id=1, source_target_pairs={{0,4},{2,6},{4,0},{6,2},{1,5},{3,7},{5,1},{7,3},{8,12},{10,14},{12... | collective-permute-start | bytes 430088 | tf_op jit(solution)/shard_map/ppermute | solution.py:289
  46.3 2.2 %collective-permute-start.2 = (bf16[448,1280]{1,0:T(8,128)(2,1)}, bf16[448,1280]{1,0:T(8,128)(2,1)S(1)}, u32[]{:S(2)}, u32[]{:S(2)}) collective-permute-start(bf16[448,1280]{1,0:T(8,128)(2,1)} %param.15), channel_id=1, source_target_pairs={{0,0},{1,8},{8,1},{9,9},{2,2},{3,10},{10,3},{11,11},{4,4},{5,12},{... | collective-permute-start | bytes 3440648 | tf_op jit(solution)/shard_map/ppermute | solution.py:294
  48.4 4.7 %collective-permute-start.3 = (bf16[448,1280]{1,0:T(8,128)(2,1)}, bf16[448,1280]{1,0:T(8,128)(2,1)S(1)}, u32[]{:S(2)}, u32[]{:S(2)}) collective-permute-start(bf16[448,1280]{1,0:T(8,128)(2,1)} %param.15), channel_id=1, source_target_pairs={{0,4},{1,12},{2,6},{3,14},{4,0},{5,8},{6,2},{7,10},{8,5},{9,13},{1... | collective-permute-start | bytes 3440648 | tf_op jit(solution)/shard_map/ppermute | solution.py:297
  53.9 11.2 %collective-permute-done.2.first_ref = bf16[448,1280]{1,0:T(8,128)(2,1)S(1)} collective-permute-done((bf16[448,1280]{1,0:T(8,128)(2,1)}, bf16[448,1280]{1,0:T(8,128)(2,1)S(1)}, u32[]{:S(2)}, u32[]{:S(2)}) %collective-permute-start.2) | collective-permute-done | bytes 1146912 | tf_op jit(solution)/shard_map/ppermute | solution.py:294
  66.2 11.0 %collective-permute-done.3.second_ref = bf16[448,1280]{1,0:T(8,128)(2,1)S(1)} collective-permute-done((bf16[448,1280]{1,0:T(8,128)(2,1)}, bf16[448,1280]{1,0:T(8,128)(2,1)S(1)}, u32[]{:S(2)}, u32[]{:S(2)}) %collective-permute-start.3) | collective-permute-done | bytes 1146912 | tf_op jit(solution)/shard_map/ppermute | solution.py:297
  78.6 35.4 %all_to_all.15.own_ref = bf16[16,120,640]{2,1,0:T(8,128)(2,1)S(1)} all-to-all(bf16[16,120,640]{2,1,0:T(8,128)(2,1)S(1)} %broadcast_in_dim.44), channel_id=1, replica_groups=mesh['x_lo'=2,'z'=16,'core'=2,'y'=4,'x_hi'=2] {'x_lo','y','x_hi'}, dimensions={0} | all-to-all | bytes 4915200 | tf_op jit(solution)/shard_map/all_to_all | solution.py:241
  114.0 3.7 %collective-permute-start.4 = (bf16[16,120,640]{2,1,0:T(8,128)(2,1)S(1)}, bf16[16,120,640]{2,1,0:T(8,128)(2,1)}, u32[]{:S(2)}, u32[]{:S(2)}) collective-permute-start(bf16[16,120,640]{2,1,0:T(8,128)(2,1)S(1)} %all_to_all.15.own_ref), channel_id=1, source_target_pairs={{0,8},{8,0},{1,9},{9,1},{2,10},{10,2},{3,11},{11,3},{4,12},{12,4},... | collective-permute-start | bytes 7372808 | tf_op jit(solution)/shard_map/ppermute | solution.py:311
  119.2 4.6 %all-to-all-start.2 = ((bf16[16,80,640]{2,1,0:T(8,128)(2,1)}), bf16[16,80,640]{2,1,0:T(8,128)(2,1)}, u32[]{:S(2)}, u32[]{:S(2)}) async-start(bf16[16,80,640]{2,1,0:T(8,128)(2,1)} %broadcast_in_dim.46), calls=%async_computation.2 | async-start | bytes 3276800 | tf_op jit(solution)/shard_map/all_to_all | solution.py:241
  124.5 5.9 %attention.1 = (bf16[1280,128]{1,0:T(8,128)(2,1)S(1)}, bf16[128,640]{1,0:T(8,128)(2,1)}) custom-call(s32[1]{0:T(128)} %copy.24.length_ref, s32[1]{0:T(128)} %bitcast.1.core_ref, bf16[128,1280]{1,0:T(8,128)(2,1)S(1)} %bitcast.37, bf16[16,120,640]{2,1,0:T(8,128)(2,1)S(1)} %all_to_all.15.own_ref, bf16[16,120,640]{2,1,0:T(8,128)(2,1)} %collective-permute-done.4.other_ref, ...), custom_call_target="tpu_custom_call" | custom-call | flops 800000000 | bytes 6000000 | tf_op jit(solution)/shard_map/attention/pallas_call | solution.py:174
  130.4 21.3 %all-to-all-done.2.own_ref = bf16[16,80,640]{2,1,0:T(8,128)(2,1)} async-done(((bf16[16,80,640]{2,1,0:T(8,128)(2,1)}), bf16[16,80,640]{2,1,0:T(8,128)(2,1)}, u32[]{:S(2)}, u32[]{:S(2)}) %all-to-all-start.2) | async-done | bytes 1638432 | tf_op jit(solution)/shard_map/all_to_all | solution.py:241
  151.6 2.7 %collective-permute-start.5 = (bf16[16,80,640]{2,1,0:T(8,128)(2,1)}, bf16[16,80,640]{2,1,0:T(8,128)(2,1)S(1)}, u32[]{:S(2)}, u32[]{:S(2)}) collective-permute-start(bf16[16,80,640]{2,1,0:T(8,128)(2,1)} %all-to-all-done.2.own_ref), channel_id=1, source_target_pairs={{0,8},{8,0},{1,9},{9,1},{2,10},{10,2},{3,11},{11,3},{4,12},{12,4},... | collective-permute-start | bytes 4915208 | tf_op jit(solution)/shard_map/ppermute | solution.py:314
  154.6 3.1 %collective-permute-done.5.other_ref = bf16[16,80,640]{2,1,0:T(8,128)(2,1)S(1)} collective-permute-done((bf16[16,80,640]{2,1,0:T(8,128)(2,1)}, bf16[16,80,640]{2,1,0:T(8,128)(2,1)S(1)}, u32[]{:S(2)}, u32[]{:S(2)}) %collective-permute-start.5) | collective-permute-done | bytes 1638432 | tf_op jit(solution)/shard_map/ppermute | solution.py:314
  157.6 3.0 %middle.1 = (f32[128,1280]{1,0:T(8,128)S(1)}, bf16[128,1280]{1,0:T(8,128)(2,1)S(1)}) custom-call(s32[1]{0:T(128)} %bitcast.1.core_ref, bf16[128,1280]{1,0:T(8,128)(2,1)S(1)} %bitcast.38, bf16[1280,128]{1,0:T(8,128)(2,1)S(1)} %get-tuple-element.14.attended_ref, bf16[16,80,640]{2,1,0:T(8,128)(2,1)} %all-to-all-done.2.own_ref, ...), custom_call_target="tpu_custom_call" | custom-call | flops 420000000 | bytes 4000000 | tf_op jit(solution)/shard_map/middle/pallas_call | solution.py:194
  162.7 8.9 %collective-permute-done.6.next_ref = bf16[128,1280]{1,0:T(8,128)(2,1)S(1)} collective-permute-done((bf16[128,1280]{1,0:T(8,128)(2,1)S(1)}, bf16[128,1280]{1,0:T(8,128)(2,1)S(1)}, u32[]{:S(2)}, u32[]{:S(2)}) %collective-permute-start.6) | collective-permute-done | bytes 327712 | tf_op jit(solution)/shard_map/ppermute | solution.py:316
  171.7 3.3 %collective-permute-start.7 = (bf16[2,128,1280]{2,1,0:T(8,128)(2,1)S(1)}, bf16[2,128,1280]{2,1,0:T(8,128)(2,1)S(1)}, u32[]{:S(2)}, u32[]{:S(2)}) collective-permute-start(bf16[2,128,1280]{2,1,0:T(8,128)(2,1)S(1)} %pad_maximum_fusion), channel_id=1, source_target_pairs={{0,8},{8,0},{1,9},{9,1},{2,10},{10,2},{3,11},{11,3},{4,12},{12,4},... | collective-permute-start | bytes 1966088 | tf_op jit(solution)/shard_map/ppermute | solution.py:317
  176.5 2.3 %copy-done.3 = bf16[1280,1792]{1,0:T(8,128)(2,1)S(1)} copy-done((bf16[1280,1792]{1,0:T(8,128)(2,1)S(1)}, bf16[1280,1792]{1,0:T(8,128)(2,1)}, u32[]{:S(2)}) %copy-start.3) | copy-done | bytes 4587544
  180.1 6.2 %hidden.1 = (f32[2,128,1280]{2,1,0:T(8,128)S(1)}, bf16[2,128,1280]{2,1,0:T(8,128)(2,1)S(1)}) custom-call(bf16[128,1280]{1,0:T(8,128)(2,1)S(1)} %get-tuple-element.18.own_ref, bf16[128,1280]{1,0:T(8,128)(2,1)S(1)} %collective-permute-done.6.next_ref, bf16[2,128,1280]{2,1,0:T(8,128)(2,1)S(1)} %collective-permute-done.7.across_ref, ...), custom_call_target="tpu_custom_call" | custom-call | flops 3500000000 | bytes 9500000 | tf_op jit(solution)/shard_map/hidden/pallas_call | solution.py:212
  186.3 2.3 %collective-permute-start.9 = (bf16[2,128,1280]{2,1,0:T(8,128)(2,1)S(1)}, bf16[2,128,1280]{2,1,0:T(8,128)(2,1)S(1)}, u32[]{:S(2)}, u32[]{:S(2)}) collective-permute-start(bf16[2,128,1280]{2,1,0:T(8,128)(2,1)S(1)} %get-tuple-element.20), channel_id=1, source_target_pairs={{0,8},{8,0},{1,9},{9,1},{2,10},{10,2},{3,11},{11,3},{4,12},{12,4},... | collective-permute-start | bytes 1966088 | tf_op jit(solution)/shard_map/ppermute | solution.py:319
  192.4 8.9 %collective-permute-done.10 = bf16[128,1280]{1,0:T(8,128)(2,1)S(1)} collective-permute-done((bf16[128,1280]{1,0:T(8,128)(2,1)S(1)}, bf16[128,1280]{1,0:T(8,128)(2,1)S(1)}, u32[]{:S(2)}, u32[]{:S(2)}) %collective-permute-start.10) | collective-permute-done | bytes 327712 | tf_op jit(solution)/shard_map/ppermute | solution.py:320
  (63 shorter events, 18.3 us)
Async XLA Ops:
  19.3 34.6 %all-to-all-start = ((bf16[16,40,256]{2,1,0:T(8,128)(2,1)}), bf16[16,40,256]{2,1,0:T(8,128)(2,1)S(1)}, u32[]{:S(2)}, u32[]{:S(2)}) async-start(bf16[16,40,256]{2,1,0:T(8,128)(2,1)} %broadcast_in_dim.43), calls=%async_computation | async-start | bytes 655360 | tf_op jit(solution)/shard_map/all_to_all | solution.py:241
  28.9 147.6 %all-gather.3.cloned.1.call-start = ((), (), s32[]{:S(2)}) async-start(), calls=%async_computation.3 | async-start | bytes 4874240 | tf_op jit(solution)/shard_map/all_gather | solution.py:290
  29.0 7.2 %collective-permute-start.1 = (bf16[40,896]{1,0:T(8,128)(2,1)S(1)}, bf16[40,896]{1,0:T(8,128)(2,1)S(1)}, u32[]{:S(2)}, u32[]{:S(2)}) collective-permute-start(bf16[40,896]{1,0:T(8,128)(2,1)S(1)} %slice.52), channel_id=1, source_target_pairs={{0,256},{1,264},{8,257},{9,265},{256,0},{257,8},{264,1},{265,9},{2... | collective-permute-start | bytes 215048 | tf_op jit(solution)/shard_map/ppermute | solution.py:285
  34.0 7.4 %collective-permute-start = (bf16[40,896]{1,0:T(8,128)(2,1)S(1)}, bf16[40,896]{1,0:T(8,128)(2,1)S(1)}, u32[]{:S(2)}, u32[]{:S(2)}) collective-permute-start(bf16[40,896]{1,0:T(8,128)(2,1)S(1)} %slice.52), channel_id=1, source_target_pairs={{0,0},{1,8},{8,1},{9,9},{256,256},{257,264},{264,257},{265,265},{2... | collective-permute-start | bytes 215048 | tf_op jit(solution)/shard_map/ppermute | solution.py:284
  41.4 11.7 %collective-permute-start.8 = (bf16[80,896]{1,0:T(8,128)(2,1)S(1)}, bf16[80,896]{1,0:T(8,128)(2,1)S(1)}, u32[]{:S(2)}, u32[]{:S(2)}) collective-permute-start(bf16[80,896]{1,0:T(8,128)(2,1)S(1)} %maximum_select_fusion), channel_id=1, source_target_pairs={{0,4},{2,6},{4,0},{6,2},{1,5},{3,7},{5,1},{7,3},{8,12},{10,14},{12... | collective-permute-start | bytes 430088 | tf_op jit(solution)/shard_map/ppermute | solution.py:289
  46.3 18.9 %collective-permute-start.2 = (bf16[448,1280]{1,0:T(8,128)(2,1)}, bf16[448,1280]{1,0:T(8,128)(2,1)S(1)}, u32[]{:S(2)}, u32[]{:S(2)}) collective-permute-start(bf16[448,1280]{1,0:T(8,128)(2,1)} %param.15), channel_id=1, source_target_pairs={{0,0},{1,8},{8,1},{9,9},{2,2},{3,10},{10,3},{11,11},{4,4},{5,12},{... | collective-permute-start | bytes 3440648 | tf_op jit(solution)/shard_map/ppermute | solution.py:294
  48.4 28.8 %collective-permute-start.3 = (bf16[448,1280]{1,0:T(8,128)(2,1)}, bf16[448,1280]{1,0:T(8,128)(2,1)S(1)}, u32[]{:S(2)}, u32[]{:S(2)}) collective-permute-start(bf16[448,1280]{1,0:T(8,128)(2,1)} %param.15), channel_id=1, source_target_pairs={{0,4},{1,12},{2,6},{3,14},{4,0},{5,8},{6,2},{7,10},{8,5},{9,13},{1... | collective-permute-start | bytes 3440648 | tf_op jit(solution)/shard_map/ppermute | solution.py:297
  65.2 1.0 copy-start.4
  77.2 1.0 copy-start.6
  114.0 10.4 %collective-permute-start.4 = (bf16[16,120,640]{2,1,0:T(8,128)(2,1)S(1)}, bf16[16,120,640]{2,1,0:T(8,128)(2,1)}, u32[]{:S(2)}, u32[]{:S(2)}) collective-permute-start(bf16[16,120,640]{2,1,0:T(8,128)(2,1)S(1)} %all_to_all.15.own_ref), channel_id=1, source_target_pairs={{0,8},{8,0},{1,9},{9,1},{2,10},{10,2},{3,11},{11,3},{4,12},{12,4},... | collective-permute-start | bytes 7372808 | tf_op jit(solution)/shard_map/ppermute | solution.py:311
  119.2 5.2 %copy-start.8 = (f32[1280]{0:T(1024)S(1)}, f32[1280]{0:T(1024)}, u32[]{:S(2)}) copy-start(f32[1280]{0:T(1024)} %param.16) | copy-start | bytes 15364
  119.2 5.3 %copy-start = (bf16[1,128,1280]{2,1,0:T(8,128)(2,1)S(1)}, bf16[1,128,1280]{2,1,0:T(8,128)(2,1)}, u32[]{:S(2)}) copy-start(bf16[1,128,1280]{2,1,0:T(8,128)(2,1)} %param.10) | copy-start | bytes 983044
  119.2 5.3 %copy-start.1 = (f32[32,128]{1,0:T(8,128)S(1)}, f32[32,128]{1,0:T(8,128)}, u32[]{:S(2)}) copy-start(f32[32,128]{1,0:T(8,128)} %constant.27.clone.cos_ref) | copy-start | bytes 49156
  119.2 5.3 %copy-start.2 = (f32[32,128]{1,0:T(8,128)S(1)}, f32[32,128]{1,0:T(8,128)}, u32[]{:S(2)}) copy-start(f32[32,128]{1,0:T(8,128)} %constant.28.clone.sin_ref) | copy-start | bytes 49156
  119.2 32.4 %all-to-all-start.2 = ((bf16[16,80,640]{2,1,0:T(8,128)(2,1)}), bf16[16,80,640]{2,1,0:T(8,128)(2,1)}, u32[]{:S(2)}, u32[]{:S(2)}) async-start(bf16[16,80,640]{2,1,0:T(8,128)(2,1)} %broadcast_in_dim.46), calls=%async_computation.2 | async-start | bytes 3276800 | tf_op jit(solution)/shard_map/all_to_all | solution.py:241
  124.5 29.8 %copy-start.9 = (f32[1280]{0:T(1024)S(1)}, f32[1280]{0:T(1024)}, u32[]{:S(2)}) copy-start(f32[1280]{0:T(1024)} %param.17) | copy-start | bytes 15364
  151.6 6.0 %collective-permute-start.5 = (bf16[16,80,640]{2,1,0:T(8,128)(2,1)}, bf16[16,80,640]{2,1,0:T(8,128)(2,1)S(1)}, u32[]{:S(2)}, u32[]{:S(2)}) collective-permute-start(bf16[16,80,640]{2,1,0:T(8,128)(2,1)} %all-to-all-done.2.own_ref), channel_id=1, source_target_pairs={{0,8},{8,0},{1,9},{9,1},{2,10},{10,2},{3,11},{11,3},{4,12},{12,4},... | collective-permute-start | bytes 4915208 | tf_op jit(solution)/shard_map/ppermute | solution.py:314
  160.6 15.8 %copy-start.5 = (bf16[448,1280]{1,0:T(8,128)(2,1)S(1)}, bf16[448,1280]{1,0:T(8,128)(2,1)}, u32[]{:S(2)}) copy-start(bf16[448,1280]{1,0:T(8,128)(2,1)} %copy-done.4) | copy-start | bytes 3440644
  160.7 10.9 %collective-permute-start.6 = (bf16[128,1280]{1,0:T(8,128)(2,1)S(1)}, bf16[128,1280]{1,0:T(8,128)(2,1)S(1)}, u32[]{:S(2)}, u32[]{:S(2)}) collective-permute-start(bf16[128,1280]{1,0:T(8,128)(2,1)S(1)} %get-tuple-element.18.own_ref), channel_id=1, source_target_pairs={{0,2},{2,0},{4,6},{6,4},{1,3},{3,1},{5,7},{7,5},{8,10},{10,8},{12,... | collective-permute-start | bytes 983048 | tf_op jit(solution)/shard_map/ppermute | solution.py:316
  171.7 4.8 %collective-permute-start.7 = (bf16[2,128,1280]{2,1,0:T(8,128)(2,1)S(1)}, bf16[2,128,1280]{2,1,0:T(8,128)(2,1)S(1)}, u32[]{:S(2)}, u32[]{:S(2)}) collective-permute-start(bf16[2,128,1280]{2,1,0:T(8,128)(2,1)S(1)} %pad_maximum_fusion), channel_id=1, source_target_pairs={{0,8},{8,0},{1,9},{9,1},{2,10},{10,2},{3,11},{11,3},{4,12},{12,4},... | collective-permute-start | bytes 1966088 | tf_op jit(solution)/shard_map/ppermute | solution.py:317
  176.5 2.3 %copy-start.3 = (bf16[1280,1792]{1,0:T(8,128)(2,1)S(1)}, bf16[1280,1792]{1,0:T(8,128)(2,1)}, u32[]{:S(2)}) copy-start(bf16[1280,1792]{1,0:T(8,128)(2,1)} %all-gather.3.cloned.1.call-done.gate_up_ref) | copy-start | bytes 13762564
  178.8 1.3 copy-start.7
  186.3 4.0 %collective-permute-start.9 = (bf16[2,128,1280]{2,1,0:T(8,128)(2,1)S(1)}, bf16[2,128,1280]{2,1,0:T(8,128)(2,1)S(1)}, u32[]{:S(2)}, u32[]{:S(2)}) collective-permute-start(bf16[2,128,1280]{2,1,0:T(8,128)(2,1)S(1)} %get-tuple-element.20), channel_id=1, source_target_pairs={{0,8},{8,0},{1,9},{9,1},{2,10},{10,2},{3,11},{11,3},{4,12},{12,4},... | collective-permute-start | bytes 1966088 | tf_op jit(solution)/shard_map/ppermute | solution.py:319
  190.5 10.8 %collective-permute-start.10 = (bf16[128,1280]{1,0:T(8,128)(2,1)S(1)}, bf16[128,1280]{1,0:T(8,128)(2,1)S(1)}, u32[]{:S(2)}, u32[]{:S(2)}) collective-permute-start(bf16[128,1280]{1,0:T(8,128)(2,1)S(1)} %fusion.5), channel_id=1, source_target_pairs={{0,2},{2,0},{4,6},{6,4},{1,3},{3,1},{5,7},{7,5},{8,10},{10,8},{12,... | collective-permute-start | bytes 983048 | tf_op jit(solution)/shard_map/ppermute | solution.py:320
Sparse Core Ops, SparseCore 0:
  54.0 70.0 all-gather.2

commit v5 on v4

--- a/solution.py
+++ b/solution.py
@@ -226,16 +226,6 @@
     )(own, beside, across, gate_up, down_first, down_second)
 
 
-def turn(same_x):
-    pairs = []
-    for lo in range(2):
-        for core in range(2):
-            for hi in range(2):
-                to_lo = lo if same_x else 1 - lo
-                pairs.append((lo * 4 + core * 2 + hi, to_lo * 4 + hi * 2 + core))
-    return pairs
-
-
 def spread(block, axes, count):
     copies = jnp.broadcast_to(block[None], (count,) + block.shape)
     return lax.all_to_all(copies, axes, 0, 0, tiled=False)
@@ -246,7 +236,9 @@
 
 
 SWAP = [(0, 1), (1, 0)]
-BESIDE = [(y, y ^ 1) for y in range(4)]
+BESIDE = [(0, 3), (3, 0), (1, 2), (2, 1)]
+FIRST = [(y, y) for y in range(4)] + [(4 + y, 4 + (y + 1) % 4) for y in range(4)]
+SECOND = [(y, (y + 3) % 4) for y in range(4)] + [(4 + y, 4 + (y + 2) % 4) for y in range(4)]
 
 
 def shards(
@@ -280,44 +272,34 @@
     )
     part = spread(part, "z", 16).reshape(KHALF, 256)
     rows = merged[:, 400:]
-    along = ("x_lo", "core", "x_hi")
-    near = lax.ppermute(rows, along, turn(True))
-    far = lax.ppermute(rows, along, turn(False))
-    near = jnp.where(
-        x_lo == 0, jnp.concatenate([near, far], axis=0), jnp.concatenate([far, near], axis=0)
-    )
-    opposite = lax.ppermute(near, "y", [(y, y ^ 2) for y in range(4)])
+    far = lax.ppermute(rows, "x_lo", SWAP)
+    rows = jnp.where(
+        x_lo == 0, jnp.concatenate([rows, far], axis=0), jnp.concatenate([far, rows], axis=0)
+    )
+    first = lax.ppermute(rows, ("core", "y"), FIRST)
+    second = lax.ppermute(rows, ("core", "y"), SECOND)
     gate_up_rows = lax.all_gather(
-        jnp.concatenate([near, opposite], axis=1), "z", axis=0, tiled=True
-    )
-    down = after(down_weight, merged)
-    down_first = lax.ppermute(
-        down, ("core", "x_hi"), [(2 * a + b, 2 * b + a) for a in range(2) for b in range(2)]
-    )
-    down_second = lax.ppermute(
-        down,
-        ("core", "y", "x_hi"),
-        [
-            (8 * a + 2 * y + b, 8 * b + 2 * (y ^ 2) + a)
-            for a in range(2)
-            for y in range(4)
-            for b in range(2)
-        ],
-    )
-    part_qkv = after(part[:, :QW].T, near, down_first, down_second)
+        jnp.concatenate([first, second], axis=1), "z", axis=0, tiled=True
+    )
+    down_first = lax.ppermute(down_weight, ("core", "y"), FIRST)
+    down_second = lax.ppermute(down_weight, ("core", "y"), SECOND)
+    part_qkv = after(part[:, :QW].T, first)
     qkv_own = spread(part_qkv, ("x_lo", "y", "x_hi"), 16)
-    part_out = after(part[:, 128 : 128 + OW].T, qkv_own)
-    out_own = spread(part_out, ("x_lo", "y", "x_hi"), 16)
+    copies = jnp.broadcast_to(part[:, 128 : 128 + OW].T[None], (16, OW, KHALF))
+    copies = after(copies, qkv_own)
+    out_own = lax.all_to_all(copies, ("x_lo", "y", "x_hi"), 0, 0, tiled=False)
     qkv_other = lax.ppermute(qkv_own, "core", SWAP)
     attended, cache = attention(lengths, core_at, tokens, qkv_own, qkv_other, attn_gain)
-    out_own = after(out_own, attended)
+    out_own = after(out_own, attended, down_first, down_second)
     out_other = lax.ppermute(out_own, "core", SWAP)
     middle, normed_mid = middle_rows(core_at, tokens, attended, out_own, out_other, mlp_gain)
-    beside = lax.ppermute(normed_mid, "y", BESIDE)
+    beside = lax.ppermute(normed_mid, ("x_lo", "x_hi"), BESIDE)
     across = lax.ppermute(jnp.stack([normed_mid, beside]), "core", SWAP)
     keep, send = hidden_rows(normed_mid, beside, across, gate_up_rows, down_first, down_second)
     sums = keep + lax.ppermute(send, "core", SWAP).astype(F32)
-    feed_out = sums[0] + lax.ppermute(sums[1].astype(BF16), "y", BESIDE).astype(F32)
+    feed_out = sums[0] + lax.ppermute(
+        sums[1].astype(BF16), ("x_lo", "x_hi"), BESIDE
+    ).astype(F32)
     live_rows = (jnp.arange(LMAX) < lengths[0]).astype(F32)[:, None]
     hidden = (live_rows * (middle + feed_out)).astype(BF16)
     return (hidden[None], cache[None])

time: 210 us -> 206 us (0.981); the launches traced: 209 us -> 202 us
  waiting for transfers between devices: 72.8 us -> 60.5 us
  starting transfers between devices: 48.9 us -> 57.7 us
  blocking collectives: 43.9 us -> 40.6 us
    all_to_all x2 -> x1, waiting for transfers between devices: 21.3 us -> 0.01 us  [spread(): return lax.all_to_all(copies, axes, 0, 0, tiled=False)]
    ppermute x7, waiting for transfers between devices: 45.2 us -> 53.8 us  [the longest x1 19.4 us: shards(): down_first = lax.ppermute(down_weight, ('core', 'y'), FIRST)]
    ppermute x1, starting transfers between devices: 3.72 us -> 9.17 us  [shards(): qkv_other = lax.ppermute(qkv_own, 'core', SWAP)]
    all_to_all x0 -> x1, starting transfers between devices: none -> 4.56 us  [shards(): out_own = lax.all_to_all(copies, ('x_lo', 'y', 'x_hi'), 0, 0, tiled=False)]
    all_to_all x2 -> x1, starting transfers between devices: 14.1 us -> 9.54 us  [spread(): return lax.all_to_all(copies, axes, 0, 0, tiled=False)]
    ppermute x7, starting transfers between devices: 22.7 us -> 27.1 us  [the longest x1 4.53 us: shards(): second = lax.ppermute(rows, ('core', 'y'), SECOND)]
    all_to_all x1, blocking collectives: 35.4 us -> 32.2 us  [spread(): return lax.all_to_all(copies, axes, 0, 0, tiled=False)]
  transfers between devices with their start and end apart: 14 -> 14, of which waited for: 10 -> 9; matrix products, arithmetic and copies ran while one was open for 1% -> 1% of each run, Pallas kernels for 4% -> 4%
where the time goes in v5:
time: 206 us; the launch traced here: 202 us
  waiting for transfers between devices  60.5 us (29%)
  starting transfers between devices  57.7 us (28%)
  blocking collectives  40.6 us (20%)
  Pallas kernels  15.1 us (7%)
  between operations  15 us (7%)
  local copies, waits for them, and re-layouts  10 us (5%)
  other arithmetic  3.27 us (2%)
    all_to_all x1, blocking collectives, spread(): return lax.all_to_all(copies, axes, 0, 0, tiled=False)  32.2 us
    ppermute x1, waiting for transfers between devices, shards(): down_first = lax.ppermute(down_weight, ('core', 'y'), FIRST)  19.4 us
    ppermute x1, waiting for transfers between devices, shards(): down_second = lax.ppermute(down_weight, ('core', 'y'), SECOND)  13.8 us
    all_to_all x1, starting transfers between devices, spread(): return lax.all_to_all(copies, axes, 0, 0, tiled=False)  9.54 us
    ppermute x1, starting transfers between devices, shards(): qkv_other = lax.ppermute(qkv_own, 'core', SWAP)  9.17 us
    all_gather x1, blocking collectives, shards(): merged = lax.all_gather(merged, 'core', axis=0, tiled=True)  8.43 us
    ppermute x1, waiting for transfers between devices, shards(): beside = lax.ppermute(normed_mid, ('x_lo', 'x_hi'), BESIDE)  7.91 us
    ppermute x1, waiting for transfers between devices, shards(): lax.ppermute(sums[1].astype(BF16), ('x_lo', 'x_hi'), BESIDE).astype(F32)  7.66 us
  transfers between devices with their start and end apart: 14, of which 9 were waited for; matrix products, arithmetic and copies ran while one was open for 1% of the time, Pallas kernels for 4%

profile of v5, /device:TPU:1, one launch (start us, length us, event | category | flops | bytes accessed | tf_op | source)
XLA Modules:
  0.0 202.2 jit_solution(11124609773313807436)
XLA Ops:
  9.7 8.4 %all-gather = bf16[2,20,1296]{2,1,0:T(8,128)(2,1)S(1)} all-gather(bf16[1,20,1296]{2,1,0:T(8,128)(2,1)S(1)} %bitcast.43), channel_id=1, replica_groups=mesh['x_lo'=2,'z'=16,'core'=2,'y'=4,'x_hi'=2] {'core'}, dimensions={0}, use_global_device_ids=true | all-gather | bytes 155520 | tf_op jit(solution)/shard_map/all_gather | solution.py:263
  19.3 9.5 %all-to-all-start = ((bf16[16,40,256]{2,1,0:T(8,128)(2,1)}), bf16[16,40,256]{2,1,0:T(8,128)(2,1)S(1)}, u32[]{:S(2)}, u32[]{:S(2)}) async-start(bf16[16,40,256]{2,1,0:T(8,128)(2,1)} %broadcast_in_dim.43), calls=%async_computation | async-start | bytes 655360 | tf_op jit(solution)/shard_map/all_to_all | solution.py:231
  29.0 3.1 %collective-permute-start = (bf16[40,896]{1,0:T(8,128)(2,1)S(1)}, bf16[40,896]{1,0:T(8,128)(2,1)S(1)}, u32[]{:S(2)}, u32[]{:S(2)}) collective-permute-start(bf16[40,896]{1,0:T(8,128)(2,1)S(1)} %slice.52), channel_id=1, source_target_pairs={{0,256},{256,0},{1,257},{257,1},{2,258},{258,2},{3,259},{259,3},{4... | collective-permute-start | bytes 215048 | tf_op jit(solution)/shard_map/ppermute | solution.py:275
  34.1 3.2 %collective-permute-start.1 = (bf16[80,896]{1,0:T(8,128)(2,1)S(1)}, bf16[80,896]{1,0:T(8,128)(2,1)S(1)}, u32[]{:S(2)}, u32[]{:S(2)}) collective-permute-start(bf16[80,896]{1,0:T(8,128)(2,1)S(1)} %maximum_select_fusion), channel_id=1, source_target_pairs={{0,0},{2,2},{4,4},{6,6},{8,10},{10,12},{12,14},{14,8},{1,1},{3,3},... | collective-permute-start | bytes 430088 | tf_op jit(solution)/shard_map/ppermute | solution.py:279
  37.4 4.5 %collective-permute-start.8 = (bf16[80,896]{1,0:T(8,128)(2,1)S(1)}, bf16[80,896]{1,0:T(8,128)(2,1)S(1)}, u32[]{:S(2)}, u32[]{:S(2)}) collective-permute-start(bf16[80,896]{1,0:T(8,128)(2,1)S(1)} %maximum_select_fusion), channel_id=1, source_target_pairs={{0,6},{2,0},{4,2},{6,4},{8,12},{10,14},{12,8},{14,10},{1,7},{3,1},... | collective-permute-start | bytes 430088 | tf_op jit(solution)/shard_map/ppermute | solution.py:280
  41.9 3.1 %collective-permute-done.8 = bf16[80,896]{1,0:T(8,128)(2,1)S(1)} collective-permute-done((bf16[80,896]{1,0:T(8,128)(2,1)S(1)}, bf16[80,896]{1,0:T(8,128)(2,1)S(1)}, u32[]{:S(2)}, u32[]{:S(2)}) %collective-permute-start.8) | collective-permute-done | bytes 143392 | tf_op jit(solution)/shard_map/ppermute | solution.py:280
  46.2 32.2 %all_to_all.15.own_ref = bf16[16,120,640]{2,1,0:T(8,128)(2,1)S(1)} all-to-all(bf16[16,120,640]{2,1,0:T(8,128)(2,1)S(1)} %broadcast_in_dim.44), channel_id=1, replica_groups=mesh['x_lo'=2,'z'=16,'core'=2,'y'=4,'x_hi'=2] {'x_lo','y','x_hi'}, dimensions={0} | all-to-all | bytes 4915200 | tf_op jit(solution)/shard_map/all_to_all | solution.py:231
  78.3 9.2 %collective-permute-start.2 = (bf16[16,120,640]{2,1,0:T(8,128)(2,1)S(1)}, bf16[16,120,640]{2,1,0:T(8,128)(2,1)}, u32[]{:S(2)}, u32[]{:S(2)}) collective-permute-start(bf16[16,120,640]{2,1,0:T(8,128)(2,1)S(1)} %all_to_all.15.own_ref), channel_id=1, source_target_pairs={{0,8},{8,0},{1,9},{9,1},{2,10},{10,2},{3,11},{11,3},{4,12},{12,4},... | collective-permute-start | bytes 7372808 | tf_op jit(solution)/shard_map/ppermute | solution.py:291
  89.0 4.6 %all-to-all-start.2 = ((bf16[16,80,640]{2,1,0:T(8,128)(2,1)}), bf16[16,80,640]{2,1,0:T(8,128)(2,1)}, u32[]{:S(2)}, u32[]{:S(2)}) async-start(bf16[16,80,640]{2,1,0:T(8,128)(2,1)} %broadcast_in_dim.46), calls=%async_computation.2 | async-start | bytes 3276800 | tf_op jit(solution)/shard_map/all_to_all | solution.py:290
  93.6 3.1 %collective-permute-start.3 = (bf16[448,1280]{1,0:T(8,128)(2,1)}, bf16[448,1280]{1,0:T(8,128)(2,1)S(1)}, u32[]{:S(2)}, u32[]{:S(2)}) collective-permute-start(bf16[448,1280]{1,0:T(8,128)(2,1)} %param.15), channel_id=1, source_target_pairs={{0,0},{2,2},{4,4},{6,6},{8,10},{10,12},{12,14},{14,8},{1,1},{3,3},... | collective-permute-start | bytes 3440648 | tf_op jit(solution)/shard_map/ppermute | solution.py:284
  96.7 4.3 %collective-permute-start.4 = (bf16[448,1280]{1,0:T(8,128)(2,1)}, bf16[448,1280]{1,0:T(8,128)(2,1)S(1)}, u32[]{:S(2)}, u32[]{:S(2)}) collective-permute-start(bf16[448,1280]{1,0:T(8,128)(2,1)} %param.15), channel_id=1, source_target_pairs={{0,6},{2,0},{4,2},{6,4},{8,12},{10,14},{12,8},{14,10},{1,7},{3,1},... | collective-permute-start | bytes 3440648 | tf_op jit(solution)/shard_map/ppermute | solution.py:285
  101.7 5.9 %attention.1 = (bf16[1280,128]{1,0:T(8,128)(2,1)S(1)}, bf16[128,640]{1,0:T(8,128)(2,1)}) custom-call(s32[1]{0:T(128)} %copy.24.length_ref, s32[1]{0:T(128)} %bitcast.1.core_ref, bf16[128,1280]{1,0:T(8,128)(2,1)S(1)} %bitcast.37, bf16[16,120,640]{2,1,0:T(8,128)(2,1)S(1)} %all_to_all.15.own_ref, bf16[16,120,640]{2,1,0:T(8,128)(2,1)} %collective-permute-done.2.other_ref, ...), custom_call_target="tpu_custom_call" | custom-call | flops 800000000 | bytes 6000000 | tf_op jit(solution)/shard_map/attention/pallas_call | solution.py:174
  107.6 19.4 %collective-permute-done.3.first_ref = bf16[448,1280]{1,0:T(8,128)(2,1)S(1)} collective-permute-done((bf16[448,1280]{1,0:T(8,128)(2,1)}, bf16[448,1280]{1,0:T(8,128)(2,1)S(1)}, u32[]{:S(2)}, u32[]{:S(2)}) %collective-permute-start.3) | collective-permute-done | bytes 1146912 | tf_op jit(solution)/shard_map/ppermute | solution.py:284
  128.0 13.8 %collective-permute-done.4.second_ref = bf16[448,1280]{1,0:T(8,128)(2,1)S(1)} collective-permute-done((bf16[448,1280]{1,0:T(8,128)(2,1)}, bf16[448,1280]{1,0:T(8,128)(2,1)S(1)}, u32[]{:S(2)}, u32[]{:S(2)}) %collective-permute-start.4) | collective-permute-done | bytes 1146912 | tf_op jit(solution)/shard_map/ppermute | solution.py:285
  145.0 3.4 %collective-permute-done.5.other_ref = bf16[16,80,640]{2,1,0:T(8,128)(2,1)S(1)} collective-permute-done((bf16[16,80,640]{2,1,0:T(8,128)(2,1)}, bf16[16,80,640]{2,1,0:T(8,128)(2,1)S(1)}, u32[]{:S(2)}, u32[]{:S(2)}) %collective-permute-start.5) | collective-permute-done | bytes 1638432 | tf_op jit(solution)/shard_map/ppermute | solution.py:294
  148.4 3.0 %middle.1 = (f32[128,1280]{1,0:T(8,128)S(1)}, bf16[128,1280]{1,0:T(8,128)(2,1)S(1)}) custom-call(s32[1]{0:T(128)} %bitcast.1.core_ref, bf16[128,1280]{1,0:T(8,128)(2,1)S(1)} %bitcast.38, bf16[1280,128]{1,0:T(8,128)(2,1)S(1)} %get-tuple-element.12.attended_ref, bf16[16,80,640]{2,1,0:T(8,128)(2,1)} %all-to-all-done.2.own_ref, ...), custom_call_target="tpu_custom_call" | custom-call | flops 420000000 | bytes 4000000 | tf_op jit(solution)/shard_map/middle/pallas_call | solution.py:194
  151.5 4.5 %collective-permute-start.6 = (bf16[128,1280]{1,0:T(8,128)(2,1)S(1)}, bf16[128,1280]{1,0:T(8,128)(2,1)S(1)}, u32[]{:S(2)}, u32[]{:S(2)}) collective-permute-start(bf16[128,1280]{1,0:T(8,128)(2,1)S(1)} %get-tuple-element.16.own_ref), channel_id=1, source_target_pairs={{0,257},{257,0},{1,256},{256,1},{2,259},{259,2},{3,258},{258,3},{4... | collective-permute-start | bytes 983048 | tf_op jit(solution)/shard_map/ppermute | solution.py:296
  155.9 7.9 %collective-permute-done.6.next_ref = bf16[128,1280]{1,0:T(8,128)(2,1)S(1)} collective-permute-done((bf16[128,1280]{1,0:T(8,128)(2,1)S(1)}, bf16[128,1280]{1,0:T(8,128)(2,1)S(1)}, u32[]{:S(2)}, u32[]{:S(2)}) %collective-permute-start.6) | collective-permute-done | bytes 327712 | tf_op jit(solution)/shard_map/ppermute | solution.py:296
  163.9 3.0 %collective-permute-start.7 = (bf16[2,128,1280]{2,1,0:T(8,128)(2,1)S(1)}, bf16[2,128,1280]{2,1,0:T(8,128)(2,1)S(1)}, u32[]{:S(2)}, u32[]{:S(2)}) collective-permute-start(bf16[2,128,1280]{2,1,0:T(8,128)(2,1)S(1)} %pad_maximum_fusion), channel_id=1, source_target_pairs={{0,8},{8,0},{1,9},{9,1},{2,10},{10,2},{3,11},{11,3},{4,12},{12,4},... | collective-permute-start | bytes 1966088 | tf_op jit(solution)/shard_map/ppermute | solution.py:297
  168.5 2.3 %copy-done.3 = bf16[1280,1792]{1,0:T(8,128)(2,1)S(1)} copy-done((bf16[1280,1792]{1,0:T(8,128)(2,1)S(1)}, bf16[1280,1792]{1,0:T(8,128)(2,1)}, u32[]{:S(2)}) %copy-start.3) | copy-done | bytes 4587544
  172.1 6.2 %hidden.1 = (f32[2,128,1280]{2,1,0:T(8,128)S(1)}, bf16[2,128,1280]{2,1,0:T(8,128)(2,1)S(1)}) custom-call(bf16[128,1280]{1,0:T(8,128)(2,1)S(1)} %get-tuple-element.16.own_ref, bf16[128,1280]{1,0:T(8,128)(2,1)S(1)} %collective-permute-done.6.next_ref, bf16[2,128,1280]{2,1,0:T(8,128)(2,1)S(1)} %collective-permute-done.7.across_ref, ...), custom_call_target="tpu_custom_call" | custom-call | flops 3500000000 | bytes 9500000 | tf_op jit(solution)/shard_map/hidden/pallas_call | solution.py:212
  178.3 2.3 %collective-permute-start.9 = (bf16[2,128,1280]{2,1,0:T(8,128)(2,1)S(1)}, bf16[2,128,1280]{2,1,0:T(8,128)(2,1)S(1)}, u32[]{:S(2)}, u32[]{:S(2)}) collective-permute-start(bf16[2,128,1280]{2,1,0:T(8,128)(2,1)S(1)} %get-tuple-element.18), channel_id=1, source_target_pairs={{0,8},{8,0},{1,9},{9,1},{2,10},{10,2},{3,11},{11,3},{4,12},{12,4},... | collective-permute-start | bytes 1966088 | tf_op jit(solution)/shard_map/ppermute | solution.py:299
  182.5 4.4 %collective-permute-start.10 = (bf16[128,1280]{1,0:T(8,128)(2,1)S(1)}, bf16[128,1280]{1,0:T(8,128)(2,1)S(1)}, u32[]{:S(2)}, u32[]{:S(2)}) collective-permute-start(bf16[128,1280]{1,0:T(8,128)(2,1)S(1)} %fusion.5), channel_id=1, source_target_pairs={{0,257},{257,0},{1,256},{256,1},{2,259},{259,2},{3,258},{258,3},{4... | collective-permute-start | bytes 983048 | tf_op jit(solution)/shard_map/ppermute | solution.py:300
  186.8 7.7 %collective-permute-done.10 = bf16[128,1280]{1,0:T(8,128)(2,1)S(1)} collective-permute-done((bf16[128,1280]{1,0:T(8,128)(2,1)S(1)}, bf16[128,1280]{1,0:T(8,128)(2,1)S(1)}, u32[]{:S(2)}, u32[]{:S(2)}) %collective-permute-start.10) | collective-permute-done | bytes 327712 | tf_op jit(solution)/shard_map/ppermute | solution.py:300
  (63 shorter events, 18.1 us)
Async XLA Ops:
  19.3 26.4 %all-to-all-start = ((bf16[16,40,256]{2,1,0:T(8,128)(2,1)}), bf16[16,40,256]{2,1,0:T(8,128)(2,1)S(1)}, u32[]{:S(2)}, u32[]{:S(2)}) async-start(bf16[16,40,256]{2,1,0:T(8,128)(2,1)} %broadcast_in_dim.43), calls=%async_computation | async-start | bytes 655360 | tf_op jit(solution)/shard_map/all_to_all | solution.py:231
  28.9 139.6 %all-gather.3.cloned.1.call-start = ((), (), s32[]{:S(2)}) async-start(), calls=%async_computation.3 | async-start | bytes 4874240 | tf_op jit(solution)/shard_map/all_gather | solution.py:281
  29.0 5.1 %collective-permute-start = (bf16[40,896]{1,0:T(8,128)(2,1)S(1)}, bf16[40,896]{1,0:T(8,128)(2,1)S(1)}, u32[]{:S(2)}, u32[]{:S(2)}) collective-permute-start(bf16[40,896]{1,0:T(8,128)(2,1)S(1)} %slice.52), channel_id=1, source_target_pairs={{0,256},{256,0},{1,257},{257,1},{2,258},{258,2},{3,259},{259,3},{4... | collective-permute-start | bytes 215048 | tf_op jit(solution)/shard_map/ppermute | solution.py:275
  34.1 7.8 %collective-permute-start.1 = (bf16[80,896]{1,0:T(8,128)(2,1)S(1)}, bf16[80,896]{1,0:T(8,128)(2,1)S(1)}, u32[]{:S(2)}, u32[]{:S(2)}) collective-permute-start(bf16[80,896]{1,0:T(8,128)(2,1)S(1)} %maximum_select_fusion), channel_id=1, source_target_pairs={{0,0},{2,2},{4,4},{6,6},{8,10},{10,12},{12,14},{14,8},{1,1},{3,3},... | collective-permute-start | bytes 430088 | tf_op jit(solution)/shard_map/ppermute | solution.py:279
  37.4 7.6 %collective-permute-start.8 = (bf16[80,896]{1,0:T(8,128)(2,1)S(1)}, bf16[80,896]{1,0:T(8,128)(2,1)S(1)}, u32[]{:S(2)}, u32[]{:S(2)}) collective-permute-start(bf16[80,896]{1,0:T(8,128)(2,1)S(1)} %maximum_select_fusion), channel_id=1, source_target_pairs={{0,6},{2,0},{4,2},{6,4},{8,12},{10,14},{12,8},{14,10},{1,7},{3,1},... | collective-permute-start | bytes 430088 | tf_op jit(solution)/shard_map/ppermute | solution.py:280
  78.3 23.3 %collective-permute-start.2 = (bf16[16,120,640]{2,1,0:T(8,128)(2,1)S(1)}, bf16[16,120,640]{2,1,0:T(8,128)(2,1)}, u32[]{:S(2)}, u32[]{:S(2)}) collective-permute-start(bf16[16,120,640]{2,1,0:T(8,128)(2,1)S(1)} %all_to_all.15.own_ref), channel_id=1, source_target_pairs={{0,8},{8,0},{1,9},{9,1},{2,10},{10,2},{3,11},{11,3},{4,12},{12,4},... | collective-permute-start | bytes 7372808 | tf_op jit(solution)/shard_map/ppermute | solution.py:291
  89.0 12.7 %copy-start.8 = (f32[1280]{0:T(1024)S(1)}, f32[1280]{0:T(1024)}, u32[]{:S(2)}) copy-start(f32[1280]{0:T(1024)} %param.16) | copy-start | bytes 15364
  89.0 12.7 %copy-start = (bf16[1,128,1280]{2,1,0:T(8,128)(2,1)S(1)}, bf16[1,128,1280]{2,1,0:T(8,128)(2,1)}, u32[]{:S(2)}) copy-start(bf16[1,128,1280]{2,1,0:T(8,128)(2,1)} %param.10) | copy-start | bytes 983044
  89.0 12.7 %copy-start.1 = (f32[32,128]{1,0:T(8,128)S(1)}, f32[32,128]{1,0:T(8,128)}, u32[]{:S(2)}) copy-start(f32[32,128]{1,0:T(8,128)} %constant.27.clone.cos_ref) | copy-start | bytes 49156
  89.0 12.7 %copy-start.2 = (f32[32,128]{1,0:T(8,128)S(1)}, f32[32,128]{1,0:T(8,128)}, u32[]{:S(2)}) copy-start(f32[32,128]{1,0:T(8,128)} %constant.28.clone.sin_ref) | copy-start | bytes 49156
  89.0 53.9 %all-to-all-start.2 = ((bf16[16,80,640]{2,1,0:T(8,128)(2,1)}), bf16[16,80,640]{2,1,0:T(8,128)(2,1)}, u32[]{:S(2)}, u32[]{:S(2)}) async-start(bf16[16,80,640]{2,1,0:T(8,128)(2,1)} %broadcast_in_dim.46), calls=%async_computation.2 | async-start | bytes 3276800 | tf_op jit(solution)/shard_map/all_to_all | solution.py:290
  93.6 33.4 %collective-permute-start.3 = (bf16[448,1280]{1,0:T(8,128)(2,1)}, bf16[448,1280]{1,0:T(8,128)(2,1)S(1)}, u32[]{:S(2)}, u32[]{:S(2)}) collective-permute-start(bf16[448,1280]{1,0:T(8,128)(2,1)} %param.15), channel_id=1, source_target_pairs={{0,0},{2,2},{4,4},{6,6},{8,10},{10,12},{12,14},{14,8},{1,1},{3,3},... | collective-permute-start | bytes 3440648 | tf_op jit(solution)/shard_map/ppermute | solution.py:284
  96.7 45.1 %collective-permute-start.4 = (bf16[448,1280]{1,0:T(8,128)(2,1)}, bf16[448,1280]{1,0:T(8,128)(2,1)S(1)}, u32[]{:S(2)}, u32[]{:S(2)}) collective-permute-start(bf16[448,1280]{1,0:T(8,128)(2,1)} %param.15), channel_id=1, source_target_pairs={{0,6},{2,0},{4,2},{6,4},{8,12},{10,14},{12,8},{14,10},{1,7},{3,1},... | collective-permute-start | bytes 3440648 | tf_op jit(solution)/shard_map/ppermute | solution.py:285
  101.7 43.0 %copy-start.9 = (f32[1280]{0:T(1024)S(1)}, f32[1280]{0:T(1024)}, u32[]{:S(2)}) copy-start(f32[1280]{0:T(1024)} %param.17) | copy-start | bytes 15364
  127.0 1.0 copy-start.4
  141.8 1.0 copy-start.6
  142.8 5.6 %collective-permute-start.5 = (bf16[16,80,640]{2,1,0:T(8,128)(2,1)}, bf16[16,80,640]{2,1,0:T(8,128)(2,1)S(1)}, u32[]{:S(2)}, u32[]{:S(2)}) collective-permute-start(bf16[16,80,640]{2,1,0:T(8,128)(2,1)} %all-to-all-done.2.own_ref), channel_id=1, source_target_pairs={{0,8},{8,0},{1,9},{9,1},{2,10},{10,2},{3,11},{11,3},{4,12},{12,4},... | collective-permute-start | bytes 4915208 | tf_op jit(solution)/shard_map/ppermute | solution.py:294
  151.4 17.1 %copy-start.5 = (bf16[448,1280]{1,0:T(8,128)(2,1)S(1)}, bf16[448,1280]{1,0:T(8,128)(2,1)}, u32[]{:S(2)}) copy-start(bf16[448,1280]{1,0:T(8,128)(2,1)} %copy-done.4) | copy-start | bytes 3440644
  151.5 12.4 %collective-permute-start.6 = (bf16[128,1280]{1,0:T(8,128)(2,1)S(1)}, bf16[128,1280]{1,0:T(8,128)(2,1)S(1)}, u32[]{:S(2)}, u32[]{:S(2)}) collective-permute-start(bf16[128,1280]{1,0:T(8,128)(2,1)S(1)} %get-tuple-element.16.own_ref), channel_id=1, source_target_pairs={{0,257},{257,0},{1,256},{256,1},{2,259},{259,2},{3,258},{258,3},{4... | collective-permute-start | bytes 983048 | tf_op jit(solution)/shard_map/ppermute | solution.py:296
  163.9 4.6 %collective-permute-start.7 = (bf16[2,128,1280]{2,1,0:T(8,128)(2,1)S(1)}, bf16[2,128,1280]{2,1,0:T(8,128)(2,1)S(1)}, u32[]{:S(2)}, u32[]{:S(2)}) collective-permute-start(bf16[2,128,1280]{2,1,0:T(8,128)(2,1)S(1)} %pad_maximum_fusion), channel_id=1, source_target_pairs={{0,8},{8,0},{1,9},{9,1},{2,10},{10,2},{3,11},{11,3},{4,12},{12,4},... | collective-permute-start | bytes 1966088 | tf_op jit(solution)/shard_map/ppermute | solution.py:297
  168.5 2.3 %copy-start.3 = (bf16[1280,1792]{1,0:T(8,128)(2,1)S(1)}, bf16[1280,1792]{1,0:T(8,128)(2,1)}, u32[]{:S(2)}) copy-start(bf16[1280,1792]{1,0:T(8,128)(2,1)} %all-gather.3.cloned.1.call-done.gate_up_ref) | copy-start | bytes 13762564
  170.8 1.3 copy-start.7
  178.3 4.0 %collective-permute-start.9 = (bf16[2,128,1280]{2,1,0:T(8,128)(2,1)S(1)}, bf16[2,128,1280]{2,1,0:T(8,128)(2,1)S(1)}, u32[]{:S(2)}, u32[]{:S(2)}) collective-permute-start(bf16[2,128,1280]{2,1,0:T(8,128)(2,1)S(1)} %get-tuple-element.18), channel_id=1, source_target_pairs={{0,8},{8,0},{1,9},{9,1},{2,10},{10,2},{3,11},{11,3},{4,12},{12,4},... | collective-permute-start | bytes 1966088 | tf_op jit(solution)/shard_map/ppermute | solution.py:299
  182.5 12.0 %collective-permute-start.10 = (bf16[128,1280]{1,0:T(8,128)(2,1)S(1)}, bf16[128,1280]{1,0:T(8,128)(2,1)S(1)}, u32[]{:S(2)}, u32[]{:S(2)}) collective-permute-start(bf16[128,1280]{1,0:T(8,128)(2,1)S(1)} %fusion.5), channel_id=1, source_target_pairs={{0,257},{257,0},{1,256},{256,1},{2,259},{259,2},{3,258},{258,3},{4... | collective-permute-start | bytes 983048 | tf_op jit(solution)/shard_map/ppermute | solution.py:300
Sparse Core Ops, SparseCore 0:
  45.9 72.9 all-gather.2

commit v6 on v5

--- a/solution.py
+++ b/solution.py
@@ -180,7 +180,7 @@
         in_specs=[SMEM, SMEM] + [VMEM] * 6,
         out_specs=(VMEM, VMEM),
         scratch_shapes=[pltpu.VMEM((1920, LMAX), F32)],
-        compiler_params=pltpu.CompilerParams(vmem_limit_bytes=32 << 20),
+        compiler_params=pltpu.CompilerParams(vmem_limit_bytes=16 << 20),
         cost_estimate=pl.CostEstimate(
             flops=800000000, bytes_accessed=6000000, transcendentals=400000
         ),
@@ -200,7 +200,7 @@
         in_specs=[SMEM] + [VMEM] * 5,
         out_specs=(VMEM, VMEM),
         scratch_shapes=[pltpu.VMEM((D, LMAX), F32), pltpu.VMEM((D, LMAX), F32)],
-        compiler_params=pltpu.CompilerParams(vmem_limit_bytes=32 << 20),
+        compiler_params=pltpu.CompilerParams(vmem_limit_bytes=16 << 20),
         cost_estimate=pl.CostEstimate(
             flops=420000000, bytes_accessed=4000000, transcendentals=1000
         ),
@@ -218,7 +218,7 @@
         in_specs=[VMEM] * 6,
         out_specs=(VMEM, VMEM),
         scratch_shapes=[pltpu.VMEM((4 * LMAX, D), BF16)],
-        compiler_params=pltpu.CompilerParams(vmem_limit_bytes=36 << 20),
+        compiler_params=pltpu.CompilerParams(vmem_limit_bytes=24 << 20),
         cost_estimate=pl.CostEstimate(
             flops=3500000000, bytes_accessed=9500000, transcendentals=500000
         ),
@@ -236,9 +236,27 @@
 
 
 SWAP = [(0, 1), (1, 0)]
-BESIDE = [(0, 3), (3, 0), (1, 2), (2, 1)]
 FIRST = [(y, y) for y in range(4)] + [(4 + y, 4 + (y + 1) % 4) for y in range(4)]
-SECOND = [(y, (y + 3) % 4) for y in range(4)] + [(4 + y, 4 + (y + 2) % 4) for y in range(4)]
+SECOND = [
+    (
+        ((lo * 2 + core) * 4 + y) * 2 + hi,
+        ((lo * 2) * 4 + (y + 3) % 4) * 2 + hi
+        if core == 0
+        else (((1 - lo) * 2 + 1) * 4 + y) * 2 + 1 - hi,
+    )
+    for lo in range(2)
+    for core in range(2)
+    for y in range(4)
+    for hi in range(2)
+]
+BESIDE = [
+    ((lo * 4 + y) * 2 + hi, ((1 - lo) * 4 + (y ^ 2)) * 2 + 1 - hi)
+    for lo in range(2)
+    for y in range(4)
+    for hi in range(2)
+]
+PLANE = ("x_lo", "y", "x_hi")
+CORES = ("x_lo", "core", "y", "x_hi")
 
 
 def shards(
@@ -277,12 +295,12 @@
         x_lo == 0, jnp.concatenate([rows, far], axis=0), jnp.concatenate([far, rows], axis=0)
     )
     first = lax.ppermute(rows, ("core", "y"), FIRST)
-    second = lax.ppermute(rows, ("core", "y"), SECOND)
+    second = lax.ppermute(rows, CORES, SECOND)
     gate_up_rows = lax.all_gather(
         jnp.concatenate([first, second], axis=1), "z", axis=0, tiled=True
     )
     down_first = lax.ppermute(down_weight, ("core", "y"), FIRST)
-    down_second = lax.ppermute(down_weight, ("core", "y"), SECOND)
+    down_second = lax.ppermute(down_weight, CORES, SECOND)
     part_qkv = after(part[:, :QW].T, first)
     qkv_own = spread(part_qkv, ("x_lo", "y", "x_hi"), 16)
     copies = jnp.broadcast_to(part[:, 128 : 128 + OW].T[None], (16, OW, KHALF))
@@ -293,13 +311,11 @@
     out_own = after(out_own, attended, down_first, down_second)
     out_other = lax.ppermute(out_own, "core", SWAP)
     middle, normed_mid = middle_rows(core_at, tokens, attended, out_own, out_other, mlp_gain)
-    beside = lax.ppermute(normed_mid, ("x_lo", "x_hi"), BESIDE)
+    beside = lax.ppermute(normed_mid, PLANE, BESIDE)
     across = lax.ppermute(jnp.stack([normed_mid, beside]), "core", SWAP)
     keep, send = hidden_rows(normed_mid, beside, across, gate_up_rows, down_first, down_second)
     sums = keep + lax.ppermute(send, "core", SWAP).astype(F32)
-    feed_out = sums[0] + lax.ppermute(
-        sums[1].astype(BF16), ("x_lo", "x_hi"), BESIDE
-    ).astype(F32)
+    feed_out = sums[0] + lax.ppermute(sums[1].astype(BF16), PLANE, BESIDE).astype(F32)
     live_rows = (jnp.arange(LMAX) < lengths[0]).astype(F32)[:, None]
     hidden = (live_rows * (middle + feed_out)).astype(BF16)
     return (hidden[None], cache[None])

time: 206 us -> 198 us (0.961)
  the two profiles are of different devices: /device:TPU:1 before, /device:TPU:34 now
where the time goes in v6:
time: 198 us; the launch traced here: 197 us
  waiting for transfers between devices  62.1 us (31%)
  starting transfers between devices  51.1 us (26%)
  blocking collectives  40.7 us (21%)
  Pallas kernels  15.1 us (8%)
  between operations  15 us (8%)
  local copies, waits for them, and re-layouts  10 us (5%)
  other arithmetic  3.31 us (2%)
    all_to_all x1, blocking collectives, spread(): return lax.all_to_all(copies, axes, 0, 0, tiled=False)  38.7 us
    ppermute x1, waiting for transfers between devices, shards(): down_second = lax.ppermute(down_weight, CORES, SECOND)  19.4 us
    all_to_all x1, starting transfers between devices, spread(): return lax.all_to_all(copies, axes, 0, 0, tiled=False)  15.2 us
    ppermute x1, waiting for transfers between devices, shards(): beside = lax.ppermute(normed_mid, PLANE, BESIDE)  12.4 us
    ppermute x1, waiting for transfers between devices, shards(): lax.ppermute(sums[1].astype(BF16), PLANE, BESIDE).astype(F32)  11.8 us
    unnamed x22, local copies, waits for them, and re-layouts  6.58 us
    pallas_call x1, Pallas kernels, hidden_rows(): pl.pallas_call(hidden_kernel, out_shape=(jax.ShapeDtypeStruct((2, LMAX, D...  6.23 us
    ppermute x1, starting transfers between devices, shards(): out_other = lax.ppermute(out_own, 'core', SWAP)  6 us
  transfers between devices with their start and end apart: 14, of which 9 were waited for; matrix products, arithmetic and copies ran while one was open for 1% of the time, Pallas kernels for 5%

profile of v6, /device:TPU:34, one launch (start us, length us, event | category | flops | bytes accessed | tf_op | source)
XLA Modules:
  0.0 197.3 jit_solution(10561291175707484591)
XLA Ops:
  12.8 15.2 %all-to-all-start = ((bf16[16,40,256]{2,1,0:T(8,128)(2,1)}), bf16[16,40,256]{2,1,0:T(8,128)(2,1)S(1)}, u32[]{:S(2)}, u32[]{:S(2)}) async-start(bf16[16,40,256]{2,1,0:T(8,128)(2,1)} %broadcast_in_dim.43), calls=%async_computation | async-start | bytes 655360 | tf_op jit(solution)/shard_map/all_to_all | solution.py:231
  28.2 2.4 %collective-permute-start = (bf16[40,896]{1,0:T(8,128)(2,1)S(1)}, bf16[40,896]{1,0:T(8,128)(2,1)S(1)}, u32[]{:S(2)}, u32[]{:S(2)}) collective-permute-start(bf16[40,896]{1,0:T(8,128)(2,1)S(1)} %slice.52), channel_id=1, source_target_pairs={{0,256},{256,0},{1,257},{257,1},{2,258},{258,2},{3,259},{259,3},{4... | collective-permute-start | bytes 215048 | tf_op jit(solution)/shard_map/ppermute | solution.py:293
  30.6 3.8 %collective-permute-done = bf16[40,896]{1,0:T(8,128)(2,1)S(1)} collective-permute-done((bf16[40,896]{1,0:T(8,128)(2,1)S(1)}, bf16[40,896]{1,0:T(8,128)(2,1)S(1)}, u32[]{:S(2)}, u32[]{:S(2)}) %collective-permute-start) | collective-permute-done | bytes 71712 | tf_op jit(solution)/shard_map/ppermute | solution.py:293
  35.1 4.9 %collective-permute-start.8 = (bf16[80,896]{1,0:T(8,128)(2,1)S(1)}, bf16[80,896]{1,0:T(8,128)(2,1)S(1)}, u32[]{:S(2)}, u32[]{:S(2)}) collective-permute-start(bf16[80,896]{1,0:T(8,128)(2,1)S(1)} %maximum_select_fusion), channel_id=1, source_target_pairs={{0,6},{1,7},{2,0},{3,1},{4,2},{5,3},{6,4},{7,5},{8,265},{9,264},{1... | collective-permute-start | bytes 430088 | tf_op jit(solution)/shard_map/ppermute | solution.py:298
  40.0 2.6 %collective-permute-done.8 = bf16[80,896]{1,0:T(8,128)(2,1)S(1)} collective-permute-done((bf16[80,896]{1,0:T(8,128)(2,1)S(1)}, bf16[80,896]{1,0:T(8,128)(2,1)S(1)}, u32[]{:S(2)}, u32[]{:S(2)}) %collective-permute-start.8) | collective-permute-done | bytes 143392 | tf_op jit(solution)/shard_map/ppermute | solution.py:298
  43.4 5.2 %all-to-all-done = bf16[16,40,256]{2,1,0:T(8,128)(2,1)S(1)} async-done(((bf16[16,40,256]{2,1,0:T(8,128)(2,1)}), bf16[16,40,256]{2,1,0:T(8,128)(2,1)S(1)}, u32[]{:S(2)}, u32[]{:S(2)}) %all-to-all-start) | async-done | bytes 327712 | tf_op jit(solution)/shard_map/all_to_all | solution.py:231
  49.0 38.7 %all_to_all.15.own_ref = bf16[16,120,640]{2,1,0:T(8,128)(2,1)S(1)} all-to-all(bf16[16,120,640]{2,1,0:T(8,128)(2,1)S(1)} %broadcast_in_dim.44), channel_id=1, replica_groups=mesh['x_lo'=2,'z'=16,'core'=2,'y'=4,'x_hi'=2] {'x_lo','y','x_hi'}, dimensions={0} | all-to-all | bytes 4915200 | tf_op jit(solution)/shard_map/all_to_all | solution.py:231
  91.1 5.0 %all-to-all-start.2 = ((bf16[16,80,640]{2,1,0:T(8,128)(2,1)}), bf16[16,80,640]{2,1,0:T(8,128)(2,1)}, u32[]{:S(2)}, u32[]{:S(2)}) async-start(bf16[16,80,640]{2,1,0:T(8,128)(2,1)} %broadcast_in_dim.46), calls=%async_computation.2 | async-start | bytes 3276800 | tf_op jit(solution)/shard_map/all_to_all | solution.py:308
  96.1 1.9 collective-permute-start.3
  98.1 4.6 %collective-permute-start.4 = (bf16[448,1280]{1,0:T(8,128)(2,1)}, bf16[448,1280]{1,0:T(8,128)(2,1)S(1)}, u32[]{:S(2)}, u32[]{:S(2)}) collective-permute-start(bf16[448,1280]{1,0:T(8,128)(2,1)} %param.15), channel_id=1, source_target_pairs={{0,6},{1,7},{2,0},{3,1},{4,2},{5,3},{6,4},{7,5},{8,265},{9,264},{1... | collective-permute-start | bytes 3440648 | tf_op jit(solution)/shard_map/ppermute | solution.py:303
  103.4 5.9 %attention.1 = (bf16[1280,128]{1,0:T(8,128)(2,1)S(1)}, bf16[128,640]{1,0:T(8,128)(2,1)}) custom-call(s32[1]{0:T(128)} %copy.24.length_ref, s32[1]{0:T(128)} %bitcast.1.core_ref, bf16[128,1280]{1,0:T(8,128)(2,1)S(1)} %bitcast.37, bf16[16,120,640]{2,1,0:T(8,128)(2,1)S(1)} %all_to_all.15.own_ref, bf16[16,120,640]{2,1,0:T(8,128)(2,1)} %collective-permute-done.2.other_ref, ...), custom_call_target="tpu_custom_call" | custom-call | flops 800000000 | bytes 6000000 | tf_op jit(solution)/shard_map/attention/pallas_call | solution.py:174
  110.3 19.4 %collective-permute-done.4.second_ref = bf16[448,1280]{1,0:T(8,128)(2,1)S(1)} collective-permute-done((bf16[448,1280]{1,0:T(8,128)(2,1)}, bf16[448,1280]{1,0:T(8,128)(2,1)S(1)}, u32[]{:S(2)}, u32[]{:S(2)}) %collective-permute-start.4) | collective-permute-done | bytes 1146912 | tf_op jit(solution)/shard_map/ppermute | solution.py:303
  130.8 6.0 %collective-permute-start.5 = (bf16[16,80,640]{2,1,0:T(8,128)(2,1)}, bf16[16,80,640]{2,1,0:T(8,128)(2,1)S(1)}, u32[]{:S(2)}, u32[]{:S(2)}) collective-permute-start(bf16[16,80,640]{2,1,0:T(8,128)(2,1)} %all-to-all-done.2.own_ref), channel_id=1, source_target_pairs={{0,8},{8,0},{1,9},{9,1},{2,10},{10,2},{3,11},{11,3},{4,12},{12,4},... | collective-permute-start | bytes 4915208 | tf_op jit(solution)/shard_map/ppermute | solution.py:312
  137.0 3.1 %collective-permute-done.5.other_ref = bf16[16,80,640]{2,1,0:T(8,128)(2,1)S(1)} collective-permute-done((bf16[16,80,640]{2,1,0:T(8,128)(2,1)}, bf16[16,80,640]{2,1,0:T(8,128)(2,1)S(1)}, u32[]{:S(2)}, u32[]{:S(2)}) %collective-permute-start.5) | collective-permute-done | bytes 1638432 | tf_op jit(solution)/shard_map/ppermute | solution.py:312
  140.1 3.0 %middle.1 = (f32[128,1280]{1,0:T(8,128)S(1)}, bf16[128,1280]{1,0:T(8,128)(2,1)S(1)}) custom-call(s32[1]{0:T(128)} %bitcast.1.core_ref, bf16[128,1280]{1,0:T(8,128)(2,1)S(1)} %bitcast.38, bf16[1280,128]{1,0:T(8,128)(2,1)S(1)} %get-tuple-element.12.attended_ref, bf16[16,80,640]{2,1,0:T(8,128)(2,1)} %all-to-all-done.2.own_ref, ...), custom_call_target="tpu_custom_call" | custom-call | flops 420000000 | bytes 4000000 | tf_op jit(solution)/shard_map/middle/pallas_call | solution.py:194
  143.1 2.1 %collective-permute-start.6 = (bf16[128,1280]{1,0:T(8,128)(2,1)S(1)}, bf16[128,1280]{1,0:T(8,128)(2,1)S(1)}, u32[]{:S(2)}, u32[]{:S(2)}) collective-permute-start(bf16[128,1280]{1,0:T(8,128)(2,1)S(1)} %get-tuple-element.16.own_ref), channel_id=1, source_target_pairs={{0,261},{1,260},{2,263},{3,262},{4,257},{5,256},{6,259},{7,258},{2... | collective-permute-start | bytes 983048 | tf_op jit(solution)/shard_map/ppermute | solution.py:314
  145.2 12.4 %collective-permute-done.6.next_ref = bf16[128,1280]{1,0:T(8,128)(2,1)S(1)} collective-permute-done((bf16[128,1280]{1,0:T(8,128)(2,1)S(1)}, bf16[128,1280]{1,0:T(8,128)(2,1)S(1)}, u32[]{:S(2)}, u32[]{:S(2)}) %collective-permute-start.6) | collective-permute-done | bytes 327712 | tf_op jit(solution)/shard_map/ppermute | solution.py:314
  157.6 2.1 %collective-permute-start.7 = (bf16[2,128,1280]{2,1,0:T(8,128)(2,1)S(1)}, bf16[2,128,1280]{2,1,0:T(8,128)(2,1)S(1)}, u32[]{:S(2)}, u32[]{:S(2)}) collective-permute-start(bf16[2,128,1280]{2,1,0:T(8,128)(2,1)S(1)} %pad_maximum_fusion), channel_id=1, source_target_pairs={{0,8},{8,0},{1,9},{9,1},{2,10},{10,2},{3,11},{11,3},{4,12},{12,4},... | collective-permute-start | bytes 1966088 | tf_op jit(solution)/shard_map/ppermute | solution.py:315
  161.6 2.3 %copy-done.3 = bf16[1280,1792]{1,0:T(8,128)(2,1)S(1)} copy-done((bf16[1280,1792]{1,0:T(8,128)(2,1)S(1)}, bf16[1280,1792]{1,0:T(8,128)(2,1)}, u32[]{:S(2)}) %copy-start.3) | copy-done | bytes 4587544
  165.1 6.2 %hidden.1 = (f32[2,128,1280]{2,1,0:T(8,128)S(1)}, bf16[2,128,1280]{2,1,0:T(8,128)(2,1)S(1)}) custom-call(bf16[128,1280]{1,0:T(8,128)(2,1)S(1)} %get-tuple-element.16.own_ref, bf16[128,1280]{1,0:T(8,128)(2,1)S(1)} %collective-permute-done.6.next_ref, bf16[2,128,1280]{2,1,0:T(8,128)(2,1)S(1)} %collective-permute-done.7.across_ref, ...), custom_call_target="tpu_custom_call" | custom-call | flops 3500000000 | bytes 9500000 | tf_op jit(solution)/shard_map/hidden/pallas_call | solution.py:212
  171.4 2.0 %collective-permute-start.9 = (bf16[2,128,1280]{2,1,0:T(8,128)(2,1)S(1)}, bf16[2,128,1280]{2,1,0:T(8,128)(2,1)S(1)}, u32[]{:S(2)}, u32[]{:S(2)}) collective-permute-start(bf16[2,128,1280]{2,1,0:T(8,128)(2,1)S(1)} %get-tuple-element.18), channel_id=1, source_target_pairs={{0,8},{8,0},{1,9},{9,1},{2,10},{10,2},{3,11},{11,3},{4,12},{12,4},... | collective-permute-start | bytes 1966088 | tf_op jit(solution)/shard_map/ppermute | solution.py:317
  173.4 1.9 collective-permute-done.9
  175.6 2.2 %collective-permute-start.10 = (bf16[128,1280]{1,0:T(8,128)(2,1)S(1)}, bf16[128,1280]{1,0:T(8,128)(2,1)S(1)}, u32[]{:S(2)}, u32[]{:S(2)}) collective-permute-start(bf16[128,1280]{1,0:T(8,128)(2,1)S(1)} %fusion.5), channel_id=1, source_target_pairs={{0,261},{1,260},{2,263},{3,262},{4,257},{5,256},{6,259},{7,258},{2... | collective-permute-start | bytes 983048 | tf_op jit(solution)/shard_map/ppermute | solution.py:318
  177.8 11.8 %collective-permute-done.10 = bf16[128,1280]{1,0:T(8,128)(2,1)S(1)} collective-permute-done((bf16[128,1280]{1,0:T(8,128)(2,1)S(1)}, bf16[128,1280]{1,0:T(8,128)(2,1)S(1)}, u32[]{:S(2)}, u32[]{:S(2)}) %collective-permute-start.10) | collective-permute-done | bytes 327712 | tf_op jit(solution)/shard_map/ppermute | solution.py:318
  (63 shorter events, 17.5 us)
Async XLA Ops:
  12.8 35.8 %all-to-all-start = ((bf16[16,40,256]{2,1,0:T(8,128)(2,1)}), bf16[16,40,256]{2,1,0:T(8,128)(2,1)S(1)}, u32[]{:S(2)}, u32[]{:S(2)}) async-start(bf16[16,40,256]{2,1,0:T(8,128)(2,1)} %broadcast_in_dim.43), calls=%async_computation | async-start | bytes 655360 | tf_op jit(solution)/shard_map/all_to_all | solution.py:231
  28.0 133.6 %all-gather.3.cloned.1.call-start = ((), (), s32[]{:S(2)}) async-start(), calls=%async_computation.3 | async-start | bytes 4874240 | tf_op jit(solution)/shard_map/all_gather | solution.py:299
  28.2 6.2 %collective-permute-start = (bf16[40,896]{1,0:T(8,128)(2,1)S(1)}, bf16[40,896]{1,0:T(8,128)(2,1)S(1)}, u32[]{:S(2)}, u32[]{:S(2)}) collective-permute-start(bf16[40,896]{1,0:T(8,128)(2,1)S(1)} %slice.52), channel_id=1, source_target_pairs={{0,256},{256,0},{1,257},{257,1},{2,258},{258,2},{3,259},{259,3},{4... | collective-permute-start | bytes 215048 | tf_op jit(solution)/shard_map/ppermute | solution.py:293
  34.4 5.6 %collective-permute-start.1 = (bf16[80,896]{1,0:T(8,128)(2,1)S(1)}, bf16[80,896]{1,0:T(8,128)(2,1)S(1)}, u32[]{:S(2)}, u32[]{:S(2)}) collective-permute-start(bf16[80,896]{1,0:T(8,128)(2,1)S(1)} %maximum_select_fusion), channel_id=1, source_target_pairs={{0,0},{2,2},{4,4},{6,6},{8,10},{10,12},{12,14},{14,8},{1,1},{3,3},... | collective-permute-start | bytes 430088 | tf_op jit(solution)/shard_map/ppermute | solution.py:297
  35.1 7.5 %collective-permute-start.8 = (bf16[80,896]{1,0:T(8,128)(2,1)S(1)}, bf16[80,896]{1,0:T(8,128)(2,1)S(1)}, u32[]{:S(2)}, u32[]{:S(2)}) collective-permute-start(bf16[80,896]{1,0:T(8,128)(2,1)S(1)} %maximum_select_fusion), channel_id=1, source_target_pairs={{0,6},{1,7},{2,0},{3,1},{4,2},{5,3},{6,4},{7,5},{8,265},{9,264},{1... | collective-permute-start | bytes 430088 | tf_op jit(solution)/shard_map/ppermute | solution.py:298
  87.7 15.6 %collective-permute-start.2 = (bf16[16,120,640]{2,1,0:T(8,128)(2,1)S(1)}, bf16[16,120,640]{2,1,0:T(8,128)(2,1)}, u32[]{:S(2)}, u32[]{:S(2)}) collective-permute-start(bf16[16,120,640]{2,1,0:T(8,128)(2,1)S(1)} %all_to_all.15.own_ref), channel_id=1, source_target_pairs={{0,8},{8,0},{1,9},{9,1},{2,10},{10,2},{3,11},{11,3},{4,12},{12,4},... | collective-permute-start | bytes 7372808 | tf_op jit(solution)/shard_map/ppermute | solution.py:309
  91.1 12.2 %copy-start.8 = (f32[1280]{0:T(1024)S(1)}, f32[1280]{0:T(1024)}, u32[]{:S(2)}) copy-start(f32[1280]{0:T(1024)} %param.16) | copy-start | bytes 15364
  91.1 12.2 %copy-start = (bf16[1,128,1280]{2,1,0:T(8,128)(2,1)S(1)}, bf16[1,128,1280]{2,1,0:T(8,128)(2,1)}, u32[]{:S(2)}) copy-start(bf16[1,128,1280]{2,1,0:T(8,128)(2,1)} %param.10) | copy-start | bytes 983044
  91.1 12.2 %copy-start.1 = (f32[32,128]{1,0:T(8,128)S(1)}, f32[32,128]{1,0:T(8,128)}, u32[]{:S(2)}) copy-start(f32[32,128]{1,0:T(8,128)} %constant.27.clone.cos_ref) | copy-start | bytes 49156
  91.1 12.2 %copy-start.2 = (f32[32,128]{1,0:T(8,128)S(1)}, f32[32,128]{1,0:T(8,128)}, u32[]{:S(2)}) copy-start(f32[32,128]{1,0:T(8,128)} %constant.28.clone.sin_ref) | copy-start | bytes 49156
  91.1 39.6 %all-to-all-start.2 = ((bf16[16,80,640]{2,1,0:T(8,128)(2,1)}), bf16[16,80,640]{2,1,0:T(8,128)(2,1)}, u32[]{:S(2)}, u32[]{:S(2)}) async-start(bf16[16,80,640]{2,1,0:T(8,128)(2,1)} %broadcast_in_dim.46), calls=%async_computation.2 | async-start | bytes 3276800 | tf_op jit(solution)/shard_map/all_to_all | solution.py:308
  96.1 13.1 %collective-permute-start.3 = (bf16[448,1280]{1,0:T(8,128)(2,1)}, bf16[448,1280]{1,0:T(8,128)(2,1)S(1)}, u32[]{:S(2)}, u32[]{:S(2)}) collective-permute-start(bf16[448,1280]{1,0:T(8,128)(2,1)} %param.15), channel_id=1, source_target_pairs={{0,0},{2,2},{4,4},{6,6},{8,10},{10,12},{12,14},{14,8},{1,1},{3,3},... | collective-permute-start | bytes 3440648 | tf_op jit(solution)/shard_map/ppermute | solution.py:302
  98.1 31.7 %collective-permute-start.4 = (bf16[448,1280]{1,0:T(8,128)(2,1)}, bf16[448,1280]{1,0:T(8,128)(2,1)S(1)}, u32[]{:S(2)}, u32[]{:S(2)}) collective-permute-start(bf16[448,1280]{1,0:T(8,128)(2,1)} %param.15), channel_id=1, source_target_pairs={{0,6},{1,7},{2,0},{3,1},{4,2},{5,3},{6,4},{7,5},{8,265},{9,264},{1... | collective-permute-start | bytes 3440648 | tf_op jit(solution)/shard_map/ppermute | solution.py:303
  103.4 33.4 %copy-start.9 = (f32[1280]{0:T(1024)S(1)}, f32[1280]{0:T(1024)}, u32[]{:S(2)}) copy-start(f32[1280]{0:T(1024)} %param.17) | copy-start | bytes 15364
  109.3 1.0 copy-start.4
  129.7 1.0 copy-start.6
  130.8 9.3 %collective-permute-start.5 = (bf16[16,80,640]{2,1,0:T(8,128)(2,1)}, bf16[16,80,640]{2,1,0:T(8,128)(2,1)S(1)}, u32[]{:S(2)}, u32[]{:S(2)}) collective-permute-start(bf16[16,80,640]{2,1,0:T(8,128)(2,1)} %all-to-all-done.2.own_ref), channel_id=1, source_target_pairs={{0,8},{8,0},{1,9},{9,1},{2,10},{10,2},{3,11},{11,3},{4,12},{12,4},... | collective-permute-start | bytes 4915208 | tf_op jit(solution)/shard_map/ppermute | solution.py:312
  143.1 18.5 %copy-start.5 = (bf16[448,1280]{1,0:T(8,128)(2,1)S(1)}, bf16[448,1280]{1,0:T(8,128)(2,1)}, u32[]{:S(2)}) copy-start(bf16[448,1280]{1,0:T(8,128)(2,1)} %copy-done.4) | copy-start | bytes 3440644
  143.1 14.4 %collective-permute-start.6 = (bf16[128,1280]{1,0:T(8,128)(2,1)S(1)}, bf16[128,1280]{1,0:T(8,128)(2,1)S(1)}, u32[]{:S(2)}, u32[]{:S(2)}) collective-permute-start(bf16[128,1280]{1,0:T(8,128)(2,1)S(1)} %get-tuple-element.16.own_ref), channel_id=1, source_target_pairs={{0,261},{1,260},{2,263},{3,262},{4,257},{5,256},{6,259},{7,258},{2... | collective-permute-start | bytes 983048 | tf_op jit(solution)/shard_map/ppermute | solution.py:314
  157.6 4.0 %collective-permute-start.7 = (bf16[2,128,1280]{2,1,0:T(8,128)(2,1)S(1)}, bf16[2,128,1280]{2,1,0:T(8,128)(2,1)S(1)}, u32[]{:S(2)}, u32[]{:S(2)}) collective-permute-start(bf16[2,128,1280]{2,1,0:T(8,128)(2,1)S(1)} %pad_maximum_fusion), channel_id=1, source_target_pairs={{0,8},{8,0},{1,9},{9,1},{2,10},{10,2},{3,11},{11,3},{4,12},{12,4},... | collective-permute-start | bytes 1966088 | tf_op jit(solution)/shard_map/ppermute | solution.py:315
  161.6 2.3 %copy-start.3 = (bf16[1280,1792]{1,0:T(8,128)(2,1)S(1)}, bf16[1280,1792]{1,0:T(8,128)(2,1)}, u32[]{:S(2)}) copy-start(bf16[1280,1792]{1,0:T(8,128)(2,1)} %all-gather.3.cloned.1.call-done.gate_up_ref) | copy-start | bytes 13762564
  163.9 1.3 copy-start.7
  171.4 4.0 %collective-permute-start.9 = (bf16[2,128,1280]{2,1,0:T(8,128)(2,1)S(1)}, bf16[2,128,1280]{2,1,0:T(8,128)(2,1)S(1)}, u32[]{:S(2)}, u32[]{:S(2)}) collective-permute-start(bf16[2,128,1280]{2,1,0:T(8,128)(2,1)S(1)} %get-tuple-element.18), channel_id=1, source_target_pairs={{0,8},{8,0},{1,9},{9,1},{2,10},{10,2},{3,11},{11,3},{4,12},{12,4},... | collective-permute-start | bytes 1966088 | tf_op jit(solution)/shard_map/ppermute | solution.py:317
  175.6 14.1 %collective-permute-start.10 = (bf16[128,1280]{1,0:T(8,128)(2,1)S(1)}, bf16[128,1280]{1,0:T(8,128)(2,1)S(1)}, u32[]{:S(2)}, u32[]{:S(2)}) collective-permute-start(bf16[128,1280]{1,0:T(8,128)(2,1)S(1)} %fusion.5), channel_id=1, source_target_pairs={{0,261},{1,260},{2,263},{3,262},{4,257},{5,256},{6,259},{7,258},{2... | collective-permute-start | bytes 983048 | tf_op jit(solution)/shard_map/ppermute | solution.py:318
Sparse Core Ops, SparseCore 0:
  43.5 80.1 all-gather.2
